TPU v7x, 32 devices: a whole 2x2x4 slice. The times are simulated.
32 devices in a mesh: grid: 2 (over x), gx: 4 (over y, core), gy: 4 (over z).
Axes of the slice: x: 2, y: 2, z: 4, core: 2. Of those that a mesh axis runs over, the one named last changes fastest.
Arguments:
- fine_field: float32 [3, 16, 256, 2048], P(None, None, 'gx', ('grid', 'gy')), may hold values from -6 to 6
- fine_previous: float32 [3, 16, 256, 2048], P(None, None, 'gx', ('grid', 'gy')), may hold values from -6 to 6
- fine_speed: float32 [16, 256, 2048], P(None, 'gx', ('grid', 'gy')), may hold values from 0.1 to 0.2
- fine_metric: float32 [16, 256, 2048], P(None, 'gx', ('grid', 'gy')), may hold values from 0.8 to 1.2
- coarse_field: float32 [3, 16, 128, 1024], P(None, None, 'gx', ('grid', 'gy')), may hold values from -6 to 6
- coarse_previous: float32 [3, 16, 128, 1024], P(None, None, 'gx', ('grid', 'gy')), may hold values from -6 to 6
- coarse_speed: float32 [16, 128, 1024], P(None, 'gx', ('grid', 'gy')), may hold values from 0.02 to 0.04
- fine_traction: float32 [256, 2048], P('gx', ('grid', 'gy')), may hold values from 0.4 to 0.8
- coarse_shear: float32 [128, 1024], P('gx', ('grid', 'gy')), may hold values from 1 to 2
Outputs:
- fine_result: float32 [3, 16, 256, 2048], P(None, None, 'gx', ('grid', 'gy'))
- coarse_result: float32 [3, 16, 128, 1024], P(None, None, 'gx', ('grid', 'gy'))
- change_history: float32 [2, 4], replicated
All inputs are finite; a program needn't handle non-finite values.
Results may differ from a plain program's by a relative error of at most 0.00002.
Values sent between devices are 32-bit elements; how exact they have to be, the bound alone decides.
No kernel may reach another device: no remote copies, remote signals or barrier semaphores. Data moves between devices by JAX's collectives and lax.ppermute only.
A program may use at most 256 MiB of HBM per device.

v0:
```python
import jax
import jax.numpy as jnp
from jax import lax
from jax.sharding import PartitionSpec as P

ITERS = 4
STEPS = 2


def extended_2(block, sides, width):
    for axis, dim in sides:
        count = lax.axis_size(axis)
        forward = [(i, i + 1) for i in range(count - 1)]
        backward = [(target, source) for source, target in forward]
        low = lax.ppermute(
            lax.slice_in_dim(block, block.shape[dim] - width, None, axis=dim), axis, forward
        )
        high = lax.ppermute(lax.slice_in_dim(block, 0, width, axis=dim), axis, backward)
        block = jnp.concatenate([low, block, high], axis=dim)
    return block


def shifted(value, axis, by):
    peers = lax.axis_size(axis)
    pairs = [(i, i + by) for i in range(peers) if 0 <= i + by < peers]
    return lax.ppermute(value, axis, pairs)


def prolong(values):
    return jnp.repeat(jnp.repeat(values, 2, axis=-2), 2, axis=-1)


def restrict(values):
    shaped = values.reshape(
        values.shape[:-2] + (values.shape[-2] // 2, 2, values.shape[-1] // 2, 2)
    )
    return (
        shaped[..., 0, :, 0] + shaped[..., 0, :, 1] + shaped[..., 1, :, 0] + shaped[..., 1, :, 1]
    ) * 0.25


def last_shift(block, lower, upper, offset):
    if offset == -2:
        return jnp.concatenate([lower, block[..., :-2]], axis=-1)
    if offset == -1:
        return jnp.concatenate([lower[..., 1:], block[..., :-1]], axis=-1)
    if offset == 1:
        return jnp.concatenate([block[..., 1:], upper[..., :1]], axis=-1)
    return jnp.concatenate([block[..., 2:], upper], axis=-1)


def depth_shift(block, above, below, offset):
    if offset == -2:
        return jnp.concatenate([above, block[:, :-2]], axis=1)
    if offset == -1:
        return jnp.concatenate([above[:, 1:], block[:, :-1]], axis=1)
    if offset == 1:
        return jnp.concatenate([block[:, 1:], below[:, :1]], axis=1)
    return jnp.concatenate([block[:, 2:], below], axis=1)


def lateral_parts(extended, center, lower, upper):
    count = center.shape[-2]
    along_x = (
        -extended[..., 0:count, :]
        + 16.0 * extended[..., 1 : 1 + count, :]
        - 30.0 * center
        + 16.0 * extended[..., 3 : 3 + count, :]
        - extended[..., 4 : 4 + count, :]
    ) / 12.0
    along_y = (
        -last_shift(center, lower, upper, -2)
        + 16.0 * last_shift(center, lower, upper, -1)
        - 30.0 * center
        + 16.0 * last_shift(center, lower, upper, 1)
        - last_shift(center, lower, upper, 2)
    ) / 12.0
    return (along_x, along_y)


def depth_part(block, above, below):
    return (
        -depth_shift(block, above, below, -2)
        + 16.0 * depth_shift(block, above, below, -1)
        - 30.0 * block
        + 16.0 * depth_shift(block, above, below, 1)
        - depth_shift(block, above, below, 2)
    ) / 12.0


def trim_rows(strip):
    return strip[..., 2:-2, :]


def record(local_change, history):
    history.append(lax.pmax(local_change, ("grid", "gx", "gy")))


def on_device(
    fine_field,
    fine_previous,
    fine_speed,
    fine_metric,
    coarse_field,
    coarse_previous,
    coarse_speed,
    fine_traction,
    coarse_shear,
):
    metric_sq = fine_metric * fine_metric
    speed_bottom = fine_speed[-1]
    metric_bottom = metric_sq[-1]
    history = []
    for step_index in range(STEPS):
        fine_ext = extended_2(fine_field, (("gx", 2),), 2)
        coarse_ext = extended_2(coarse_field, (("gx", 2),), 2)
        fine_lower, coarse_lower = shifted(
            (fine_ext[..., -2:], coarse_ext[..., -2:]), ("grid", "gy"), 1
        )
        fine_upper, coarse_upper = shifted(
            (fine_ext[..., :2], coarse_ext[..., :2]), ("grid", "gy"), -1
        )
        fine_lower = trim_rows(fine_lower)
        fine_upper = trim_rows(fine_upper)
        coarse_lower = trim_rows(coarse_lower)
        coarse_upper = trim_rows(coarse_upper)
        u_bottom = fine_field[:, -1]
        fine_higher = fine_field[:, -2]
        fine_highest = fine_field[:, -3]
        plane_x, plane_y = lateral_parts(
            fine_ext[:, -1], u_bottom, fine_lower[:, -1], fine_upper[:, -1]
        )
        fine_const = (
            -12.0 * (plane_x + plane_y) / metric_bottom
            + fine_highest
            - 16.0 * fine_higher
            + 29.0 * u_bottom
        )
        fine_gain = 12.0 / (speed_bottom * metric_bottom)
        fine_base = fine_highest - 8.0 * fine_higher + u_bottom
        coarse_top = coarse_field[:, 0]
        coarse_next = coarse_field[:, 1]
        coarse_third = coarse_field[:, 2]
        top_x, top_y = lateral_parts(
            coarse_ext[:, 0], coarse_top, coarse_lower[:, 0], coarse_upper[:, 0]
        )
        coarse_const = (
            top_x + top_y + (-29.0 * coarse_top + 16.0 * coarse_next - coarse_third) / 12.0
        )
        coarse_base = -coarse_top + 8.0 * coarse_next - coarse_third
        ghost_fine = u_bottom
        ghost_coarse = coarse_top
        for sweep in range(ITERS):
            send_coarse = prolong(coarse_speed[0] * (coarse_const + 14.0 * ghost_coarse / 12.0))
            send_fine = fine_traction * (fine_base + 6.0 * ghost_fine) / 12.0
            next_fine = (fine_gain * send_coarse + fine_const) / 14.0
            next_coarse = (coarse_base - 24.0 * restrict(send_fine) / coarse_shear) / 6.0
            local_change = jnp.maximum(
                jnp.max(jnp.abs(next_fine - ghost_fine)),
                jnp.max(jnp.abs(next_coarse - ghost_coarse)),
            )
            record(local_change, history)
            ghost_fine = next_fine
            ghost_coarse = next_coarse
        fine_above = jnp.zeros((3, 2) + u_bottom.shape[1:], jnp.float32)
        fine_below = jnp.stack([ghost_fine, 2.0 * ghost_fine - u_bottom], axis=1)
        coarse_above = jnp.stack([2.0 * ghost_coarse - coarse_top, ghost_coarse], axis=1)
        coarse_below = jnp.zeros((3, 2) + coarse_top.shape[1:], jnp.float32)
        fine_x, fine_y = lateral_parts(fine_ext, fine_field, fine_lower, fine_upper)
        fine_change = fine_speed * (
            fine_x + fine_y + metric_sq * depth_part(fine_field, fine_above, fine_below)
        )
        coarse_x, coarse_y = lateral_parts(coarse_ext, coarse_field, coarse_lower, coarse_upper)
        coarse_change = coarse_speed * (
            coarse_x + coarse_y + depth_part(coarse_field, coarse_above, coarse_below)
        )
        new_fine = 2.0 * fine_field - fine_previous + fine_change
        new_coarse = 2.0 * coarse_field - coarse_previous + coarse_change
        fine_previous = fine_field
        fine_field = new_fine
        coarse_previous = coarse_field
        coarse_field = new_coarse
    change_history = jnp.stack(history).reshape(STEPS, ITERS)
    return (fine_field, coarse_field, change_history)


def solution(mesh):
    placed = (
        P(None, None, "gx", ("grid", "gy")),
        P(None, None, "gx", ("grid", "gy")),
        P(None, "gx", ("grid", "gy")),
        P(None, "gx", ("grid", "gy")),
        P(None, None, "gx", ("grid", "gy")),
        P(None, None, "gx", ("grid", "gy")),
        P(None, "gx", ("grid", "gy")),
        P("gx", ("grid", "gy")),
        P("gx", ("grid", "gy")),
    )
    return jax.shard_map(
        on_device,
        mesh=mesh,
        in_specs=placed,
        out_specs=(P(None, None, "gx", ("grid", "gy")), P(None, None, "gx", ("grid", "gy")), P()),
        check_vma=False,
    )
```

profile of v0, /device:TPU:0, one launch (start us, length us, event | category | flops | bytes accessed | tf_op | source)
XLA Modules:
  0.0 645.6 jit_solution(5785937403898104391)
XLA Ops:
  18.2 5.8 copy.759
  27.1 12.0 %fusion.159 = (f32[3,16,64,254]{2,3,0,1:T(8,128)}, f32[3,16,64,254]{2,3,0,1:T(8,128)}) fusion(f32[3,16,64,256]{2,3,0,1:T(8,128)} %copy.759), kind=kLoop, calls=%fused_computation.339 | loop fusion | bytes 12484608 | tf_op jit(solution)/shard_map/slice | solution.py:49
  39.1 5.7 fusion.160
  44.9 6.1 fusion.158
  50.9 5.7 fusion.157
  63.5 14.0 %add.483 = f32[3,32,2,128,2]{4,3,2,1,0:T(8,128)} reshape(f32[3,1,64,256]{3,2,0,1:T(8,128)S(1)} %copy.794) | data formatting | bytes 393216 | tf_op jit(solution)/shard_map/add | solution.py:155
  82.9 13.8 %multiply_multiply_fusion.1 = f32[3,32,2,128,2]{4,3,2,1,0:T(8,128)} fusion(f32[3,32,2,128,2]{4,3,2,1,0:T(8,128)} %add.483, f32[32,2,128,2]{3,2,1,0:T(8,128)} %mul.619), kind=kLoop, calls=%fused_computation.1 | loop fusion | flops 98304 | bytes 458752 | tf_op jit(solution)/shard_map/div | solution.py:155
  96.8 11.7 %fusion.25 = f32[3,32,128]{2,1,0:T(8,128)} fusion(f32[3,32,2,128,2]{4,3,2,1,0:T(8,128)} %multiply_multiply_fusion.1), kind=kLoop, calls=%fused_computation.53 | loop fusion | flops 49152 | bytes 245760 | tf_op jit(solution)/shard_map/mul | solution.py:157
  114.3 5.7 copy.760
  166.3 14.2 %reshape.271 = f32[3,32,2,128,2]{4,3,2,1,0:T(8,128)} reshape(f32[3,64,256]{2,1,0:T(8,128)S(1)} %copy.822) | data formatting | bytes 393216 | tf_op jit(solution)/shard_map/reshape | solution.py:34
  180.5 10.9 %fusion.11 = f32[3,32,128]{2,1,0:T(8,128)S(1)} fusion(f32[3,32,2,128,2]{4,3,2,1,0:T(8,128)} %reshape.271), kind=kLoop, calls=%fused_computation.29 | loop fusion | flops 49152 | bytes 245760 | tf_op jit(solution)/shard_map/mul | solution.py:157
  194.0 14.0 %reshape.266 = f32[3,32,2,128,2]{4,3,2,1,0:T(8,128)} reshape(f32[3,64,256]{2,1,0:T(8,128)S(1)} %copy.797) | data formatting | bytes 393216 | tf_op jit(solution)/shard_map/reshape | solution.py:34
  208.0 10.8 %fusion.23 = f32[3,32,128]{2,1,0:T(8,128)S(1)} fusion(f32[3,32,2,128,2]{4,3,2,1,0:T(8,128)} %reshape.266), kind=kLoop, calls=%fused_computation.48 | loop fusion | flops 49152 | bytes 245760 | tf_op jit(solution)/shard_map/mul | solution.py:157
  224.7 14.0 %reshape.274 = f32[3,32,2,128,2]{4,3,2,1,0:T(8,128)} reshape(f32[3,64,256]{2,1,0:T(8,128)S(1)} %copy.824) | data formatting | bytes 393216 | tf_op jit(solution)/shard_map/reshape | solution.py:34
  238.9 11.2 %fusion.9 = f32[3,32,128]{2,1,0:T(8,128)S(1)} fusion(f32[3,32,2,128,2]{4,3,2,1,0:T(8,128)} %reshape.274), kind=kLoop, calls=%fused_computation.24 | loop fusion | flops 49152 | bytes 245760 | tf_op jit(solution)/shard_map/mul | solution.py:157
  256.3 43.3 %fusion.31 = f32[3,16,64,256]{2,3,0,1:T(8,128)S(1)} fusion(f32[3,16,2,256]{2,3,0,1:T(8,128)} %copy.768, f32[3,16,64,256]{2,3,0,1:T(8,128)} %copy.759, f32[3,16,2,256]{2,3,0,1:T(8,128)} %copy.763, f32[3,16,64,254]{2,3,0,1:T(8,128)} %get-tuple-element.118, f32[3,16,64,2]{2,3,0,1:T(2,128)S(1)} %slice.759, f32[3,16,64,255]{2,3,0,1:T(8,128)} %get-tuple-element.120, ...), kind=kLoop, calls=%fused_computation.62 | loop fusion | flops 32243712 | bytes 36110336 | tf_op jit(solution)/shard_map/add | solution.py:177
  299.6 6.9 %fusion.156 = (f32[3,16,2,256]{2,3,0,1:T(8,128)}, f32[3,16,2,256]{2,3,0,1:T(8,128)}) fusion(f32[3,16,64,256]{2,3,0,1:T(8,128)S(1)} %fusion.31), kind=kLoop, calls=%fused_computation.336 | loop fusion | bytes 393216 | tf_op jit(solution)/shard_map/slice | solution.py:16
  327.6 6.1 fusion.153
  333.7 5.7 fusion.152
  359.9 14.2 %add.544 = f32[3,32,2,128,2]{4,3,2,1,0:T(8,128)} reshape(f32[3,1,64,256]{3,2,0,1:T(8,128)S(1)} %copy.833) | data formatting | bytes 393216 | tf_op jit(solution)/shard_map/add | solution.py:155
  374.1 13.8 %multiply_multiply_fusion = f32[3,32,2,128,2]{4,3,2,1,0:T(8,128)} fusion(f32[3,32,2,128,2]{4,3,2,1,0:T(8,128)} %add.544, f32[32,2,128,2]{3,2,1,0:T(8,128)} %mul.619), kind=kLoop, calls=%fused_computation | loop fusion | flops 98304 | bytes 458752 | tf_op jit(solution)/shard_map/div | solution.py:155
  387.9 11.5 %fusion.7 = f32[3,32,128]{2,1,0:T(8,128)} fusion(f32[3,32,2,128,2]{4,3,2,1,0:T(8,128)} %multiply_multiply_fusion), kind=kLoop, calls=%fused_computation.19 | loop fusion | flops 49152 | bytes 245760 | tf_op jit(solution)/shard_map/mul | solution.py:157
  430.7 6.9 %collective-permute-start.10 = (f32[3,16,68,2]{2,3,0,1:T(2,128)S(1)}, f32[3,16,68,2]{2,3,0,1:T(2,128)S(1)}, u32[]{:S(2)}, u32[]{:S(2)}) collective-permute-start(f32[3,16,68,2]{2,3,0,1:T(2,128)S(1)} %get-tuple-element.96), channel_id=1, source_target_pairs={{0,1},{1,2},{2,3},{3,16},{16,17},{17,18},{18,19},{4,5},{5,6},{6,7}... | collective-permute-start | bytes 78344 | tf_op jit(solution)/shard_map/ppermute | solution.py:26
  447.9 14.2 %reshape.282 = f32[3,32,2,128,2]{4,3,2,1,0:T(8,128)} reshape(f32[3,64,256]{2,1,0:T(8,128)S(1)} %copy.843) | data formatting | bytes 393216 | tf_op jit(solution)/shard_map/reshape | solution.py:34
  462.1 10.9 %fusion.3 = f32[3,32,128]{2,1,0:T(8,128)S(1)} fusion(f32[3,32,2,128,2]{4,3,2,1,0:T(8,128)} %reshape.282), kind=kLoop, calls=%fused_computation.9 | loop fusion | flops 49152 | bytes 245760 | tf_op jit(solution)/shard_map/mul | solution.py:157
  475.6 14.0 %reshape.277 = f32[3,32,2,128,2]{4,3,2,1,0:T(8,128)} reshape(f32[3,64,256]{2,1,0:T(8,128)S(1)} %copy.835) | data formatting | bytes 393216 | tf_op jit(solution)/shard_map/reshape | solution.py:34
  489.6 10.8 %fusion.5 = f32[3,32,128]{2,1,0:T(8,128)S(1)} fusion(f32[3,32,2,128,2]{4,3,2,1,0:T(8,128)} %reshape.277), kind=kLoop, calls=%fused_computation.14 | loop fusion | flops 49152 | bytes 245760 | tf_op jit(solution)/shard_map/mul | solution.py:157
  506.3 14.0 %reshape.285 = f32[3,32,2,128,2]{4,3,2,1,0:T(8,128)} reshape(f32[3,64,256]{2,1,0:T(8,128)S(1)} %copy.845) | data formatting | bytes 393216 | tf_op jit(solution)/shard_map/reshape | solution.py:34
  520.4 11.3 %fusion.1 = f32[3,32,128]{2,1,0:T(8,128)S(1)} fusion(f32[3,32,2,128,2]{4,3,2,1,0:T(8,128)} %reshape.285), kind=kLoop, calls=%fused_computation.4 | loop fusion | flops 49152 | bytes 245760 | tf_op jit(solution)/shard_map/mul | solution.py:157
  543.1 50.0 %all-reduce.8 = (f32[1]{0:T(128)}, f32[1]{0:T(128)}, f32[1]{0:T(128)}, f32[1]{0:T(128)}, f32[1]{0:T(128)}, /*index=5*/f32[1]{0:T(128)}, f32[1]{0:T(128)}, f32[1]{0:T(128)}) all-reduce(f32[1]{0:T(128)} %bitcast.51, f32[1]{0:T(128)} %bitcast.52, f32[1]{0:T(128)} %bitcast.53, ...), channel_id=1, replica_groups=mesh['grid'=2,'gx'=4,'gy'=4] {'grid','gx','gy'}, use_global_device_ids=true, to_apply=%region_2.0 | all-reduce | flops 8 | bytes 64 | tf_op jit(solution)/shard_map/pmax | solution.py:96
  606.0 33.0 %fusion.17 = f32[3,16,64,256]{2,3,0,1:T(8,128)} fusion(f32[3,16,2,256]{2,3,0,1:T(8,128)} %copy.805, f32[3,16,64,256]{2,3,0,1:T(8,128)S(1)} %bitcast.189, f32[3,16,2,256]{2,3,0,1:T(8,128)} %copy.803, f32[3,16,64,254]{2,3,0,1:T(8,128)} %get-tuple-element.106, f32[3,16,64,2]{2,3,0,1:T(2,128)S(1)} %slice.820, f32[3,16,64,255]{2,3,0,1:T(8,128)} %get-tuple-element.108, ...), kind=kLoop, calls=%fused_computation.38 | loop fusion | flops 32243712 | bytes 36110336 | tf_op jit(solution)/shard_map/add | solution.py:177
  639.0 6.1 copy.846
  (386 shorter events, 204.9 us)
Async XLA Ops:
  3.6 116.4 %collective-permute-start.4 = (f32[3,16,2,128]{3,2,0,1:T(2,128)}, f32[3,16,2,128]{3,2,0,1:T(2,128)}, u32[]{:S(2)}, u32[]{:S(2)}) collective-permute-start(f32[3,16,2,128]{3,2,0,1:T(2,128)} %get-tuple-element.151), channel_id=1, source_target_pairs={{0,4},{4,8},{8,12},{1,5},{5,9},{9,13},{2,6},{6,10},{10,14},{3,7},{... | collective-permute-start | bytes 147464 | tf_op jit(solution)/shard_map/ppermute | solution.py:15
  6.6 113.4 %collective-permute-start.5 = (f32[3,16,2,128]{3,2,0,1:T(2,128)}, f32[3,16,2,128]{3,2,0,1:T(2,128)}, u32[]{:S(2)}, u32[]{:S(2)}) collective-permute-start(f32[3,16,2,128]{3,2,0,1:T(2,128)} %get-tuple-element.152), channel_id=1, source_target_pairs={{4,0},{8,4},{12,8},{5,1},{9,5},{13,9},{6,2},{10,6},{14,10},{7,3},{... | collective-permute-start | bytes 147464 | tf_op jit(solution)/shard_map/ppermute | solution.py:18
  9.7 130.6 %collective-permute-start = (f32[3,16,2,256]{3,1,2,0:T(8,128)}, f32[3,16,2,256]{3,1,2,0:T(8,128)}, u32[]{:S(2)}, u32[]{:S(2)}) collective-permute-start(f32[3,16,2,256]{3,1,2,0:T(8,128)} %copy.848), channel_id=1, source_target_pairs={{0,4},{4,8},{8,12},{1,5},{5,9},{9,13},{2,6},{6,10},{10,14},{3,7},{... | collective-permute-start | bytes 294920 | tf_op jit(solution)/shard_map/ppermute | solution.py:15
  15.5 129.5 %collective-permute-start.1 = (f32[3,16,2,256]{3,1,2,0:T(8,128)}, f32[3,16,2,256]{3,1,2,0:T(8,128)}, u32[]{:S(2)}, u32[]{:S(2)}) collective-permute-start(f32[3,16,2,256]{3,1,2,0:T(8,128)} %copy.849), channel_id=1, source_target_pairs={{4,0},{8,4},{12,8},{5,1},{9,5},{13,9},{6,2},{10,6},{14,10},{7,3},{... | collective-permute-start | bytes 294920 | tf_op jit(solution)/shard_map/ppermute | solution.py:18
  112.3 51.0 %copy-start.50 = (f32[64,256]{0,1:T(8,128)}, f32[64,256]{0,1:T(8,128)S(1)}, u32[]{:S(2)}) copy-start(f32[64,256]{0,1:T(8,128)S(1)} %copy.796) | copy-start | bytes 196612
  122.4 7.4 %collective-permute-start.6 = (f32[3,16,36,2]{2,1,3,0:T(8,128)}, f32[3,16,36,2]{2,1,3,0:T(8,128)S(1)}, u32[]{:S(2)}, u32[]{:S(2)}) collective-permute-start(f32[3,16,36,2]{2,1,3,0:T(8,128)} %copy.784), channel_id=1, source_target_pairs={{0,1},{1,2},{2,3},{3,16},{16,17},{17,18},{18,19},{4,5},{5,6},{6,7}... | collective-permute-start | bytes 41480 | tf_op jit(solution)/shard_map/ppermute | solution.py:26
  126.3 6.7 %collective-permute-start.7 = (f32[3,16,36,2]{2,1,3,0:T(8,128)S(1)}, f32[3,16,36,2]{2,1,3,0:T(8,128)S(1)}, u32[]{:S(2)}, u32[]{:S(2)}) collective-permute-start(f32[3,16,36,2]{2,1,3,0:T(8,128)S(1)} %copy.786), channel_id=1, source_target_pairs={{1,0},{2,1},{3,2},{16,3},{17,16},{18,17},{19,18},{5,4},{6,5},{7,6}... | collective-permute-start | bytes 41480 | tf_op jit(solution)/shard_map/ppermute | solution.py:26
  151.6 6.1 collective-permute-start.2
  156.4 6.7 %collective-permute-start.3 = (f32[3,16,68,2]{2,3,0,1:T(2,128)S(1)}, f32[3,16,68,2]{2,3,0,1:T(2,128)S(1)}, u32[]{:S(2)}, u32[]{:S(2)}) collective-permute-start(f32[3,16,68,2]{2,3,0,1:T(2,128)S(1)} %get-tuple-element.97), channel_id=1, source_target_pairs={{1,0},{2,1},{3,2},{16,3},{17,16},{18,17},{19,18},{5,4},{6,5},{7,6}... | collective-permute-start | bytes 78344 | tf_op jit(solution)/shard_map/ppermute | solution.py:26
  192.0 26.8 %copy-start.56 = (f32[3,32,128]{2,1,0:T(8,128)}, f32[3,32,128]{2,1,0:T(8,128)S(1)}, u32[]{:S(2)}) copy-start(f32[3,32,128]{2,1,0:T(8,128)S(1)} %get-tuple-element.84) | copy-start | bytes 147460
  299.6 34.0 %copy-start = (f32[3,16,64,256]{2,3,0,1:T(8,128)}, f32[3,16,64,256]{2,3,0,1:T(8,128)S(1)}, u32[]{:S(2)}) copy-start(f32[3,16,64,256]{2,3,0,1:T(8,128)S(1)} %fusion.31) | copy-start | bytes 9437188
  339.4 18.4 %copy-start.85 = (f32[3,16,2,128]{3,2,0,1:T(2,128)S(1)}, f32[3,16,2,128]{3,2,0,1:T(2,128)}, u32[]{:S(2)}) copy-start(f32[3,16,2,128]{3,2,0,1:T(2,128)} %get-tuple-element.140) | copy-start | bytes 147460
  339.4 20.4 %copy-start.45 = (f32[3,1,64,256]{2,3,0,1:T(8,128)S(1)}, f32[3,1,64,256]{2,3,0,1:T(8,128)}, u32[]{:S(2)}) copy-start(f32[3,1,64,256]{2,3,0,1:T(8,128)} %get-tuple-element.103) | copy-start | bytes 589828
  344.5 74.8 %collective-permute-start.8 = (f32[3,16,2,256]{3,1,2,0:T(8,128)}, f32[3,16,2,256]{3,1,2,0:T(8,128)}, u32[]{:S(2)}, u32[]{:S(2)}) collective-permute-start(f32[3,16,2,256]{3,1,2,0:T(8,128)} %copy.802), channel_id=1, source_target_pairs={{0,4},{4,8},{8,12},{1,5},{5,9},{9,13},{2,6},{6,10},{10,14},{3,7},{... | collective-permute-start | bytes 294920 | tf_op jit(solution)/shard_map/ppermute | solution.py:15
  352.1 71.9 %collective-permute-start.9 = (f32[3,16,2,256]{3,1,2,0:T(8,128)}, f32[3,16,2,256]{3,1,2,0:T(8,128)}, u32[]{:S(2)}, u32[]{:S(2)}) collective-permute-start(f32[3,16,2,256]{3,1,2,0:T(8,128)} %copy.804), channel_id=1, source_target_pairs={{4,0},{8,4},{12,8},{5,1},{9,5},{13,9},{6,2},{10,6},{14,10},{7,3},{... | collective-permute-start | bytes 294920 | tf_op jit(solution)/shard_map/ppermute | solution.py:18
  353.4 46.8 %collective-permute-start.12 = (f32[3,16,2,128]{3,2,0,1:T(2,128)S(1)}, f32[3,16,2,128]{3,2,0,1:T(2,128)S(1)}, u32[]{:S(2)}, u32[]{:S(2)}) collective-permute-start(f32[3,16,2,128]{3,2,0,1:T(2,128)S(1)} %copy-done.86), channel_id=1, source_target_pairs={{0,4},{4,8},{8,12},{1,5},{5,9},{9,13},{2,6},{6,10},{10,14},{3,7},{... | collective-permute-start | bytes 147464 | tf_op jit(solution)/shard_map/ppermute | solution.py:15
  357.8 42.3 %collective-permute-start.13 = (f32[3,16,2,128]{3,2,0,1:T(2,128)S(1)}, f32[3,16,2,128]{3,2,0,1:T(2,128)S(1)}, u32[]{:S(2)}, u32[]{:S(2)}) collective-permute-start(f32[3,16,2,128]{3,2,0,1:T(2,128)S(1)} %copy-done.85), channel_id=1, source_target_pairs={{4,0},{8,4},{12,8},{5,1},{9,5},{13,9},{6,2},{10,6},{14,10},{7,3},{... | collective-permute-start | bytes 147464 | tf_op jit(solution)/shard_map/ppermute | solution.py:18
  400.1 17.8 %copy-start.58 = (f32[3,16,2,128]{3,2,0,1:T(2,128)}, f32[3,16,2,128]{3,2,0,1:T(2,128)S(1)}, u32[]{:S(2)}) copy-start(f32[3,16,2,128]{3,2,0,1:T(2,128)S(1)} %collective-permute-done.12) | copy-start | bytes 147460
  400.1 17.8 %copy-start.60 = (f32[3,16,2,128]{3,2,0,1:T(2,128)}, f32[3,16,2,128]{3,2,0,1:T(2,128)S(1)}, u32[]{:S(2)}) copy-start(f32[3,16,2,128]{3,2,0,1:T(2,128)S(1)} %collective-permute-done.13) | copy-start | bytes 147460
  401.0 6.0 collective-permute-start.14
  405.7 6.2 collective-permute-start.15
  430.6 14.3 %copy-start.35 = (f32[3,64,254]{1,2,0:T(8,128)S(1)}, f32[3,64,254]{1,2,0:T(8,128)}, u32[]{:S(2)}) copy-start(f32[3,64,254]{1,2,0:T(8,128)} %get-tuple-element.155) | copy-start | bytes 585220
  430.6 14.3 %copy-start.36 = (f32[3,64,254]{1,2,0:T(8,128)S(1)}, f32[3,64,254]{1,2,0:T(8,128)}, u32[]{:S(2)}) copy-start(f32[3,64,254]{1,2,0:T(8,128)} %get-tuple-element.156) | copy-start | bytes 585220
  430.6 14.3 %copy-start.37 = (f32[3,64,255]{1,2,0:T(8,128)S(1)}, f32[3,64,255]{1,2,0:T(8,128)}, u32[]{:S(2)}) copy-start(f32[3,64,255]{1,2,0:T(8,128)} %get-tuple-element.157) | copy-start | bytes 587524
  430.7 8.8 %collective-permute-start.10 = (f32[3,16,68,2]{2,3,0,1:T(2,128)S(1)}, f32[3,16,68,2]{2,3,0,1:T(2,128)S(1)}, u32[]{:S(2)}, u32[]{:S(2)}) collective-permute-start(f32[3,16,68,2]{2,3,0,1:T(2,128)S(1)} %get-tuple-element.96), channel_id=1, source_target_pairs={{0,1},{1,2},{2,3},{3,16},{16,17},{17,18},{18,19},{4,5},{5,6},{6,7}... | collective-permute-start | bytes 78344 | tf_op jit(solution)/shard_map/ppermute | solution.py:26
  437.9 6.8 %collective-permute-start.11 = (f32[3,16,68,2]{2,3,0,1:T(2,128)S(1)}, f32[3,16,68,2]{2,3,0,1:T(2,128)S(1)}, u32[]{:S(2)}, u32[]{:S(2)}) collective-permute-start(f32[3,16,68,2]{2,3,0,1:T(2,128)S(1)} %get-tuple-element.95), channel_id=1, source_target_pairs={{1,0},{2,1},{3,2},{16,3},{17,16},{18,17},{19,18},{5,4},{6,5},{7,6}... | collective-permute-start | bytes 78344 | tf_op jit(solution)/shard_map/ppermute | solution.py:26
  439.4 22.7 %copy-start.79 = (f32[3,16,68,2]{2,3,0,1:T(2,128)}, f32[3,16,68,2]{2,3,0,1:T(2,128)S(1)}, u32[]{:S(2)}) copy-start(f32[3,16,68,2]{2,3,0,1:T(2,128)S(1)} %collective-permute-done.10) | copy-start | bytes 78340
  520.4 78.5 %copy-start.19 = (f32[3,16,32,2]{3,2,0,1:T(8,128)S(1)}, f32[3,16,32,2]{3,2,0,1:T(8,128)}, u32[]{:S(2)}) copy-start(f32[3,16,32,2]{3,2,0,1:T(8,128)} %copy.838) | copy-start | bytes 36868
  520.4 78.5 %copy-start.20 = (f32[3,16,32,2]{3,2,0,1:T(8,128)S(1)}, f32[3,16,32,2]{3,2,0,1:T(8,128)}, u32[]{:S(2)}) copy-start(f32[3,16,32,2]{3,2,0,1:T(8,128)} %copy.841) | copy-start | bytes 36868
  520.4 78.5 %copy-start.34 = (f32[16,32,128]{2,1,0:T(8,128)S(1)}, f32[16,32,128]{2,1,0:T(8,128)}, u32[]{:S(2)}) copy-start(f32[16,32,128]{2,1,0:T(8,128)} %broadcast_multiply_fusion.1) | copy-start | bytes 786436
  520.4 78.5 %copy-start.59 = (f32[3,16,2,128]{3,2,0,1:T(2,128)S(1)}, f32[3,16,2,128]{3,2,0,1:T(2,128)}, u32[]{:S(2)}) copy-start(f32[3,16,2,128]{3,2,0,1:T(2,128)} %copy-done.58) | copy-start | bytes 147460
  520.4 78.5 %copy-start.61 = (f32[3,16,2,128]{3,2,0,1:T(2,128)S(1)}, f32[3,16,2,128]{3,2,0,1:T(2,128)}, u32[]{:S(2)}) copy-start(f32[3,16,2,128]{3,2,0,1:T(2,128)} %copy-done.60) | copy-start | bytes 147460
  (79 other events, 781.6 us)
where the time goes:
time: 655 us; the launch traced here: 646 us
  local copies, waits for them, and re-layouts  290 us (44%)
  other arithmetic  231 us (35%)
  blocking collectives  50 us (8%)
  starting transfers between devices  43.2 us (7%)
  waiting for transfers between devices  18.3 us (3%)
  between operations  12.5 us (2%)
    mul x8, other arithmetic, on_device(): 24.0 * restrict(send_fine) / coarse_shear  89.1 us
    reshape x6, local copies, waits for them, and re-layouts, restrict(): values.reshape(values.shape[:-2] + (values.shape[-2] // 2, 2, values.shap...  84.4 us
    add x2, other arithmetic, on_device(): new_fine = 2.0 * fine_field - fine_previous + fine_change  76.3 us
    pmax x1, blocking collectives, record(): history.append(lax.pmax(local_change, ('grid', 'gx', 'gy')))  50 us
    div x8, other arithmetic, on_device(): send_fine = fine_traction * (fine_base + 6.0 * ghost_fine) / 12.0  33.1 us
    add x4, local copies, waits for them, and re-layouts, on_device(): send_fine = fine_traction * (fine_base + 6.0 * ghost_fine) / 12.0  28.4 us
    unnamed x203, local copies, waits for them, and re-layouts  27.1 us
    ppermute x8, starting transfers between devices, shifted(): return lax.ppermute(value, axis, pairs)  23 us
  transfers between devices with their start and end apart: 16, of which 5 were waited for; matrix products, arithmetic and copies ran while one was open for 28% of the time, Pallas kernels for 0%

commit v1 on v0

v1 whole, which is shorter than its diff:
```python
import functools

import jax
import jax.numpy as jnp
import numpy as np
from jax import lax
from jax.experimental import pallas as pl
from jax.experimental.pallas import tpu as pltpu
from jax.sharding import PartitionSpec as P

STEPS = 2
LANES = 128
TWELFTH = 1.0 / 12.0
Y = ("grid", "gy")
VMEM_LIMIT = 24 << 20


def turn(x, by, axis):
    return pltpu.roll(x, by % x.shape[axis], axis)


def lateral12(u):
    near = (turn(u, 1, 0) + turn(u, -1, 0)) + (turn(u, 1, 1) + turn(u, -1, 1))
    far = (turn(u, 2, 0) + turn(u, -2, 0)) + (turn(u, 2, 1) + turn(u, -2, 1))
    return 16.0 * near - far - 60.0 * u


def depth12(ref, c, k):
    last = ref.shape[1] - 1

    def tap(offset, weight):
        at = k + offset
        inside = jnp.logical_and(at >= 0, at <= last)
        return jnp.where(inside, weight, 0.0) * ref[c, jnp.clip(at, 0, last)]

    return (tap(-1, 16.0) + tap(1, 16.0)) + (tap(-2, -1.0) + tap(2, -1.0)) - 30.0 * ref[c, k]


def pack_columns(ref):
    comps, layers, rows, cols = ref.shape
    lane = lax.broadcasted_iota(jnp.int32, (rows, LANES), 1)
    zero = jnp.zeros((rows, LANES), jnp.float32)

    def body(k, carry):
        first, last = carry
        for c in range(comps):
            at = 2 * (c * layers + k)
            here = jnp.logical_and(lane >= at, lane < at + 2)
            first = jnp.where(here, pltpu.roll(ref[c, k, :, :LANES], at, 1), first)
            last = jnp.where(here, pltpu.roll(ref[c, k, :, cols - LANES :], lax.rem(at + 2, LANES), 1), last)
        return first, last

    first, last = lax.fori_loop(0, layers, body, (zero, zero))
    even = lax.rem(lane, 2) == 0
    before = jnp.where(even, -first, 16.0 * turn(first, 1, 1) - first)
    after = jnp.where(even, 16.0 * turn(last, -1, 1) - last, -last)
    return before, after


def pack_rows(ref, c, k):
    rows = ref.shape[2]
    u0, u1 = ref[c, k, 0:1, :], ref[c, k, 1:2, :]
    v0, v1 = ref[c, k, rows - 2 : rows - 1, :], ref[c, k, rows - 1 : rows, :]
    return (-u0, 16.0 * u0 - u1), (16.0 * v1 - v0, -v1)


def pack_all(uf, uc, x_down, x_up, y_down, y_up):
    comps, layers, rows, cols = uf.shape
    crows = uc.shape[2]
    for ref, lo, hi in ((uf, 0, rows), (uc, rows, rows + crows)):
        before, after = pack_columns(ref)
        y_down[lo:hi, :] = before
        y_up[lo:hi, :] = after

    def body(k, _):
        for c in range(comps):
            p = c * layers + k
            for ref, at in ((uf, slice(0, cols)), (uc, slice(cols, None))):
                down, up = pack_rows(ref, c, k)
                for r in range(2):
                    x_down[p, r : r + 1, at] = down[r]
                    x_up[p, r : r + 1, at] = up[r]
        return 0

    lax.fori_loop(0, layers, body, 0)


def pack_kernel(uf, uc, x_down, x_up, y_down, y_up):
    pack_all(uf, uc, x_down, x_up, y_down, y_up)


def main_kernel(uf, pf, sp, me, uc, pc, cs, vf, vc, latf, latc):
    comps, layers = uf.shape[:2]

    def fine(k, _):
        s12 = sp[k] * TWELFTH
        m2 = me[k] * me[k]
        for c in range(comps):
            u = uf[c, k]
            lat = lateral12(u)
            latf[c] = lat
            vf[c, k] = 2.0 * u - pf[c, k] + s12 * (lat + m2 * depth12(uf, c, k))
        return 0

    lax.fori_loop(0, layers, fine, 0)

    def coarse(i, _):
        k = layers - 1 - i
        s12 = cs[k] * TWELFTH
        for c in range(comps):
            u = uc[c, k]
            lat = lateral12(u)
            latc[c] = lat
            vc[c, k] = 2.0 * u - pc[c, k] + s12 * (lat + depth12(uc, c, k))
        return 0

    lax.fori_loop(0, layers, coarse, 0)


def pieces(x):
    a = x.astype(jnp.bfloat16)
    rest = x - a.astype(jnp.float32)
    b = rest.astype(jnp.bfloat16)
    c = (rest - b.astype(jnp.float32)).astype(jnp.bfloat16)
    return jnp.concatenate([a, b, c], axis=-1)


def edges_of(mine, theirs, there):
    return jnp.where(there, theirs, 0.0) - mine


def interface(lf, lc, uf, sp, me, uc, cs, tr, sh, widen, narrow, tall, change, row):
    comps, layers, rows, cols = uf.shape
    crows, ccols = sh.shape
    b = layers - 1

    def stretch(planes):
        wide = jnp.dot(pieces(jnp.concatenate(planes, axis=0)), widen[...], preferred_element_type=jnp.float32)
        n = len(planes) * crows
        for half in range(cols // LANES):
            part = wide[:, half * LANES : (half + 1) * LANES]
            tall[half, pl.ds(0, n, 2), :] = part
            tall[half, pl.ds(1, n, 2), :] = part
        return [
            jnp.concatenate(
                [tall[half, i * rows : (i + 1) * rows, :] for half in range(cols // LANES)], axis=1
            )
            for i in range(len(planes))
        ]

    def rows_of(planes):
        n = len(planes) * crows
        for i, plane in enumerate(planes):
            for half in range(cols // LANES):
                tall[half, i * rows : (i + 1) * rows, :] = plane[:, half * LANES : (half + 1) * LANES]
        return tuple(
            jnp.concatenate([tall[half, pl.ds(start, n, 2), :] for half in range(cols // LANES)], axis=1)
            for start in range(2)
        )

    s, m = sp[b], me[b]
    m2 = m * m
    gain = 1.0 / (s * m2)
    inv_m2 = 1.0 / m2
    cs0 = cs[0]
    inv_sh = 1.0 / sh[...]
    t = tr[...]
    c0 = [uc[c, 0] for c in range(comps)]
    pull = [
        cs0 * (lc[c] - 29.0 * uc[c, 0] + 16.0 * uc[c, 1] - uc[c, 2]) * TWELFTH for c in range(comps)
    ]
    wide = stretch([cs0] + pull + c0)
    alpha = gain * wide[0]
    beta, first, weighted = [], [], []
    for c in range(comps):
        ub, u1, u2 = uf[c, b], uf[c, b - 1], uf[c, b - 2]
        e = u2 - lf[c] * inv_m2 - 16.0 * u1 + 29.0 * ub
        bc = (12.0 * gain * wide[1 + c] + e) * (1.0 / 14.0)
        beta.append(bc)
        first.append(jnp.max(jnp.abs(alpha * wide[1 + comps + c] + bc - ub), axis=0, keepdims=True))
        weighted.append(t * bc)
        weighted.append(t * (u2 - 8.0 * u1 + 7.0 * ub))
        weighted.append(t * (u2 - 8.0 * u1 + ub))
    even_rows, odd_rows = rows_of([t * alpha] + weighted)
    sums = jnp.dot(pieces(even_rows + odd_rows), narrow[...], preferred_element_type=jnp.float32)
    even_rows, odd_rows = rows_of([alpha])
    top = jnp.maximum(even_rows, odd_rows)
    top = jnp.maximum(top, turn(top, -1, 1))
    lane = lax.broadcasted_iota(jnp.int32, top.shape, 1)
    top = jnp.where(lax.rem(lane, 2) == 0, top, 0.0)
    top = jnp.dot(pieces(top), narrow[...], preferred_element_type=jnp.float32)

    def part(i):
        return sums[i * crows : (i + 1) * crows, :]

    rate = part(0) * (0.5 * inv_sh)
    history = [[], [], [], []]
    c3s, c4s = [], []
    for c in range(comps):
        q6 = (8.0 * uc[c, 1] - uc[c, 0] - uc[c, 2]) * (1.0 / 6.0)
        pushed, start, still = part(1 + 3 * c), part(2 + 3 * c), part(3 + 3 * c)
        base = q6 - (still * TWELFTH + 0.5 * pushed) * inv_sh
        c1 = q6 - start * (TWELFTH * inv_sh)
        c2 = base - rate * c0[c]
        c3 = base - rate * c1
        c4 = base - rate * c2
        d1, d2, d3, d4 = (jnp.abs(x) for x in (c1 - c0[c], c2 - c1, c3 - c2, c4 - c3))
        history[0].append(d1)
        history[1].append(jnp.maximum(d2, top * d1))
        history[2].append(jnp.maximum(d3, top * d2))
        history[3].append(jnp.maximum(d4, top * d3))
        c3s.append(c3)
        c4s.append(c4)
    for n in range(4):
        d = jnp.maximum(jnp.maximum(history[n][0], history[n][1]), history[n][2])
        d = jnp.max(d, axis=0, keepdims=True)
        if n == 0:
            f = jnp.maximum(jnp.maximum(first[0], first[1]), first[2])
            for half in range(cols // LANES):
                d = jnp.maximum(d, f[:, half * LANES : (half + 1) * LANES])
        change[row + n : row + n + 1, :] = jnp.broadcast_to(jnp.max(d, axis=1, keepdims=True), (1, LANES))
    wide = stretch(c3s)
    return [alpha * wide[c] + beta[c] for c in range(comps)], c4s


def fix_kernel(
    row,
    vf_in, vc_in, latf, latc, uf, sp, me, uc, cs, tr, sh, widen, narrow, change_in,
    own_xd, own_xu, own_yd, own_yu, got_xd, got_xu, got_yd, got_yu,
    *refs,
):
    repack = len(refs) > 7
    vf, vc, change = refs[:3]
    lf, lc, tall, ycorr = refs[-4:]
    comps, layers, rows, cols = uf.shape
    crows = uc.shape[2]
    x_at, x_n = lax.axis_index("gx"), lax.axis_size("gx")
    y_at, y_n = lax.axis_index(Y), lax.axis_size(Y)
    ycorr[0] = edges_of(own_yu[...], got_yu[...], y_at > 0)
    ycorr[1] = edges_of(own_yd[...], got_yd[...], y_at < y_n - 1)
    change[...] = change_in[...]

    def row_edges(p, at):
        low = edges_of(own_xu[p, :, at], got_xu[p, :, at], x_at > 0)
        high = edges_of(own_xd[p, :, at], got_xd[p, :, at], x_at < x_n - 1)
        return low, high

    def column_edges(p, at, n):
        lane = lax.broadcasted_iota(jnp.int32, (n, LANES), 1)
        low = pltpu.roll(ycorr[0, at, :], lax.rem(LANES - 2 * p, LANES), 1)
        high = pltpu.roll(ycorr[1, at, :], lax.rem(2 * LANES - 2 - 2 * p, LANES), 1)
        return jnp.where(lane < 2, low, 0.0), jnp.where(lane >= LANES - 2, high, 0.0)

    def add_edges(get, put, scale, p, xs, ys, n, width):
        low, high = column_edges(p, ys, n)
        if width == LANES:
            put(slice(0, n), slice(0, width), scale(slice(0, n), slice(0, width), low + high))
        else:
            put(slice(0, n), slice(0, LANES), scale(slice(0, n), slice(0, LANES), low))
            put(slice(0, n), slice(width - LANES, width), scale(slice(0, n), slice(width - LANES, width), high))
        low, high = row_edges(p, xs)
        put(slice(0, 2), slice(0, width), scale(slice(0, 2), slice(0, width), low))
        put(slice(n - 2, n), slice(0, width), scale(slice(n - 2, n), slice(0, width), high))

    fine_x, fine_y = slice(0, cols), slice(0, rows)
    coarse_x, coarse_y = slice(cols, cols + uc.shape[3]), slice(rows, rows + crows)

    for c in range(comps):
        lf[c] = latf[c]
        lc[c] = latc[c]

        def put_f(r, l, x, c=c):
            lf[c, r, l] = lf[c, r, l] + x

        def put_c(r, l, x, c=c):
            lc[c, r, l] = lc[c, r, l] + x

        plain = lambda r, l, x: x
        add_edges(None, put_f, plain, c * layers + layers - 1, fine_x, fine_y, rows, cols)
        add_edges(None, put_c, plain, c * layers, coarse_x, coarse_y, crows, uc.shape[3])

    ghost_f, ghost_c = interface(lf, lc, uf, sp, me, uc, cs, tr, sh, widen, narrow, tall, change, row)

    def all_edges(k, _):
        for c in range(comps):
            p = c * layers + k
            for v, v_in, speed, xs, ys, n, width in (
                (vf, vf_in, sp, fine_x, fine_y, rows, cols),
                (vc, vc_in, cs, coarse_x, coarse_y, crows, uc.shape[3]),
            ):

                def scale(r, l, x, speed=speed):
                    return speed[k, r, l] * TWELFTH * x

                def put(r, l, x, v=v):
                    v[c, k, r, l] = v[c, k, r, l] + x

                add_edges(None, put, scale, p, xs, ys, n, width)
        return 0

    b = layers - 1
    s_last = sp[b] * me[b] * me[b] * TWELFTH
    s_next = sp[b - 1] * me[b - 1] * me[b - 1] * TWELFTH
    for c in range(comps):
        vf[c, b] = vf_in[c, b] + s_last * (14.0 * ghost_f[c] + uf[c, b])
        vf[c, b - 1] = vf_in[c, b - 1] - s_next * ghost_f[c]
        vc[c, 0] = vc_in[c, 0] + cs[0] * TWELFTH * (14.0 * ghost_c[c] + uc[c, 0])
        vc[c, 1] = vc_in[c, 1] - cs[1] * TWELFTH * ghost_c[c]
    lax.fori_loop(0, layers, all_edges, 0)
    if repack:
        pack_all(vf, vc, *refs[3:7])


def spec():
    return pl.BlockSpec(memory_space=pltpu.VMEM)


def here(x):
    return pltpu.with_memory_space_constraint(x, pltpu.VMEM)


def call(kernel, args, outs, scratch=(), alias={}, flops=0):
    return pl.pallas_call(
        kernel,
        out_shape=tuple(outs),
        in_specs=[spec() for _ in args],
        out_specs=tuple(spec() for _ in outs),
        scratch_shapes=list(scratch),
        input_output_aliases=alias,
        cost_estimate=pl.CostEstimate(flops=flops, bytes_accessed=flops, transcendentals=0),
        compiler_params=pltpu.CompilerParams(vmem_limit_bytes=VMEM_LIMIT),
    )(*[here(x) for x in args])


def exchange(parts):
    x_down, x_up, y_down, y_up = parts

    def ring(value, axis, by):
        n = lax.axis_size(axis)
        return lax.ppermute(value, axis, [(i, (i + by) % n) for i in range(n)])

    return (ring(x_down, "gx", -1), ring(x_up, "gx", 1), ring(y_down, Y, -1), ring(y_up, Y, 1))


def largest(value):
    for axis in ("gx", "gy", "grid"):
        n, far = lax.axis_size(axis), 1
        while far < n:
            value = jnp.maximum(value, lax.ppermute(value, axis, [(i, (i + far) % n) for i in range(n)]))
            far *= 2
    return value


def on_device(
    fine_field, fine_previous, fine_speed, fine_metric, coarse_field, coarse_previous, coarse_speed,
    fine_traction, coarse_shear,
):
    f32 = jnp.float32
    comps, layers, rows, cols = fine_field.shape
    crows, ccols = coarse_field.shape[2:]
    fine = pltpu.VMEM(fine_field.shape, f32)
    coarse = pltpu.VMEM(coarse_field.shape, f32)
    edge_outs = [
        pltpu.VMEM((comps * layers, 2, cols + ccols), f32),
        pltpu.VMEM((comps * layers, 2, cols + ccols), f32),
        pltpu.VMEM((rows + crows, LANES), f32),
        pltpu.VMEM((rows + crows, LANES), f32),
    ]
    picks = np.zeros((cols, ccols), np.float32)
    picks[np.arange(cols), np.arange(cols) // 2] = 1.0
    narrow = jnp.asarray(np.tile(picks, (3, 1)), jnp.bfloat16)
    widen = jnp.asarray(np.tile(picks.T, (3, 1)), jnp.bfloat16)
    change = jnp.zeros((4 * STEPS, LANES), f32)
    uf, uc, pf, pc = fine_field, coarse_field, fine_previous, coarse_previous
    mine = call(pack_kernel, (uf, uc), edge_outs)
    for step in range(STEPS):
        theirs = exchange(mine)
        vf, vc, latf, latc = call(
            main_kernel,
            (uf, pf, fine_speed, fine_metric, uc, pc, coarse_speed),
            [fine, coarse, pltpu.VMEM((comps, rows, cols), f32), pltpu.VMEM((comps, crows, ccols), f32)],
            flops=40_000_000,
        )
        more = step < STEPS - 1
        results = call(
            functools.partial(fix_kernel, 4 * step),
            (vf, vc, latf, latc, uf, fine_speed, fine_metric, uc, coarse_speed, fine_traction, coarse_shear)
            + (widen, narrow, change) + tuple(mine) + tuple(theirs),
            [fine, coarse, pltpu.VMEM(change.shape, f32)] + (edge_outs if more else []),
            scratch=[
                pltpu.VMEM((comps, rows, cols), f32),
                pltpu.VMEM((comps, crows, ccols), f32),
                pltpu.VMEM((cols // LANES, 10 * rows, LANES), f32),
                pltpu.VMEM((2, rows + crows, LANES), f32),
            ],
            alias={0: 0, 1: 1},
            flops=20_000_000,
        )
        pf, pc = uf, uc
        uf, uc, change = results[:3]
        mine = results[3:]
    history = largest(change)
    return uf, uc, history[:, 0].reshape(STEPS, 4)


def solution(mesh):
    field = P(None, None, "gx", Y)
    layered = P(None, "gx", Y)
    plane = P("gx", Y)
    return jax.shard_map(
        on_device,
        mesh=mesh,
        in_specs=(field, field, layered, layered, field, field, layered, plane, plane),
        out_specs=(field, field, P()),
        check_vma=False,
    )
```

time: 655 us -> 70.1 us (0.11); the launches traced: 646 us -> 69.9 us
  local copies, waits for them, and re-layouts: 290 us -> 8.24 us
  other arithmetic: 231 us -> 0.02 us
  blocking collectives: 50 us -> 0 us
  Pallas kernels: 0 us -> 29.7 us
  starting transfers between devices: 43.2 us -> 15.8 us
  between operations: 12.5 us -> 0.85 us
    slice x70 -> x1, local copies, waits for them, and re-layouts: 106 us -> 0.12 us  [on_device(): return (uf, uc, history[:, 0].reshape(STEPS, 4))]
    mul x18 -> x0, other arithmetic: 95.5 us -> none  [the longest x8 89.1 us: on_device(): 24.0 * restrict(send_fine) / coarse_shear]
    reshape x15 -> x0, local copies, waits for them, and re-layouts: 88.8 us -> none  [the longest x6 84.4 us: restrict(): values.reshape(values.shape[:-2] + (values.shape[-2] // 2, 2, values.shap...]
    add x6 -> x0, other arithmetic: 85.7 us -> none  [the longest x2 76.3 us: on_device(): new_fine = 2.0 * fine_field - fine_previous + fine_change]
    pmax x1 -> x0, blocking collectives: 50 us -> none  [record(): history.append(lax.pmax(local_change, ('grid', 'gx', 'gy')))]
    div x11 -> x0, other arithmetic: 33.9 us -> none  [the longest x8 33.1 us: on_device(): send_fine = fine_traction * (fine_base + 6.0 * ghost_fine) / 12.0]
    pallas_call x0 -> x5, Pallas kernels: none -> 29.7 us  [call(): pl.pallas_call(kernel, out_shape=tuple(outs), in_specs=[spec() for _ in a...]
    add x4 -> x0, local copies, waits for them, and re-layouts: 28.4 us -> none  [on_device(): send_fine = fine_traction * (fine_base + 6.0 * ghost_fine) / 12.0]
  transfers between devices with their start and end apart: 16 -> 13, of which waited for: 5 -> 4; matrix products, arithmetic and copies ran while one was open for 28% -> 4% of each run, Pallas kernels for 0% -> 21%
where the time goes in v1:
time: 70.1 us; the launch traced here: 69.9 us
  Pallas kernels  29.7 us (42%)
  starting transfers between devices  15.8 us (23%)
  waiting for transfers between devices  15.2 us (22%)
  local copies, waits for them, and re-layouts  8.24 us (12%)
  between operations  0.85 us (1%)
    pallas_call x5, Pallas kernels, call(): pl.pallas_call(kernel, out_shape=tuple(outs), in_specs=[spec() for _ in a...  29.7 us
    ppermute x5, waiting for transfers between devices, largest(): lax.ppermute(value, axis, [(i, (i + far) % n) for i in range(n)])  15.2 us
    ppermute x8, starting transfers between devices, ring(): return lax.ppermute(value, axis, [(i, (i + by) % n) for i in range(n)])  12.9 us
    unnamed x26, local copies, waits for them, and re-layouts  7.48 us
    ppermute x5, starting transfers between devices, largest(): lax.ppermute(value, axis, [(i, (i + far) % n) for i in range(n)])  2.91 us
  transfers between devices with their start and end apart: 13, of which 4 were waited for; matrix products, arithmetic and copies ran while one was open for 4% of the time, Pallas kernels for 21%

profile of v1, /device:TPU:0, one launch (start us, length us, event | category | flops | bytes accessed | tf_op | source)
XLA Modules:
  0.0 69.9 jit_solution(15418151005018410904)
XLA Ops:
  0.6 1.9 %copy-done = f32[3,16,64,256]{3,2,1,0:T(8,128)S(1)} copy-done((f32[3,16,64,256]{3,2,1,0:T(8,128)S(1)}, f32[3,16,64,256]{3,2,1,0:T(8,128)}, u32[]{:S(2)}) %copy-start) | copy-done | bytes 3145752
  2.5 1.1 %copy-done.3 = f32[3,16,32,128]{3,2,1,0:T(8,128)S(1)} copy-done((f32[3,16,32,128]{3,2,1,0:T(8,128)S(1)}, f32[3,16,32,128]{3,2,1,0:T(8,128)}, u32[]{:S(2)}) %copy-start.3) | copy-done | bytes 786456
  3.7 3.8 %shard_map.131 = (f32[48,2,384]{2,1,0:T(2,128)S(1)}, f32[48,2,384]{2,1,0:T(2,128)S(1)}, f32[96,128]{1,0:T(8,128)S(1)}, f32[96,128]{1,0:T(8,128)S(1)}) custom-call(f32[3,16,64,256]{3,2,1,0:T(8,128)S(1)} %copy-done, f32[3,16,32,128]{3,2,1,0:T(8,128)S(1)} %copy-done.3), custom_call_target="tpu_custom_call" | custom-call | tf_op jit(solution)/shard_map/pallas_call | solution.py:323
  7.5 2.5 %collective-permute-start = (f32[48,2,384]{2,1,0:T(2,128)S(1)}, f32[48,2,384]{2,1,0:T(2,128)S(1)}, u32[]{:S(2)}, u32[]{:S(2)}) collective-permute-start(f32[48,2,384]{2,1,0:T(2,128)S(1)} %get-tuple-element.29.own_xd), channel_id=1, source_target_pairs={{0,12},{4,0},{8,4},{12,8},{1,13},{5,1},{9,5},{13,9},{2,14},{6,2},{... | collective-permute-start | bytes 442376 | tf_op jit(solution)/shard_map/ppermute | solution.py:340
  9.9 0.0 collective-permute-start.1
  9.9 4.5 %collective-permute-start.2 = (f32[96,128]{1,0:T(8,128)S(1)}, f32[96,128]{1,0:T(8,128)S(1)}, u32[]{:S(2)}, u32[]{:S(2)}) collective-permute-start(f32[96,128]{1,0:T(8,128)S(1)} %get-tuple-element.31.own_yd), channel_id=1, source_target_pairs={{0,19},{1,0},{2,1},{3,2},{16,3},{17,16},{18,17},{19,18},{4,23},{5,... | collective-permute-start | bytes 147464 | tf_op jit(solution)/shard_map/ppermute | solution.py:340
  14.5 0.0 collective-permute-start.3
  14.5 0.0 copy-start.6
  14.5 1.9 %copy-done.6 = f32[3,16,64,256]{3,2,1,0:T(8,128)S(1)} copy-done((f32[3,16,64,256]{3,2,1,0:T(8,128)S(1)}, f32[3,16,64,256]{3,2,1,0:T(8,128)}, u32[]{:S(2)}) %copy-start.6) | copy-done | bytes 3145752
  16.4 7.2 %shard_map.130 = (f32[3,16,64,256]{3,2,1,0:T(8,128)S(1)}, f32[3,16,32,128]{3,2,1,0:T(8,128)S(1)}, f32[3,64,256]{2,1,0:T(8,128)S(1)}, f32[3,32,128]{2,1,0:T(8,128)S(1)}) custom-call(f32[3,16,64,256]{3,2,1,0:T(8,128)S(1)} %copy-done, f32[3,16,64,256]{3,2,1,0:T(8,128)S(1)} %copy-done.6, f32[16,64,256]{2,1,0:T(8,128)S(1)} %copy-done.1, ...), custom_call_target="tpu_custom_call" | custom-call | flops 40000000 | bytes 40000000 | tf_op jit(solution)/shard_map/pallas_call | solution.py:323
  23.6 0.0 collective-permute-done.2.got_yd
  23.7 0.0 collective-permute-done.got_xd
  23.7 0.0 collective-permute-done.1.got_xu
  23.7 7.7 %shard_map.132 = (f32[3,16,64,256]{3,2,1,0:T(8,128)S(1)}, f32[3,16,32,128]{3,2,1,0:T(8,128)S(1)}, f32[8,128]{1,0:T(8,128)S(1)}, f32[48,2,384]{2,1,0:T(2,128)S(1)...) custom-call(f32[3,16,64,256]{3,2,1,0:T(8,128)S(1)} %get-tuple-elemen, ...), custom_call_target="tpu_custom_call", output_to_operand_aliasing={{0}: (0, {}), {1}: (1, {})} | custom-call | flops 20000000 | bytes 20000000 | tf_op jit(solution)/shard_map/pallas_call | solution.py:323
  31.4 1.5 %collective-permute-start.4 = (f32[48,2,384]{2,1,0:T(2,128)S(1)}, f32[48,2,384]{2,1,0:T(2,128)S(1)}, u32[]{:S(2)}, u32[]{:S(2)}) collective-permute-start(f32[48,2,384]{2,1,0:T(2,128)S(1)} %get-tuple-element.40.own_xd), channel_id=1, source_target_pairs={{0,12},{4,0},{8,4},{12,8},{1,13},{5,1},{9,5},{13,9},{2,14},{6,2},{... | collective-permute-start | bytes 442376 | tf_op jit(solution)/shard_map/ppermute | solution.py:340
  33.0 4.4 %collective-permute-start.6 = (f32[96,128]{1,0:T(8,128)S(1)}, f32[96,128]{1,0:T(8,128)S(1)}, u32[]{:S(2)}, u32[]{:S(2)}) collective-permute-start(f32[96,128]{1,0:T(8,128)S(1)} %get-tuple-element.42.own_yd), channel_id=1, source_target_pairs={{0,19},{1,0},{2,1},{3,2},{16,3},{17,16},{18,17},{19,18},{4,23},{5,... | collective-permute-start | bytes 147464 | tf_op jit(solution)/shard_map/ppermute | solution.py:340
  37.4 0.0 collective-permute-start.7
  37.4 7.3 %shard_map.133 = (f32[3,16,64,256]{3,2,1,0:T(8,128)S(1)}, f32[3,16,32,128]{3,2,1,0:T(8,128)S(1)}, f32[3,64,256]{2,1,0:T(8,128)S(1)}, f32[3,32,128]{2,1,0:T(8,128)S(1)}) custom-call(f32[3,16,64,256]{3,2,1,0:T(8,128)S(1)} %get-tuple-element.33.uf, f32[3,16,64,256]{3,2,1,0:T(8,128)S(1)} %copy-done, f32[16,64,256]{2,1,0:T(8,128)S(1)} %copy-done.1, ...), custom_call_target="tpu_custom_call" | custom-call | flops 40000000 | bytes 40000000 | tf_op jit(solution)/shard_map/pallas_call | solution.py:323
  44.7 0.0 collective-permute-done.6.got_yd
  44.7 3.7 %shard_map.134 = (f32[3,16,64,256]{3,2,1,0:T(8,128)S(1)}, f32[3,16,32,128]{3,2,1,0:T(8,128)S(1)}, f32[8,128]{1,0:T(8,128)S(1)}) custom-call(f32[3,16,64,256]{3,2,1,0:T(8,128)S(1)} %get-tuple-element.35.vf_in, f32[3,16,32,128]{3,2,1,0:T(8,128)S(1)} %get-tuple-element.36.vc_in, ...), custom_call_target="tpu_custom_call", output_to_operand_aliasing={{0}: (0, {}), {1}: (1, {})} | custom-call | flops 20000000 | bytes 20000000 | tf_op jit(solution)/shard_map/pallas_call | solution.py:323
  48.4 0.5 collective-permute-start.8
  48.9 2.6 %collective-permute-done.8 = f32[8,128]{1,0:T(8,128)S(1)} collective-permute-done((f32[8,128]{1,0:T(8,128)S(1)}, f32[8,128]{1,0:T(8,128)S(1)}, u32[]{:S(2)}, u32[]{:S(2)}) %collective-permute-start.8) | collective-permute-done | bytes 4128 | tf_op jit(solution)/shard_map/ppermute | solution.py:349
  51.5 0.6 collective-permute-start.9
  52.2 3.0 %collective-permute-done.9 = f32[8,128]{1,0:T(8,128)S(1)} collective-permute-done((f32[8,128]{1,0:T(8,128)S(1)}, f32[8,128]{1,0:T(8,128)S(1)}, u32[]{:S(2)}, u32[]{:S(2)}) %collective-permute-start.9) | collective-permute-done | bytes 4128 | tf_op jit(solution)/shard_map/ppermute | solution.py:349
  55.1 5.4 %collective-permute-done.10 = f32[8,128]{1,0:T(8,128)S(1)} collective-permute-done((f32[8,128]{1,0:T(8,128)S(1)}, f32[8,128]{1,0:T(8,128)S(1)}, u32[]{:S(2)}, u32[]{:S(2)}) %collective-permute-start.10) | collective-permute-done | bytes 4128 | tf_op jit(solution)/shard_map/ppermute | solution.py:349
  60.6 0.3 collective-permute-start.11
  60.8 4.2 %collective-permute-done.11 = f32[8,128]{1,0:T(8,128)S(1)} collective-permute-done((f32[8,128]{1,0:T(8,128)S(1)}, f32[8,128]{1,0:T(8,128)S(1)}, u32[]{:S(2)}, u32[]{:S(2)}) %collective-permute-start.11) | collective-permute-done | bytes 4128 | tf_op jit(solution)/shard_map/ppermute | solution.py:349
  65.1 1.5 %collective-permute-start.12 = (f32[8,128]{1,0:T(8,128)S(1)}, f32[8,128]{1,0:T(8,128)S(1)}, u32[]{:S(2)}, u32[]{:S(2)}) collective-permute-start(f32[8,128]{1,0:T(8,128)S(1)} %max.18), channel_id=1, source_target_pairs={{0,16},{16,0},{1,17},{17,1},{2,18},{18,2},{3,19},{19,3},{4,20},{20... | collective-permute-start | bytes 12296 | tf_op jit(solution)/shard_map/ppermute | solution.py:349
  66.6 1.7 %copy.22 = f32[3,16,64,256]{3,2,1,0:T(8,128)} copy(f32[3,16,64,256]{3,2,1,0:T(8,128)S(1)} %get-tuple-element.47) | data formatting | bytes 6291456
  68.2 0.9 %copy.23 = f32[3,16,32,128]{3,2,1,0:T(8,128)} copy(f32[3,16,32,128]{3,2,1,0:T(8,128)S(1)} %get-tuple-element.48) | data formatting | bytes 1572864
  69.1 0.1 slice_reduce_fusion
  69.2 0.6 reshape_squeeze.3
  (33 shorter events, 0.1 us)
Async XLA Ops:
  0.6 1.9 %copy-start = (f32[3,16,64,256]{3,2,1,0:T(8,128)S(1)}, f32[3,16,64,256]{3,2,1,0:T(8,128)}, u32[]{:S(2)}) copy-start(f32[3,16,64,256]{3,2,1,0:T(8,128)} %pf.3) | copy-start | bytes 9437188
  2.5 1.1 %copy-start.3 = (f32[3,16,32,128]{3,2,1,0:T(8,128)S(1)}, f32[3,16,32,128]{3,2,1,0:T(8,128)}, u32[]{:S(2)}) copy-start(f32[3,16,32,128]{3,2,1,0:T(8,128)} %pc.3) | copy-start | bytes 2359300
  3.7 10.8 %copy-start.1 = (f32[16,64,256]{2,1,0:T(8,128)S(1)}, f32[16,64,256]{2,1,0:T(8,128)}, u32[]{:S(2)}) copy-start(f32[16,64,256]{2,1,0:T(8,128)} %sp.7) | copy-start | bytes 3145732
  3.7 10.8 %copy-start.2 = (f32[16,64,256]{2,1,0:T(8,128)S(1)}, f32[16,64,256]{2,1,0:T(8,128)}, u32[]{:S(2)}) copy-start(f32[16,64,256]{2,1,0:T(8,128)} %me.7) | copy-start | bytes 3145732
  3.7 10.8 %copy-start.4 = (f32[3,16,32,128]{3,2,1,0:T(8,128)S(1)}, f32[3,16,32,128]{3,2,1,0:T(8,128)}, u32[]{:S(2)}) copy-start(f32[3,16,32,128]{3,2,1,0:T(8,128)} %pc.3) | copy-start | bytes 2359300
  3.7 10.8 %copy-start.5 = (f32[16,32,128]{2,1,0:T(8,128)S(1)}, f32[16,32,128]{2,1,0:T(8,128)}, u32[]{:S(2)}) copy-start(f32[16,32,128]{2,1,0:T(8,128)} %cs.7) | copy-start | bytes 786436
  3.7 10.8 %copy-start.7 = (f32[3,16,32,128]{3,2,1,0:T(8,128)S(1)}, f32[3,16,32,128]{3,2,1,0:T(8,128)}, u32[]{:S(2)}) copy-start(f32[3,16,32,128]{3,2,1,0:T(8,128)} %pc.2) | copy-start | bytes 2359300
  7.5 16.2 %collective-permute-start = (f32[48,2,384]{2,1,0:T(2,128)S(1)}, f32[48,2,384]{2,1,0:T(2,128)S(1)}, u32[]{:S(2)}, u32[]{:S(2)}) collective-permute-start(f32[48,2,384]{2,1,0:T(2,128)S(1)} %get-tuple-element.29.own_xd), channel_id=1, source_target_pairs={{0,12},{4,0},{8,4},{12,8},{1,13},{5,1},{9,5},{13,9},{2,14},{6,2},{... | collective-permute-start | bytes 442376 | tf_op jit(solution)/shard_map/ppermute | solution.py:340
  9.9 13.7 %collective-permute-start.1 = (f32[48,2,384]{2,1,0:T(2,128)S(1)}, f32[48,2,384]{2,1,0:T(2,128)S(1)}, u32[]{:S(2)}, u32[]{:S(2)}) collective-permute-start(f32[48,2,384]{2,1,0:T(2,128)S(1)} %get-tuple-element.30.own_xu), channel_id=1, source_target_pairs={{0,4},{4,8},{8,12},{12,0},{1,5},{5,9},{9,13},{13,1},{2,6},{6,10},{... | collective-permute-start | bytes 442376 | tf_op jit(solution)/shard_map/ppermute | solution.py:340
  9.9 13.7 %collective-permute-start.2 = (f32[96,128]{1,0:T(8,128)S(1)}, f32[96,128]{1,0:T(8,128)S(1)}, u32[]{:S(2)}, u32[]{:S(2)}) collective-permute-start(f32[96,128]{1,0:T(8,128)S(1)} %get-tuple-element.31.own_yd), channel_id=1, source_target_pairs={{0,19},{1,0},{2,1},{3,2},{16,3},{17,16},{18,17},{19,18},{4,23},{5,... | collective-permute-start | bytes 147464 | tf_op jit(solution)/shard_map/ppermute | solution.py:340
  14.5 9.2 %collective-permute-start.3 = (f32[96,128]{1,0:T(8,128)S(1)}, f32[96,128]{1,0:T(8,128)S(1)}, u32[]{:S(2)}, u32[]{:S(2)}) collective-permute-start(f32[96,128]{1,0:T(8,128)S(1)} %get-tuple-element.32.own_yu), channel_id=1, source_target_pairs={{0,1},{1,2},{2,3},{3,16},{16,17},{17,18},{18,19},{19,0},{4,5},{5,6... | collective-permute-start | bytes 147464 | tf_op jit(solution)/shard_map/ppermute | solution.py:340
  14.5 1.9 %copy-start.6 = (f32[3,16,64,256]{3,2,1,0:T(8,128)S(1)}, f32[3,16,64,256]{3,2,1,0:T(8,128)}, u32[]{:S(2)}) copy-start(f32[3,16,64,256]{3,2,1,0:T(8,128)} %pf.2) | copy-start | bytes 9437188
  16.4 7.3 %copy-start.8 = (bf16[384,256]{1,0:T(8,128)(2,1)S(1)}, bf16[384,256]{1,0:T(8,128)(2,1)}, u32[]{:S(2)}) copy-start(bf16[384,256]{1,0:T(8,128)(2,1)} %constant.7.clone.widen) | copy-start | bytes 589828
  16.4 7.3 %copy-start.9 = (bf16[768,128]{1,0:T(8,128)(2,1)S(1)}, bf16[768,128]{1,0:T(8,128)(2,1)}, u32[]{:S(2)}) copy-start(bf16[768,128]{1,0:T(8,128)(2,1)} %constant.6.clone.narrow) | copy-start | bytes 589828
  16.4 7.3 %copy-start.10 = (f32[64,256]{1,0:T(8,128)S(1)}, f32[64,256]{1,0:T(8,128)}, u32[]{:S(2)}) copy-start(f32[64,256]{1,0:T(8,128)} %tr.3) | copy-start | bytes 196612
  16.4 7.3 %copy-start.11 = (f32[32,128]{1,0:T(8,128)S(1)}, f32[32,128]{1,0:T(8,128)}, u32[]{:S(2)}) copy-start(f32[32,128]{1,0:T(8,128)} %sh.3) | copy-start | bytes 49156
  31.4 13.2 %collective-permute-start.4 = (f32[48,2,384]{2,1,0:T(2,128)S(1)}, f32[48,2,384]{2,1,0:T(2,128)S(1)}, u32[]{:S(2)}, u32[]{:S(2)}) collective-permute-start(f32[48,2,384]{2,1,0:T(2,128)S(1)} %get-tuple-element.40.own_xd), channel_id=1, source_target_pairs={{0,12},{4,0},{8,4},{12,8},{1,13},{5,1},{9,5},{13,9},{2,14},{6,2},{... | collective-permute-start | bytes 442376 | tf_op jit(solution)/shard_map/ppermute | solution.py:340
  33.0 11.7 %collective-permute-start.5 = (f32[48,2,384]{2,1,0:T(2,128)S(1)}, f32[48,2,384]{2,1,0:T(2,128)S(1)}, u32[]{:S(2)}, u32[]{:S(2)}) collective-permute-start(f32[48,2,384]{2,1,0:T(2,128)S(1)} %get-tuple-element.41.own_xu), channel_id=1, source_target_pairs={{0,4},{4,8},{8,12},{12,0},{1,5},{5,9},{9,13},{13,1},{2,6},{6,10},{... | collective-permute-start | bytes 442376 | tf_op jit(solution)/shard_map/ppermute | solution.py:340
  33.0 11.7 %collective-permute-start.6 = (f32[96,128]{1,0:T(8,128)S(1)}, f32[96,128]{1,0:T(8,128)S(1)}, u32[]{:S(2)}, u32[]{:S(2)}) collective-permute-start(f32[96,128]{1,0:T(8,128)S(1)} %get-tuple-element.42.own_yd), channel_id=1, source_target_pairs={{0,19},{1,0},{2,1},{3,2},{16,3},{17,16},{18,17},{19,18},{4,23},{5,... | collective-permute-start | bytes 147464 | tf_op jit(solution)/shard_map/ppermute | solution.py:340
  37.4 7.3 %collective-permute-start.7 = (f32[96,128]{1,0:T(8,128)S(1)}, f32[96,128]{1,0:T(8,128)S(1)}, u32[]{:S(2)}, u32[]{:S(2)}) collective-permute-start(f32[96,128]{1,0:T(8,128)S(1)} %get-tuple-element.43.own_yu), channel_id=1, source_target_pairs={{0,1},{1,2},{2,3},{3,16},{16,17},{17,18},{18,19},{19,0},{4,5},{5,6... | collective-permute-start | bytes 147464 | tf_op jit(solution)/shard_map/ppermute | solution.py:340
  48.4 3.1 %collective-permute-start.8 = (f32[8,128]{1,0:T(8,128)S(1)}, f32[8,128]{1,0:T(8,128)S(1)}, u32[]{:S(2)}, u32[]{:S(2)}) collective-permute-start(f32[8,128]{1,0:T(8,128)S(1)} %get-tuple-element.46), channel_id=1, source_target_pairs={{0,4},{4,8},{8,12},{12,0},{1,5},{5,9},{9,13},{13,1},{2,6},{6,10},{... | collective-permute-start | bytes 12296 | tf_op jit(solution)/shard_map/ppermute | solution.py:349
  51.5 3.6 %collective-permute-start.9 = (f32[8,128]{1,0:T(8,128)S(1)}, f32[8,128]{1,0:T(8,128)S(1)}, u32[]{:S(2)}, u32[]{:S(2)}) collective-permute-start(f32[8,128]{1,0:T(8,128)S(1)} %max.15), channel_id=1, source_target_pairs={{0,8},{4,12},{8,0},{12,4},{1,9},{5,13},{9,1},{13,5},{2,10},{6,14},... | collective-permute-start | bytes 12296 | tf_op jit(solution)/shard_map/ppermute | solution.py:349
  55.1 5.4 %collective-permute-start.10 = (f32[8,128]{1,0:T(8,128)S(1)}, f32[8,128]{1,0:T(8,128)S(1)}, u32[]{:S(2)}, u32[]{:S(2)}) collective-permute-start(f32[8,128]{1,0:T(8,128)S(1)} %max.16), channel_id=1, source_target_pairs={{0,1},{1,2},{2,3},{3,0},{4,5},{5,6},{6,7},{7,4},{8,9},{9,10},{10,1... | collective-permute-start | bytes 12296 | tf_op jit(solution)/shard_map/ppermute | solution.py:349
  60.6 4.5 %collective-permute-start.11 = (f32[8,128]{1,0:T(8,128)S(1)}, f32[8,128]{1,0:T(8,128)S(1)}, u32[]{:S(2)}, u32[]{:S(2)}) collective-permute-start(f32[8,128]{1,0:T(8,128)S(1)} %max.17), channel_id=1, source_target_pairs={{0,2},{1,3},{2,0},{3,1},{4,6},{5,7},{6,4},{7,5},{8,10},{9,11},{10,... | collective-permute-start | bytes 12296 | tf_op jit(solution)/shard_map/ppermute | solution.py:349
  65.1 4.0 %collective-permute-start.12 = (f32[8,128]{1,0:T(8,128)S(1)}, f32[8,128]{1,0:T(8,128)S(1)}, u32[]{:S(2)}, u32[]{:S(2)}) collective-permute-start(f32[8,128]{1,0:T(8,128)S(1)} %max.18), channel_id=1, source_target_pairs={{0,16},{16,0},{1,17},{17,1},{2,18},{18,2},{3,19},{19,3},{4,20},{20... | collective-permute-start | bytes 12296 | tf_op jit(solution)/shard_map/ppermute | solution.py:349

commit v2 on v1

v2 whole, which is shorter than its diff:
```python
import functools

import jax
import jax.numpy as jnp
import numpy as np
from jax import lax
from jax.experimental import pallas as pl
from jax.experimental.pallas import tpu as pltpu
from jax.sharding import PartitionSpec as P

STEPS = 2
LANES = 128
TWELFTH = 1.0 / 12.0
Y = ("grid", "gy")
VMEM_LIMIT = 16 << 20
EARLY = 4


def turn(x, by, axis):
    return pltpu.roll(x, by % x.shape[axis], axis)


def lateral12(u):
    near = (turn(u, 1, 0) + turn(u, -1, 0)) + (turn(u, 1, 1) + turn(u, -1, 1))
    far = (turn(u, 2, 0) + turn(u, -2, 0)) + (turn(u, 2, 1) + turn(u, -2, 1))
    return 16.0 * near - far - 60.0 * u


def depth12(ref, c, k):
    last = ref.shape[1] - 1

    def pair(offset):
        taps = [ref[c, k + o] for o in (-offset, offset) if not isinstance(k, int) or 0 <= k + o <= last]
        return taps[0] + taps[1] if len(taps) == 2 else taps[0]

    return 16.0 * pair(1) - pair(2) - 30.0 * ref[c, k]


def layers_do(first, stop, total, body):
    a, b = max(first, 2), min(stop, total - 2)
    for k in range(first, min(stop, 2)):
        body(k)
    if b > a:
        pl.loop(a, b)(body)
    for k in range(max(first, total - 2), stop):
        body(k)


def pack_columns(ref, here, k, first, last):
    comps, layers, rows, cols = ref.shape
    for c in range(comps):
        at = 2 * (c * layers + k)
        inside = jnp.logical_and(here >= at, here < at + 2)
        first = jnp.where(inside, pltpu.roll(ref[c, k, :, :LANES], at, 1), first)
        last = jnp.where(inside, pltpu.roll(ref[c, k, :, cols - LANES :], (at + 2) % LANES, 1), last)
    return first, last


def pack_rows(ref, x_down, x_up, k, at):
    comps, layers, rows, cols = ref.shape
    sub = lax.broadcasted_iota(jnp.int32, (8, cols), 0)
    for c in range(comps):
        p = c * layers + k
        top, bottom = ref[c, k, 0:8, :], ref[c, k, rows - 8 : rows, :]
        down = jnp.where(sub == 1, 16.0 * turn(top, 1, 0), 0.0) - top
        up = jnp.where(sub == 0, 16.0 * turn(bottom, 1, 0), 0.0) - turn(bottom, 2, 0)
        x_down[p, :, at] = down[0:2]
        x_up[p, :, at] = up[0:2]


def pack_all(uf, uc, x_down, x_up, y_down, y_up, ready=None):
    layers, rows, cols = uf.shape[1:]
    crows, ccols = uc.shape[2:]
    for ref, ys, xs in ((uf, (0, rows), (0, cols)), (uc, (rows, rows + crows), (cols, cols + ccols))):
        n = ys[1] - ys[0]
        lane = lax.broadcasted_iota(jnp.int32, (n, LANES), 1)
        first = last = jnp.zeros((n, LANES), jnp.float32)
        for k in range(layers):
            if ready is not None:
                ready(ref is uc, k)
            first, last = pack_columns(ref, lane, k, first, last)
            pack_rows(ref, x_down, x_up, k, slice(*xs))
        even = lax.rem(lane, 2) == 0
        y_down[slice(*ys), :] = jnp.where(even, 0.0, 16.0 * turn(first, 1, 1)) - first
        y_up[slice(*ys), :] = jnp.where(even, 16.0 * turn(last, -1, 1), 0.0) - last


def load_kernel(uf_hbm, uc_hbm, uf, uc, x_down, x_up, y_down, y_up, sem):
    layers = uf.shape[1]
    group = 4
    copies = {}
    for coarse, src, dst in ((False, uf_hbm, uf), (True, uc_hbm, uc)):
        for g in range(0, layers, group):
            at = pl.ds(g, group)
            copies[coarse, g] = pltpu.make_async_copy(
                src.at[:, at], dst.at[:, at], sem.at[int(coarse) * (layers // group) + g // group]
            )
            copies[coarse, g].start()

    def ready(coarse, k):
        if (coarse, k) in copies:
            copies[coarse, k].wait()

    pack_all(uf, uc, x_down, x_up, y_down, y_up, ready)


def fine_plane(uf, pf, s12, m2, c, k):
    u = uf[c, k]
    return 2.0 * u - pf[c, k] + s12 * (lateral12(u) + m2 * depth12(uf, c, k))


def coarse_plane(uc, pc, s12, c, k):
    u = uc[c, k]
    return 2.0 * u - pc[c, k] + s12 * (lateral12(u) + depth12(uc, c, k))


def main_kernel(stop, uf, pf, sp, me, uc, pc, cs, vf, vc):
    comps, layers = uf.shape[:2]

    def fine(k):
        s12, m2 = sp[k] * TWELFTH, me[k] * me[k]
        for c in range(comps):
            vf[c, k] = fine_plane(uf, pf, s12, m2, c, k)

    def coarse(k):
        s12 = cs[k] * TWELFTH
        for c in range(comps):
            vc[c, k] = coarse_plane(uc, pc, s12, c, k)

    layers_do(0, stop, layers, fine)
    layers_do(0, layers, layers, coarse)


class Edges:
    def __init__(self, own, got, ycorr, shapes):
        self.own_xd, self.own_xu, own_yd, own_yu = own
        self.got_xd, self.got_xu, got_yd, got_yu = got
        self.ycorr = ycorr
        (self.layers, rows, cols), (crows, ccols) = shapes
        self.fine = (slice(0, rows), slice(0, cols), rows, cols)
        self.coarse = (slice(rows, rows + crows), slice(cols, cols + ccols), crows, ccols)
        x_at, x_n = lax.axis_index("gx"), lax.axis_size("gx")
        y_at, y_n = lax.axis_index(Y), lax.axis_size(Y)
        self.x_low, self.x_high = x_at > 0, x_at < x_n - 1
        ycorr[0] = jnp.where(y_at > 0, got_yu[...], 0.0) - own_yu[...]
        ycorr[1] = jnp.where(y_at < y_n - 1, got_yd[...], 0.0) - own_yd[...]

    def columns(self, grid, p):
        ys, xs, n, width = grid
        lane = lax.broadcasted_iota(jnp.int32, (n, LANES), 1)
        low = pltpu.roll(self.ycorr[0, ys, :], (LANES - 2 * p) % LANES, 1)
        high = pltpu.roll(self.ycorr[1, ys, :], (2 * LANES - 2 - 2 * p) % LANES, 1)
        low, high = jnp.where(lane < 2, low, 0.0), jnp.where(lane >= LANES - 2, high, 0.0)
        if width == LANES:
            return [(slice(0, LANES), low + high)]
        return [(slice(0, LANES), low), (slice(width - LANES, width), high)]

    def rows(self, grid, p):
        ys, xs, n, width = grid
        low = jnp.where(self.x_low, self.got_xu[p, :, xs], 0.0) - self.own_xu[p, :, xs]
        high = jnp.where(self.x_high, self.got_xd[p, :, xs], 0.0) - self.own_xd[p, :, xs]
        return [(slice(0, 2), low), (slice(n - 2, n), high)]

    def add(self, plane, grid, p, speed=None):
        for lanes, x in self.columns(grid, p):
            x = x if speed is None else x * (speed[:, lanes] * TWELFTH)
            plane[:, lanes] = plane[:, lanes] + x
        for rows, x in self.rows(grid, p):
            x = x if speed is None else x * (speed[rows, :] * TWELFTH)
            plane[rows, :] = plane[rows, :] + x


def pieces(x):
    a = x.astype(jnp.bfloat16)
    rest = x - a.astype(jnp.float32)
    b = rest.astype(jnp.bfloat16)
    c = (rest - b.astype(jnp.float32)).astype(jnp.bfloat16)
    return jnp.concatenate([a, b, c], axis=-1)


def interface(edges, uf, sp, me, uc, cs, tr, sh, widen, narrow, lf, lc, tall):
    comps, layers, rows, cols = uf.shape
    crows, ccols = sh.shape
    b = layers - 1

    for c in range(comps):
        lf[c] = lateral12(uf[c, b])
        lc[c] = lateral12(uc[c, 0])
        edges.add(lf.at[c], edges.fine, c * layers + b)
        edges.add(lc.at[c], edges.coarse, c * layers)

    def stretch(planes):
        wide = jnp.dot(pieces(jnp.concatenate(planes, axis=0)), widen[...], preferred_element_type=jnp.float32)
        n = len(planes) * crows
        for half in range(cols // LANES):
            part = wide[:, half * LANES : (half + 1) * LANES]
            tall[half, pl.ds(0, n, 2), :] = part
            tall[half, pl.ds(1, n, 2), :] = part
        return [
            jnp.concatenate(
                [tall[half, i * rows : (i + 1) * rows, :] for half in range(cols // LANES)], axis=1
            )
            for i in range(len(planes))
        ]

    def rows_of(planes):
        n = len(planes) * crows
        for i, plane in enumerate(planes):
            for half in range(cols // LANES):
                tall[half, i * rows : (i + 1) * rows, :] = plane[:, half * LANES : (half + 1) * LANES]
        return tuple(
            jnp.concatenate([tall[half, pl.ds(start, n, 2), :] for half in range(cols // LANES)], axis=1)
            for start in range(2)
        )

    s, m = sp[b], me[b]
    m2 = m * m
    gain = 1.0 / (s * m2)
    inv_m2 = 1.0 / m2
    cs0 = cs[0]
    inv_sh = 1.0 / sh[...]
    t = tr[...]
    c0 = [uc[c, 0] for c in range(comps)]
    pull = [
        cs0 * (lc[c] - 29.0 * uc[c, 0] + 16.0 * uc[c, 1] - uc[c, 2]) * TWELFTH for c in range(comps)
    ]
    wide = stretch([cs0] + pull + c0)
    alpha = gain * wide[0]
    beta, first, weighted = [], [], []
    for c in range(comps):
        ub, u1, u2 = uf[c, b], uf[c, b - 1], uf[c, b - 2]
        e = u2 - lf[c] * inv_m2 - 16.0 * u1 + 29.0 * ub
        bc = (12.0 * gain * wide[1 + c] + e) * (1.0 / 14.0)
        beta.append(bc)
        first.append(jnp.max(jnp.abs(alpha * wide[1 + comps + c] + bc - ub), axis=0, keepdims=True))
        weighted.append(t * bc)
        weighted.append(t * (u2 - 8.0 * u1 + 7.0 * ub))
        weighted.append(t * (u2 - 8.0 * u1 + ub))
    even_rows, odd_rows = rows_of([t * alpha] + weighted)
    sums = jnp.dot(pieces(even_rows + odd_rows), narrow[...], preferred_element_type=jnp.float32)
    even_rows, odd_rows = rows_of([alpha])
    top = jnp.maximum(even_rows, odd_rows)
    top = jnp.maximum(top, turn(top, -1, 1))
    lane = lax.broadcasted_iota(jnp.int32, top.shape, 1)
    top = jnp.where(lax.rem(lane, 2) == 0, top, 0.0)
    top = jnp.dot(pieces(top), narrow[...], preferred_element_type=jnp.float32)

    def part(i):
        return sums[i * crows : (i + 1) * crows, :]

    rate = part(0) * (0.5 * inv_sh)
    history = [[], [], [], []]
    c3s, c4s = [], []
    for c in range(comps):
        q6 = (8.0 * uc[c, 1] - uc[c, 0] - uc[c, 2]) * (1.0 / 6.0)
        pushed, start, still = part(1 + 3 * c), part(2 + 3 * c), part(3 + 3 * c)
        base = q6 - (still * TWELFTH + 0.5 * pushed) * inv_sh
        c1 = q6 - start * (TWELFTH * inv_sh)
        c2 = base - rate * c0[c]
        c3 = base - rate * c1
        c4 = base - rate * c2
        d1, d2, d3, d4 = (jnp.abs(x) for x in (c1 - c0[c], c2 - c1, c3 - c2, c4 - c3))
        history[0].append(d1)
        history[1].append(jnp.maximum(d2, top * d1))
        history[2].append(jnp.maximum(d3, top * d2))
        history[3].append(jnp.maximum(d4, top * d3))
        c3s.append(c3)
        c4s.append(c4)
    lane = lax.broadcasted_iota(jnp.int32, (1, LANES), 1)
    line = jnp.zeros((1, LANES), jnp.float32)
    for n in range(4):
        d = jnp.maximum(jnp.maximum(history[n][0], history[n][1]), history[n][2])
        d = jnp.max(d, axis=0, keepdims=True)
        if n == 0:
            f = jnp.maximum(jnp.maximum(first[0], first[1]), first[2])
            for half in range(cols // LANES):
                d = jnp.maximum(d, f[:, half * LANES : (half + 1) * LANES])
        line = jnp.where(lane == n, jnp.max(d, axis=1, keepdims=True), line)
    wide = stretch(c3s)
    return [alpha * wide[c] + beta[c] for c in range(comps)], c4s, line[:, 0:4]


def fix_kernel(vf_in, vc_in, uf, sp, me, uc, cs, tr, sh, widen, narrow, *refs):
    own, got = refs[0:4], refs[4:8]
    vf, vc, change = refs[8:11]
    packed = refs[11:15]
    lf, lc, tall, ycorr = refs[15:]
    comps, layers, rows, cols = uf.shape
    edges = Edges(own, got, ycorr, (uf.shape[1:], uc.shape[2:]))
    ghost_f, ghost_c, line = interface(edges, uf, sp, me, uc, cs, tr, sh, widen, narrow, lf, lc, tall)
    change[...] = line
    b = layers - 1
    s_last = sp[b] * me[b] * me[b] * TWELFTH
    s_next = sp[b - 1] * me[b - 1] * me[b - 1] * TWELFTH
    for c in range(comps):
        vf[c, b] = vf_in[c, b] + s_last * (14.0 * ghost_f[c] + uf[c, b])
        vf[c, b - 1] = vf_in[c, b - 1] - s_next * ghost_f[c]
        vc[c, 0] = vc_in[c, 0] + cs[0] * TWELFTH * (14.0 * ghost_c[c] + uc[c, 0])
        vc[c, 1] = vc_in[c, 1] - cs[1] * TWELFTH * ghost_c[c]

    @pl.loop(0, layers)
    def _(k):
        for c in range(comps):
            edges.add(vf.at[c, k], edges.fine, c * layers + k, sp.at[k])
            edges.add(vc.at[c, k], edges.coarse, c * layers + k, cs.at[k])

    pack_all(vf, vc, *packed)


def interface_kernel(uf, sp, me, uc, cs, tr, sh, widen, narrow, *refs):
    own, got = refs[0:4], refs[4:8]
    ghost_f, ghost_c, change = refs[8:11]
    lf, lc, tall, ycorr = refs[11:]
    edges = Edges(own, got, ycorr, (uf.shape[1:], uc.shape[2:]))
    g, c4, line = interface(edges, uf, sp, me, uc, cs, tr, sh, widen, narrow, lf, lc, tall)
    for c in range(uf.shape[0]):
        ghost_f[c] = g[c]
        ghost_c[c] = c4[c]
    change[...] = line


def last_kernel(first, stop, early, gate, uf, pf, sp, me, uc, cs, vf, vc, ghost_f, ghost_c, *refs):
    own, got = refs[0:4], refs[4:8]
    with_coarse = first == 0
    outs = refs[10:12] if not with_coarse else refs[8:10]
    out_f, out_c = outs
    done_f, done_c, ycorr, sem = refs[-4:]
    comps, layers, rows, cols = uf.shape
    b = layers - 1
    edges = Edges(own, got, ycorr, (uf.shape[1:], uc.shape[2:]))

    def copy(k):
        return pltpu.make_async_copy(done_f.at[:, k - first], out_f.at[:, k], sem.at[k - first])

    def copy_coarse():
        return pltpu.make_async_copy(done_c, out_c, sem.at[stop - first])

    def fine(k):
        s12, m2 = sp[k] * TWELFTH, me[k] * me[k]
        for c in range(comps):
            if stop <= early:
                done_f[c, k - first] = vf[c, k]
            else:
                u = uf[c, k]
                z = depth12(uf, c, k)
                if isinstance(k, int) and k == b:
                    z = z + 14.0 * ghost_f[c] + u
                if isinstance(k, int) and k == b - 1:
                    z = z - ghost_f[c]
                done_f[c, k - first] = 2.0 * u - pf[c, k] + s12 * (lateral12(u) + m2 * z)
            edges.add(done_f.at[c, k - first], edges.fine, c * layers + k, sp.at[k])
        copy(k).start()

    layers_do(first, stop, layers, fine)
    if with_coarse:

        @pl.loop(0, layers)
        def _(k):
            for c in range(comps):
                done_c[c, k] = vc[c, k]
                edges.add(done_c.at[c, k], edges.coarse, c * layers + k, cs.at[k])

        for c in range(comps):
            done_c[c, 0] = done_c[c, 0] + cs[0] * TWELFTH * (14.0 * ghost_c[c] + uc[c, 0])
            done_c[c, 1] = done_c[c, 1] - cs[1] * TWELFTH * ghost_c[c]
        copy_coarse().start()
    for k in range(first, stop):
        copy(k).wait()
    if with_coarse:
        copy_coarse().wait()


def call(kernel, args, outs, scratch=(), alias={}, flops=0, hbm=()):
    spaces = [pltpu.HBM if i in hbm else pltpu.VMEM for i in range(len(args))]
    return pl.pallas_call(
        kernel,
        out_shape=tuple(outs),
        in_specs=[pl.BlockSpec(memory_space=s) for s in spaces],
        out_specs=tuple(pl.BlockSpec(memory_space=o.memory_space) for o in outs),
        scratch_shapes=list(scratch),
        input_output_aliases=alias,
        cost_estimate=pl.CostEstimate(flops=flops, bytes_accessed=flops, transcendentals=0),
        compiler_params=pltpu.CompilerParams(vmem_limit_bytes=VMEM_LIMIT),
    )(*[pltpu.with_memory_space_constraint(x, s) for x, s in zip(args, spaces)])


def exchange(parts):
    x_down, x_up, y_down, y_up = parts

    def ring(value, axis, by):
        n = lax.axis_size(axis)
        return lax.ppermute(value, axis, [(i, (i + by) % n) for i in range(n)])

    return (ring(x_down, "gx", -1), ring(x_up, "gx", 1), ring(y_down, Y, -1), ring(y_up, Y, 1))


def rounds():
    found = []
    for axis in ("gx", "gy", "grid"):
        n, far = lax.axis_size(axis), 1
        while far < n:
            pairs = [(i, i ^ far) if n & (n - 1) == 0 else (i, (i + far) % n) for i in range(n)]
            found.append((axis, pairs))
            far *= 2
    return found


def on_device(
    fine_field, fine_previous, fine_speed, fine_metric, coarse_field, coarse_previous, coarse_speed,
    fine_traction, coarse_shear,
):
    f32 = jnp.float32
    comps, layers, rows, cols = fine_field.shape
    crows, ccols = coarse_field.shape[2:]
    fine = pltpu.VMEM(fine_field.shape, f32)
    coarse = pltpu.VMEM(coarse_field.shape, f32)
    plane_f = pltpu.VMEM((comps, rows, cols), f32)
    plane_c = pltpu.VMEM((comps, crows, ccols), f32)
    line = pltpu.VMEM((1, 4), f32)
    corrections = pltpu.VMEM((2, rows + crows, LANES), f32)
    edge_outs = [
        pltpu.VMEM((comps * layers, 2, cols + ccols), f32),
        pltpu.VMEM((comps * layers, 2, cols + ccols), f32),
        pltpu.VMEM((rows + crows, LANES), f32),
        pltpu.VMEM((rows + crows, LANES), f32),
    ]
    solve_scratch = [plane_f, plane_c, pltpu.VMEM((cols // LANES, 10 * rows, LANES), f32), corrections]
    picks = np.zeros((cols, ccols), np.float32)
    picks[np.arange(cols), np.arange(cols) // 2] = 1.0
    narrow = jnp.asarray(np.tile(picks, (3, 1)), jnp.bfloat16)
    widen = jnp.asarray(np.tile(picks.T, (3, 1)), jnp.bfloat16)
    sp, me, cs = fine_speed, fine_metric, coarse_speed
    fixed = (fine_traction, coarse_shear, widen, narrow)

    uf, uc, *mine = call(
        load_kernel, (fine_field, coarse_field), [fine, coarse] + edge_outs,
        scratch=[pltpu.SemaphoreType.DMA((2 * layers // 4,))], hbm=(0, 1),
    )
    pf, pc = fine_previous, coarse_previous
    theirs = exchange(mine)
    vf, vc = call(
        functools.partial(main_kernel, layers), (uf, pf, sp, me, uc, pc, cs), [fine, coarse], flops=40_000_000
    )
    vf, vc, change0, *ours = call(
        fix_kernel,
        (vf, vc, uf, sp, me, uc, cs) + fixed + (*mine, *theirs),
        [fine, coarse, line] + edge_outs, scratch=solve_scratch, alias={0: 0, 1: 1}, flops=20_000_000,
    )
    pf, pc, uf, uc, mine = uf, uc, vf, vc, ours
    theirs = exchange(mine)
    vf, vc = call(
        functools.partial(main_kernel, EARLY), (uf, pf, sp, me, uc, pc, cs), [fine, coarse], flops=20_000_000
    )
    ghost_f, ghost_c, change1 = call(
        interface_kernel,
        (uf, sp, me, uc, cs) + fixed + (*mine, *theirs),
        [plane_f, plane_c, line], scratch=solve_scratch, flops=10_000_000,
    )
    history = jnp.concatenate([change0, change1], axis=0)
    steps = rounds()
    bounds = [0, EARLY] + [EARLY + (layers - EARLY) * (i + 1) // 4 for i in range(4)]
    outs = ()
    for i in range(max(len(steps), len(bounds) - 1)):
        if i < len(steps):
            axis, pairs = steps[i]
            arrived = lax.ppermute(history, axis, pairs)
        if i < len(bounds) - 1:
            first, stop = bounds[i : i + 2]
            args = (history, uf, pf, sp, me, uc, cs, vf, vc, ghost_f, ghost_c, *mine, *theirs, *outs)
            n = len(args)
            outs = call(
                functools.partial(last_kernel, first, stop, EARLY), args,
                [pltpu.HBM(fine_field.shape, f32), pltpu.HBM(coarse_field.shape, f32)],
                scratch=[
                    pltpu.VMEM((comps, stop - first, rows, cols), f32), coarse, corrections,
                    pltpu.SemaphoreType.DMA((stop - first + 1,)),
                ],
                alias={n - 2: 0, n - 1: 1} if outs else {}, hbm=(n - 2, n - 1) if outs else (), flops=10_000_000,
            )
        if i < len(steps):
            history = jnp.maximum(history, arrived)
    return outs[0], outs[1], history


def solution(mesh):
    field = P(None, None, "gx", Y)
    layered = P(None, "gx", Y)
    plane = P("gx", Y)
    return jax.shard_map(
        on_device,
        mesh=mesh,
        in_specs=(field, field, layered, layered, field, field, layered, plane, plane),
        out_specs=(field, field, P()),
        check_vma=False,
    )
```

time: 70.1 us -> 58.6 us (0.84)
  local copies, waits for them, and re-layouts: 8.24 us -> 1.92 us
  waiting for transfers between devices: 15.2 us -> 9.78 us
  starting transfers between devices: 15.8 us -> 14.7 us
  Pallas kernels: 29.7 us -> 30.5 us
    ppermute x5, waiting for transfers between devices: 15.2 us -> 6.08 us  [on_device(): arrived = lax.ppermute(history, axis, pairs)]
    unnamed x26 -> x18, local copies, waits for them, and re-layouts: 7.48 us -> 1.92 us
    ppermute x8, waiting for transfers between devices: 0.02 us -> 3.71 us  [ring(): return lax.ppermute(value, axis, [(i, (i + by) % n) for i in range(n)])]
    ppermute x5, starting transfers between devices: 2.91 us -> 1.74 us  [on_device(): arrived = lax.ppermute(history, axis, pairs)]
    pallas_call x5 -> x10, Pallas kernels: 29.7 us -> 30.5 us  [call(): pl.pallas_call(kernel, out_shape=tuple(outs), in_specs=[pl.BlockSpec(memo...]
  transfers between devices with their start and end apart: 13 -> 13, of which waited for: 4 -> 5; matrix products, arithmetic and copies ran while one was open for 4% -> 0% of each run, Pallas kernels for 21% -> 35%
where the time goes in v2:
time: 58.6 us; the launch traced here: 58.4 us
  Pallas kernels  30.5 us (52%)
  starting transfers between devices  14.7 us (25%)
  waiting for transfers between devices  9.78 us (17%)
  local copies, waits for them, and re-layouts  1.92 us (3%)
  between operations  0.89 us (2%)
  other arithmetic  0.6 us (1%)
    pallas_call x10, Pallas kernels, call(): pl.pallas_call(kernel, out_shape=tuple(outs), in_specs=[pl.BlockSpec(memo...  30.5 us
    ppermute x8, starting transfers between devices, ring(): return lax.ppermute(value, axis, [(i, (i + by) % n) for i in range(n)])  12.9 us
    ppermute x5, waiting for transfers between devices, on_device(): arrived = lax.ppermute(history, axis, pairs)  6.08 us
    ppermute x8, waiting for transfers between devices, ring(): return lax.ppermute(value, axis, [(i, (i + by) % n) for i in range(n)])  3.71 us
    unnamed x18, local copies, waits for them, and re-layouts  1.92 us
    ppermute x5, starting transfers between devices, on_device(): arrived = lax.ppermute(history, axis, pairs)  1.74 us
  transfers between devices with their start and end apart: 13, of which 5 were waited for; matrix products, arithmetic and copies ran while one was open for 0% of the time, Pallas kernels for 35%

profile of v2, /device:TPU:0, one launch (start us, length us, event | category | flops | bytes accessed | tf_op | source)
XLA Modules:
  0.0 58.4 jit_solution(14263649988887740833)
XLA Ops:
  0.7 3.3 %shard_map.130 = (f32[3,16,64,256]{3,2,1,0:T(8,128)S(1)}, f32[3,16,32,128]{3,2,1,0:T(8,128)S(1)}, f32[48,2,384]{2,1,0:T(2,128)S(1)}, f32[48,2,384]{2,1,0:T(2,128...) custom-call(f32[3,16,64,256]{3,2,1,0:T(8,128)} %uf_hbm.1, f32[3,16,32,128]{3,2,1,0:T(8,128)} %uc_hbm.1), custom_call_target="tpu_custom_call" | custom-call | tf_op jit(solution)/shard_map/pallas_call | solution.py:375
  4.0 2.5 %collective-permute-start = (f32[48,2,384]{2,1,0:T(2,128)S(1)}, f32[48,2,384]{2,1,0:T(2,128)S(1)}, u32[]{:S(2)}, u32[]{:S(2)}) collective-permute-start(f32[48,2,384]{2,1,0:T(2,128)S(1)} %get-tuple-element.37.refs_0_), channel_id=1, source_target_pairs={{0,12},{4,0},{8,4},{12,8},{1,13},{5,1},{9,5},{13,9},{2,14},{6,2},{... | collective-permute-start | bytes 442376 | tf_op jit(solution)/shard_map/ppermute | solution.py:392
  6.4 4.5 %collective-permute-start.2 = (f32[96,128]{1,0:T(8,128)S(1)}, f32[96,128]{1,0:T(8,128)S(1)}, u32[]{:S(2)}, u32[]{:S(2)}) collective-permute-start(f32[96,128]{1,0:T(8,128)S(1)} %get-tuple-element.39.refs_2_), channel_id=1, source_target_pairs={{0,19},{1,0},{2,1},{3,2},{16,3},{17,16},{18,17},{19,18},{4,23},{5,... | collective-permute-start | bytes 147464 | tf_op jit(solution)/shard_map/ppermute | solution.py:392
  11.0 0.0 copy-start.3
  11.0 1.9 %copy-done.3 = f32[3,16,64,256]{3,2,1,0:T(8,128)S(1)} copy-done((f32[3,16,64,256]{3,2,1,0:T(8,128)S(1)}, f32[3,16,64,256]{3,2,1,0:T(8,128)}, u32[]{:S(2)}) %copy-start.3) | copy-done | bytes 3145752
  12.9 6.9 %shard_map.131 = (f32[3,16,64,256]{3,2,1,0:T(8,128)S(1)}, f32[3,16,32,128]{3,2,1,0:T(8,128)S(1)}) custom-call(f32[3,16,64,256]{3,2,1,0:T(8,128)S(1)} %get-tuple-element.33.uf.pf, f32[3,16,64,256]{3,2,1,0:T(8,128)S(1)} %copy-done.3, f32[16,64,256]{2,1,0:T(8,128)S(1)} %copy-done, f32[16,64,256]{2,1,0:T(8,128)S(1)} %copy-done.1, ...), custom_call_target="tpu_custom_call" | custom-call | flops 40000000 | bytes 40000000 | tf_op jit(solution)/shard_map/pallas_call | solution.py:375
  19.9 0.0 collective-permute-done.2.refs_6_
  19.9 0.0 collective-permute-done.refs_4_
  19.9 0.0 collective-permute-done.1.refs_5_
  19.9 5.4 %shard_map.132 = (f32[3,16,64,256]{3,2,1,0:T(8,128)S(1)}, f32[3,16,32,128]{3,2,1,0:T(8,128)S(1)}, f32[1,4]{1,0:T(1,128)S(1)}, f32[48,2,384]{2,1,0:T(2,128)S(1)},...) custom-call(f32[3,16,64,256]{3,2,1,0:T(8,128)S(1)} %get-tuple-elemen, ...), custom_call_target="tpu_custom_call", output_to_operand_aliasing={{0}: (0, {}), {1}: (1, {})} | custom-call | flops 20000000 | bytes 20000000 | tf_op jit(solution)/shard_map/pallas_call | solution.py:375
  25.4 1.5 %collective-permute-start.4 = (f32[48,2,384]{2,1,0:T(2,128)S(1)}, f32[48,2,384]{2,1,0:T(2,128)S(1)}, u32[]{:S(2)}, u32[]{:S(2)}) collective-permute-start(f32[48,2,384]{2,1,0:T(2,128)S(1)} %get-tuple-element.44.refs_0_), channel_id=1, source_target_pairs={{0,12},{4,0},{8,4},{12,8},{1,13},{5,1},{9,5},{13,9},{2,14},{6,2},{... | collective-permute-start | bytes 442376 | tf_op jit(solution)/shard_map/ppermute | solution.py:392
  26.9 4.4 %collective-permute-start.6 = (f32[96,128]{1,0:T(8,128)S(1)}, f32[96,128]{1,0:T(8,128)S(1)}, u32[]{:S(2)}, u32[]{:S(2)}) collective-permute-start(f32[96,128]{1,0:T(8,128)S(1)} %get-tuple-element.46.refs_2_), channel_id=1, source_target_pairs={{0,19},{1,0},{2,1},{3,2},{16,3},{17,16},{18,17},{19,18},{4,23},{5,... | collective-permute-start | bytes 147464 | tf_op jit(solution)/shard_map/ppermute | solution.py:392
  31.3 0.0 collective-permute-start.7
  31.3 3.1 %shard_map.134 = (f32[3,16,64,256]{3,2,1,0:T(8,128)S(1)}, f32[3,16,32,128]{3,2,1,0:T(8,128)S(1)}) custom-call(f32[3,16,64,256]{3,2,1,0:T(8,128)S(1)} %get-tuple-element.42.uf, f32[3,16,64,256]{3,2,1,0:T(8,128)S(1)} %get-tuple-element.33.uf.pf, f32[16,64,256]{2,1,0:T(8,128)S(1)} %copy-done, f32[16,64,256]{2,1,0:T(8,128)S(1)} %copy-done.1, ...), custom_call_target="tpu_custom_call" | custom-call | flops 20000000 | bytes 20000000 | tf_op jit(solution)/shard_map/pallas_call | solution.py:375
  34.4 0.0 collective-permute-done.6.refs_6_
  34.4 3.7 %collective-permute-done.7.refs_7_ = f32[96,128]{1,0:T(8,128)S(1)} collective-permute-done((f32[96,128]{1,0:T(8,128)S(1)}, f32[96,128]{1,0:T(8,128)S(1)}, u32[]{:S(2)}, u32[]{:S(2)}) %collective-permute-start.7) | collective-permute-done | bytes 49184 | tf_op jit(solution)/shard_map/ppermute | solution.py:392
  38.1 1.2 %shard_map.133 = (f32[3,64,256]{2,1,0:T(8,128)S(1)}, f32[3,32,128]{2,1,0:T(8,128)S(1)}, f32[1,4]{1,0:T(1,128)S(1)}) custom-call(f32[3,16,64,256]{3,2,1,0:T(8,128)S(1)} %get-tuple-element.42.uf, f32[16,64,256]{2,1,0:T(8,128)S(1)} %copy-done, f32[16,64,256]{2,1,0:T(8,128)S(1)} %copy-done.1, f32[3,16,32,128]{3,2,1,0:T(8,128)S(1)} %get-tuple-element.43.uc, ...), custom_call_target="tpu_custom_call" | custom-call | flops 10000000 | bytes 10000000 | tf_op jit(solution)/shard_map/pallas_call | solution.py:375
  39.3 0.1 collective-permute-start.8
  39.4 3.1 %shard_map.135 = (f32[3,16,64,256]{3,2,1,0:T(8,128)}, f32[3,16,32,128]{3,2,1,0:T(8,128)}) custom-call(f32[2,4]{1,0:T(2,128)S(1)} %pad_maximum_fusion.gate, f32[3,16,64,256]{3,2,1,0:T(8,128)S(1)} %get-tuple-element.42.uf, f32[3,16,64,256]{3,2,1,0:T(8,128)S(1)} %get-tuple-element.33.uf.pf, f32[16,64,256]{2,1,0:T(8,128)S(1)} %copy-done, ...), custom_call_target="tpu_custom_call" | custom-call | flops 10000000 | bytes 10000000 | tf_op jit(solution)/shard_map/pallas_call | solution.py:375
  42.5 0.0 collective-permute-done.8
  42.5 1.1 %collective-permute-start.9 = (f32[2,4]{1,0:T(2,128)S(1)}, f32[2,4]{1,0:T(2,128)S(1)}, u32[]{:S(2)}, u32[]{:S(2)}) collective-permute-start(f32[2,4]{1,0:T(2,128)S(1)} %fusion.gate), channel_id=1, source_target_pairs={{0,8},{4,12},{8,0},{12,4},{1,9},{5,13},{9,1},{13,5},{2,10},{6,14},... | collective-permute-start | bytes 104 | tf_op jit(solution)/shard_map/ppermute | solution.py:466
  43.6 1.9 %shard_map.136 = (f32[3,16,64,256]{3,2,1,0:T(8,128)}, f32[3,16,32,128]{3,2,1,0:T(8,128)}) custom-call(f32[2,4]{1,0:T(2,128)S(1)} %fusion.gate, f32[3,16,64,256]{3,2,1,0:T(8,128)S(1)} %get-tuple-element.42.uf, f32[3,16,64,256]{3,2,1,0:T(8,128)S(1)} %get-tuple-element.33.uf.pf, ...), custom_call_target="tpu_custom_call", output_to_operand_aliasing={{0}: (19, {}), {1}: (20, {})} | custom-call | flops 10000000 | bytes 10000000 | tf_op jit(solution)/shard_map/pallas_call | solution.py:375
  45.5 0.7 %collective-permute-done.9 = f32[2,4]{1,0:T(2,128)S(1)} collective-permute-done((f32[2,4]{1,0:T(2,128)S(1)}, f32[2,4]{1,0:T(2,128)S(1)}, u32[]{:S(2)}, u32[]{:S(2)}) %collective-permute-start.9) | collective-permute-done | bytes 64 | tf_op jit(solution)/shard_map/ppermute | solution.py:466
  46.2 0.1 collective-permute-start.10
  46.2 1.9 %shard_map.137 = (f32[3,16,64,256]{3,2,1,0:T(8,128)}, f32[3,16,32,128]{3,2,1,0:T(8,128)}) custom-call(f32[2,4]{1,0:T(2,128)S(1)} %fusion.1.gate, f32[3,16,64,256]{3,2,1,0:T(8,128)S(1)} %get-tuple-element.42.uf, f32[3,16,64,256]{3,2,1,0:T(8,128)S(1)} %get-tuple-element.33.uf.pf, ...), custom_call_target="tpu_custom_call", output_to_operand_aliasing={{0}: (19, {}), {1}: (20, {})} | custom-call | flops 10000000 | bytes 10000000 | tf_op jit(solution)/shard_map/pallas_call | solution.py:375
  48.2 1.6 %collective-permute-done.10 = f32[2,4]{1,0:T(2,128)S(1)} collective-permute-done((f32[2,4]{1,0:T(2,128)S(1)}, f32[2,4]{1,0:T(2,128)S(1)}, u32[]{:S(2)}, u32[]{:S(2)}) %collective-permute-start.10) | collective-permute-done | bytes 64 | tf_op jit(solution)/shard_map/ppermute | solution.py:466
  49.8 1.9 %shard_map.138 = (f32[3,16,64,256]{3,2,1,0:T(8,128)}, f32[3,16,32,128]{3,2,1,0:T(8,128)}) custom-call(f32[2,4]{1,0:T(2,128)S(1)} %max.17.gate, f32[3,16,64,256]{3,2,1,0:T(8,128)S(1)} %get-tuple-element.42.uf, f32[3,16,64,256]{3,2,1,0:T(8,128)S(1)} %get-tuple-element.33.uf.pf, ...), custom_call_target="tpu_custom_call", output_to_operand_aliasing={{0}: (19, {}), {1}: (20, {})} | custom-call | flops 10000000 | bytes 10000000 | tf_op jit(solution)/shard_map/pallas_call | solution.py:375
  51.7 2.5 %collective-permute-done.11 = f32[2,4]{1,0:T(2,128)S(1)} collective-permute-done((f32[2,4]{1,0:T(2,128)S(1)}, f32[2,4]{1,0:T(2,128)S(1)}, u32[]{:S(2)}, u32[]{:S(2)}) %collective-permute-start.11) | collective-permute-done | bytes 64 | tf_op jit(solution)/shard_map/ppermute | solution.py:466
  54.3 0.5 collective-permute-start.12
  54.8 1.8 %shard_map.139 = (f32[3,16,64,256]{3,2,1,0:T(8,128)}, f32[3,16,32,128]{3,2,1,0:T(8,128)}) custom-call(f32[2,4]{1,0:T(2,128)S(1)} %max.18.gate, f32[3,16,64,256]{3,2,1,0:T(8,128)S(1)} %get-tuple-element.42.uf, f32[3,16,64,256]{3,2,1,0:T(8,128)S(1)} %get-tuple-element.33.uf.pf, ...), custom_call_target="tpu_custom_call", output_to_operand_aliasing={{0}: (19, {}), {1}: (20, {})} | custom-call | flops 10000000 | bytes 10000000 | tf_op jit(solution)/shard_map/pallas_call | solution.py:375
  56.6 1.2 %collective-permute-done.12 = f32[2,4]{1,0:T(2,128)S(1)} collective-permute-done((f32[2,4]{1,0:T(2,128)S(1)}, f32[2,4]{1,0:T(2,128)S(1)}, u32[]{:S(2)}, u32[]{:S(2)}) %collective-permute-start.12) | collective-permute-done | bytes 64 | tf_op jit(solution)/shard_map/ppermute | solution.py:466
  57.8 0.6 max.19
  (28 shorter events, 0.1 us)
Async XLA Ops:
  0.6 10.3 %copy-start = (f32[16,64,256]{2,1,0:T(8,128)S(1)}, f32[16,64,256]{2,1,0:T(8,128)}, u32[]{:S(2)}) copy-start(f32[16,64,256]{2,1,0:T(8,128)} %sp.17) | copy-start | bytes 3145732
  0.6 10.3 %copy-start.1 = (f32[16,64,256]{2,1,0:T(8,128)S(1)}, f32[16,64,256]{2,1,0:T(8,128)}, u32[]{:S(2)}) copy-start(f32[16,64,256]{2,1,0:T(8,128)} %me.17) | copy-start | bytes 3145732
  0.7 10.3 %copy-start.4 = (f32[3,16,32,128]{3,2,1,0:T(8,128)S(1)}, f32[3,16,32,128]{3,2,1,0:T(8,128)}, u32[]{:S(2)}) copy-start(f32[3,16,32,128]{3,2,1,0:T(8,128)} %pc.1) | copy-start | bytes 2359300
  0.7 10.3 %copy-start.2 = (f32[16,32,128]{2,1,0:T(8,128)S(1)}, f32[16,32,128]{2,1,0:T(8,128)}, u32[]{:S(2)}) copy-start(f32[16,32,128]{2,1,0:T(8,128)} %cs.17) | copy-start | bytes 786436
  4.0 15.9 %collective-permute-start = (f32[48,2,384]{2,1,0:T(2,128)S(1)}, f32[48,2,384]{2,1,0:T(2,128)S(1)}, u32[]{:S(2)}, u32[]{:S(2)}) collective-permute-start(f32[48,2,384]{2,1,0:T(2,128)S(1)} %get-tuple-element.37.refs_0_), channel_id=1, source_target_pairs={{0,12},{4,0},{8,4},{12,8},{1,13},{5,1},{9,5},{13,9},{2,14},{6,2},{... | collective-permute-start | bytes 442376 | tf_op jit(solution)/shard_map/ppermute | solution.py:392
  6.4 13.5 %collective-permute-start.1 = (f32[48,2,384]{2,1,0:T(2,128)S(1)}, f32[48,2,384]{2,1,0:T(2,128)S(1)}, u32[]{:S(2)}, u32[]{:S(2)}) collective-permute-start(f32[48,2,384]{2,1,0:T(2,128)S(1)} %get-tuple-element.38.refs_1_), channel_id=1, source_target_pairs={{0,4},{4,8},{8,12},{12,0},{1,5},{5,9},{9,13},{13,1},{2,6},{6,10},{... | collective-permute-start | bytes 442376 | tf_op jit(solution)/shard_map/ppermute | solution.py:392
  6.4 13.4 %collective-permute-start.2 = (f32[96,128]{1,0:T(8,128)S(1)}, f32[96,128]{1,0:T(8,128)S(1)}, u32[]{:S(2)}, u32[]{:S(2)}) collective-permute-start(f32[96,128]{1,0:T(8,128)S(1)} %get-tuple-element.39.refs_2_), channel_id=1, source_target_pairs={{0,19},{1,0},{2,1},{3,2},{16,3},{17,16},{18,17},{19,18},{4,23},{5,... | collective-permute-start | bytes 147464 | tf_op jit(solution)/shard_map/ppermute | solution.py:392
  11.0 8.9 %collective-permute-start.3 = (f32[96,128]{1,0:T(8,128)S(1)}, f32[96,128]{1,0:T(8,128)S(1)}, u32[]{:S(2)}, u32[]{:S(2)}) collective-permute-start(f32[96,128]{1,0:T(8,128)S(1)} %get-tuple-element.40.refs_3_), channel_id=1, source_target_pairs={{0,1},{1,2},{2,3},{3,16},{16,17},{17,18},{18,19},{19,0},{4,5},{5,6... | collective-permute-start | bytes 147464 | tf_op jit(solution)/shard_map/ppermute | solution.py:392
  11.0 1.9 %copy-start.3 = (f32[3,16,64,256]{3,2,1,0:T(8,128)S(1)}, f32[3,16,64,256]{3,2,1,0:T(8,128)}, u32[]{:S(2)}) copy-start(f32[3,16,64,256]{3,2,1,0:T(8,128)} %pf.1) | copy-start | bytes 9437188
  12.9 7.0 %copy-start.5 = (bf16[768,128]{1,0:T(8,128)(2,1)S(1)}, bf16[768,128]{1,0:T(8,128)(2,1)}, u32[]{:S(2)}) copy-start(bf16[768,128]{1,0:T(8,128)(2,1)} %constant.4.clone.narrow) | copy-start | bytes 589828
  12.9 7.0 %copy-start.6 = (bf16[384,256]{1,0:T(8,128)(2,1)S(1)}, bf16[384,256]{1,0:T(8,128)(2,1)}, u32[]{:S(2)}) copy-start(bf16[384,256]{1,0:T(8,128)(2,1)} %constant.5.clone.widen) | copy-start | bytes 589828
  12.9 7.0 %copy-start.7 = (f32[64,256]{1,0:T(8,128)S(1)}, f32[64,256]{1,0:T(8,128)}, u32[]{:S(2)}) copy-start(f32[64,256]{1,0:T(8,128)} %tr.3) | copy-start | bytes 196612
  12.9 7.0 %copy-start.8 = (f32[32,128]{1,0:T(8,128)S(1)}, f32[32,128]{1,0:T(8,128)}, u32[]{:S(2)}) copy-start(f32[32,128]{1,0:T(8,128)} %sh.3) | copy-start | bytes 49156
  25.4 12.8 %collective-permute-start.4 = (f32[48,2,384]{2,1,0:T(2,128)S(1)}, f32[48,2,384]{2,1,0:T(2,128)S(1)}, u32[]{:S(2)}, u32[]{:S(2)}) collective-permute-start(f32[48,2,384]{2,1,0:T(2,128)S(1)} %get-tuple-element.44.refs_0_), channel_id=1, source_target_pairs={{0,12},{4,0},{8,4},{12,8},{1,13},{5,1},{9,5},{13,9},{2,14},{6,2},{... | collective-permute-start | bytes 442376 | tf_op jit(solution)/shard_map/ppermute | solution.py:392
  26.9 11.2 %collective-permute-start.5 = (f32[48,2,384]{2,1,0:T(2,128)S(1)}, f32[48,2,384]{2,1,0:T(2,128)S(1)}, u32[]{:S(2)}, u32[]{:S(2)}) collective-permute-start(f32[48,2,384]{2,1,0:T(2,128)S(1)} %get-tuple-element.45.refs_1_), channel_id=1, source_target_pairs={{0,4},{4,8},{8,12},{12,0},{1,5},{5,9},{9,13},{13,1},{2,6},{6,10},{... | collective-permute-start | bytes 442376 | tf_op jit(solution)/shard_map/ppermute | solution.py:392
  26.9 7.5 %collective-permute-start.6 = (f32[96,128]{1,0:T(8,128)S(1)}, f32[96,128]{1,0:T(8,128)S(1)}, u32[]{:S(2)}, u32[]{:S(2)}) collective-permute-start(f32[96,128]{1,0:T(8,128)S(1)} %get-tuple-element.46.refs_2_), channel_id=1, source_target_pairs={{0,19},{1,0},{2,1},{3,2},{16,3},{17,16},{18,17},{19,18},{4,23},{5,... | collective-permute-start | bytes 147464 | tf_op jit(solution)/shard_map/ppermute | solution.py:392
  31.3 6.8 %collective-permute-start.7 = (f32[96,128]{1,0:T(8,128)S(1)}, f32[96,128]{1,0:T(8,128)S(1)}, u32[]{:S(2)}, u32[]{:S(2)}) collective-permute-start(f32[96,128]{1,0:T(8,128)S(1)} %get-tuple-element.47.refs_3_), channel_id=1, source_target_pairs={{0,1},{1,2},{2,3},{3,16},{16,17},{17,18},{18,19},{19,0},{4,5},{5,6... | collective-permute-start | bytes 147464 | tf_op jit(solution)/shard_map/ppermute | solution.py:392
  39.3 3.2 %collective-permute-start.8 = (f32[2,4]{1,0:T(2,128)S(1)}, f32[2,4]{1,0:T(2,128)S(1)}, u32[]{:S(2)}, u32[]{:S(2)}) collective-permute-start(f32[2,4]{1,0:T(2,128)S(1)} %pad_maximum_fusion.gate), channel_id=1, source_target_pairs={{0,4},{4,0},{8,12},{12,8},{1,5},{5,1},{9,13},{13,9},{2,6},{6,2},{1... | collective-permute-start | bytes 104 | tf_op jit(solution)/shard_map/ppermute | solution.py:466
  42.5 3.6 %collective-permute-start.9 = (f32[2,4]{1,0:T(2,128)S(1)}, f32[2,4]{1,0:T(2,128)S(1)}, u32[]{:S(2)}, u32[]{:S(2)}) collective-permute-start(f32[2,4]{1,0:T(2,128)S(1)} %fusion.gate), channel_id=1, source_target_pairs={{0,8},{4,12},{8,0},{12,4},{1,9},{5,13},{9,1},{13,5},{2,10},{6,14},... | collective-permute-start | bytes 104 | tf_op jit(solution)/shard_map/ppermute | solution.py:466
  46.2 3.6 %collective-permute-start.10 = (f32[2,4]{1,0:T(2,128)S(1)}, f32[2,4]{1,0:T(2,128)S(1)}, u32[]{:S(2)}, u32[]{:S(2)}) collective-permute-start(f32[2,4]{1,0:T(2,128)S(1)} %fusion.1.gate), channel_id=1, source_target_pairs={{0,1},{1,0},{2,3},{3,2},{4,5},{5,4},{6,7},{7,6},{8,9},{9,8},{10,11... | collective-permute-start | bytes 104 | tf_op jit(solution)/shard_map/ppermute | solution.py:466
  49.8 4.5 %collective-permute-start.11 = (f32[2,4]{1,0:T(2,128)S(1)}, f32[2,4]{1,0:T(2,128)S(1)}, u32[]{:S(2)}, u32[]{:S(2)}) collective-permute-start(f32[2,4]{1,0:T(2,128)S(1)} %max.17.gate), channel_id=1, source_target_pairs={{0,2},{1,3},{2,0},{3,1},{4,6},{5,7},{6,4},{7,5},{8,10},{9,11},{10,... | collective-permute-start | bytes 104 | tf_op jit(solution)/shard_map/ppermute | solution.py:466
  54.3 3.6 %collective-permute-start.12 = (f32[2,4]{1,0:T(2,128)S(1)}, f32[2,4]{1,0:T(2,128)S(1)}, u32[]{:S(2)}, u32[]{:S(2)}) collective-permute-start(f32[2,4]{1,0:T(2,128)S(1)} %max.18.gate), channel_id=1, source_target_pairs={{0,16},{16,0},{1,17},{17,1},{2,18},{18,2},{3,19},{19,3},{4,20},{20... | collective-permute-start | bytes 104 | tf_op jit(solution)/shard_map/ppermute | solution.py:466

commit v3 on v2

v3 whole, which is shorter than its diff:
```python
import functools

import jax
import jax.numpy as jnp
import numpy as np
from jax import lax
from jax.experimental import pallas as pl
from jax.experimental.pallas import tpu as pltpu
from jax.sharding import PartitionSpec as P

STEPS = 2
LANES = 128
TWELFTH = 1.0 / 12.0
Y = ("grid", "gy")
VMEM_LIMIT = 16 << 20


def turn(x, by, axis):
    return pltpu.roll(x, by % x.shape[axis], axis)


def bands(length, copies):
    one = sum(w * np.eye(length, k=o) for o, w in ((1, 16.0), (-1, 16.0), (2, -1.0), (-2, -1.0)))
    return np.kron(np.eye(copies), one)


def lateral_tables(rows, cols):
    stack = 256 // rows
    left, right = bands(rows, stack), bands(cols, 1)
    return (
        jnp.asarray(np.concatenate([left, left], axis=1), jnp.bfloat16),
        jnp.asarray(np.concatenate([right, right], axis=0), jnp.bfloat16),
    )


def lateral12(planes, left, right):
    a = planes.astype(jnp.bfloat16)
    b = (planes - a.astype(jnp.float32)).astype(jnp.bfloat16)
    y = jnp.dot(jnp.concatenate([a, b], axis=1), right[...], preferred_element_type=jnp.float32)
    x = jnp.dot(left[...], jnp.concatenate([a, b], axis=0), preferred_element_type=jnp.float32)
    return (x + y) - 60.0 * planes


def depth12(ref, c, k):
    last = ref.shape[1] - 1

    def pair(offset):
        taps = [ref[c, k + o] for o in (-offset, offset) if not isinstance(k, int) or 0 <= k + o <= last]
        return taps[0] + taps[1] if len(taps) == 2 else taps[0]

    return 16.0 * pair(1) - pair(2) - 30.0 * ref[c, k]


def slot(p):
    return (p // 32) * LANES + (p % 32) * 4


def column_tables(planes):
    pack, unpack = np.zeros((2 * LANES, 2 * LANES)), np.zeros((2 * LANES, 2 * LANES))
    for p in range(planes):
        v0, v1, u0, u1 = (slot(p) + i for i in range(4))
        down, up = 2 * p, LANES + 2 * p
        pack[u0, down] = -1.0
        pack[u0, down + 1], pack[u1, down + 1] = 16.0, -1.0
        pack[v0, up], pack[v1, up] = -1.0, 16.0
        pack[v1, up + 1] = -1.0
        unpack[2 * p, slot(p) + 2] = unpack[2 * p + 1, slot(p) + 3] = 1.0
        unpack[LANES + 2 * p, slot(p)] = unpack[LANES + 2 * p + 1, slot(p) + 1] = 1.0
    return tuple(jnp.asarray(np.tile(t, (3, 1)), jnp.bfloat16) for t in (pack, unpack))


def pieces(x):
    a = x.astype(jnp.bfloat16)
    rest = x - a.astype(jnp.float32)
    b = rest.astype(jnp.bfloat16)
    c = (rest - b.astype(jnp.float32)).astype(jnp.bfloat16)
    return jnp.concatenate([a, b, c], axis=-1)


def times(x, table):
    return jnp.dot(pieces(x), table[...], preferred_element_type=jnp.float32)


def pack_all(uf, uc, pack, x_down, x_up, y_down, y_up, ready=None, ready_table=None):
    comps, layers, rows, cols = uf.shape
    crows, ccols = uc.shape[2:]
    raw = []
    for ref, at in ((uf, slice(0, cols)), (uc, slice(cols, cols + ccols))):
        n, width = ref.shape[2:]
        lane = lax.broadcasted_iota(jnp.int32, (n, LANES), 1)
        sub = lax.broadcasted_iota(jnp.int32, (8, width), 0)
        columns = [jnp.zeros((n, LANES), jnp.float32) for _ in range(2)]
        for g in range(0, layers, 4):
            if ready is not None:
                ready(ref is uc, g)
            for c in range(comps):
                first = last = jnp.zeros((8, width), jnp.float32)
                for i in range(4):
                    p = c * layers + g + i
                    u = ref[c, g + i, :, 0:LANES]
                    if width > LANES:
                        u = jnp.where(lane < 2, u, ref[c, g + i, :, width - LANES : width])
                    u = turn(u, slot(p) % LANES + 2, 1)
                    half = slot(p) // LANES
                    columns[half] = jnp.where(lane // 4 == slot(p) % LANES // 4, u, columns[half])
                    first = jnp.where(sub // 2 == i, turn(ref[c, g + i, 0:8, :], 2 * i, 0), first)
                    last = jnp.where(sub // 2 == i, turn(ref[c, g + i, n - 8 : n, :], 2 * i + 2, 0), last)
                tile = (c * layers + g) // 4
                x_down[tile, :, at] = jnp.where(lax.rem(sub, 2) == 1, 16.0 * turn(first, 1, 0), 0.0) - first
                x_up[tile, :, at] = jnp.where(lax.rem(sub, 2) == 0, 16.0 * turn(last, -1, 0), 0.0) - last
        raw.append(jnp.concatenate(columns, axis=1))
    if ready_table is not None:
        ready_table()
    packed = times(jnp.concatenate(raw, axis=0), pack)
    y_down[...] = packed[:, 0:LANES]
    y_up[...] = packed[:, LANES : 2 * LANES]


def load_kernel(uf_hbm, uc_hbm, pack_hbm, uf, uc, x_down, x_up, y_down, y_up, pack, sem):
    layers = uf.shape[1]
    copies = {}
    for coarse, src, dst in ((False, uf_hbm, uf), (True, uc_hbm, uc)):
        for g in range(0, layers, 4):
            at = pl.ds(g, 4)
            copies[coarse, g] = pltpu.make_async_copy(src.at[:, at], dst.at[:, at], sem.at[int(coarse), g // 4])
            copies[coarse, g].start()
    table = pltpu.make_async_copy(pack_hbm, pack, sem.at[2, 0])
    table.start()

    def ready(coarse, g):
        copies[coarse, g].wait()

    pack_all(uf, uc, pack, x_down, x_up, y_down, y_up, ready, table.wait)


def groups_do(total, size, body):
    body(0)
    if total > 2 * size:

        @pl.loop(1, total // size - 1)
        def _(g):
            body(g * size)

    body(total - size)


def main_kernel(fetch, uf, pf_in, sp, me, uc, pc, cs, left_f, right_f, left_c, right_c, vf, vc, lat, *rest):
    comps, layers, rows, cols = uf.shape
    crows, ccols = uc.shape[2:]
    size_f, size_c = 256 // rows, 256 // crows
    pf = pf_in
    if fetch:
        pf, sem = rest

        def copy(k):
            at = pl.ds(k, size_f)
            return pltpu.make_async_copy(pf_in.at[:, at], pf.at[:, at], sem.at[k // size_f])

        for k in range(0, layers, size_f):
            copy(k).start()

    def coarse(first):
        for c in range(comps):
            planes = uc[c, pl.ds(first, size_c)].reshape(256, ccols)
            part = lateral12(planes, left_c, right_c)
            for i in range(size_c):
                k = first + i
                total = part[i * crows : (i + 1) * crows, :] + depth12(uc, c, k)
                vc[c, k] = 2.0 * uc[c, k] - pc[c, k] + cs[k] * TWELFTH * total

    def fine(first):
        for c in range(comps):
            planes = uf[c, pl.ds(first, size_f)].reshape(256, cols)
            lat[c] = lateral12(planes, left_f, right_f)
        if fetch:
            copy(first).wait()
        for i in range(size_f):
            k = first + i
            s12, m2 = sp[k] * TWELFTH, me[k] * me[k]
            for c in range(comps):
                total = lat[c, i * rows : (i + 1) * rows, :] + m2 * depth12(uf, c, k)
                vf[c, k] = 2.0 * uf[c, k] - pf[c, k] + s12 * total

    groups_do(layers, size_c, coarse)
    groups_do(layers, size_f, fine)


class Edges:
    def __init__(self, got, unpack, slots, shapes):
        self.got_xd, self.got_xu, got_yd, got_yu = got
        self.slots = slots
        (self.layers, rows, cols), (crows, ccols) = shapes
        self.fine = (slice(0, rows), slice(0, cols), rows, cols)
        self.coarse = (slice(rows, rows + crows), slice(cols, cols + ccols), crows, ccols)
        x_at, x_n = lax.axis_index("gx"), lax.axis_size("gx")
        y_at, y_n = lax.axis_index(Y), lax.axis_size(Y)
        self.x_low, self.x_high = x_at > 0, x_at < x_n - 1
        up = jnp.where(y_at > 0, got_yu[...], 0.0)
        down = jnp.where(y_at < y_n - 1, got_yd[...], 0.0)
        both = times(jnp.concatenate([up, down], axis=1), unpack)
        slots[0] = both[:, 0:LANES]
        slots[1] = both[:, LANES : 2 * LANES]

    def plane(self, grid, c, g, i):
        ys, xs, n, width = grid
        p = c * self.layers + g + i
        lane = lax.broadcasted_iota(jnp.int32, (n, LANES), 1)
        sub = lax.broadcasted_iota(jnp.int32, (8, width), 0)
        half, quad = (p // 32, p % 32) if isinstance(p, int) else (lax.div(p, 32), lax.rem(p, 32))
        u = pltpu.roll(self.slots[half, ys, :], LANES - 2 - 4 * quad, 1)
        low, high = jnp.where(lane < 2, u, 0.0), jnp.where(lane >= LANES - 2, u, 0.0)
        if width == LANES:
            columns = low + high
        else:
            columns = jnp.concatenate([low, high], axis=1)
        tile = p // 4 if isinstance(p, int) else lax.div(c * self.layers + g, 4)
        first = jnp.where(jnp.logical_and(sub < 2, self.x_low), turn(self.got_xu[tile, :, xs], -2 * i, 0), 0.0)
        last = jnp.where(jnp.logical_and(sub >= 6, self.x_high), turn(self.got_xd[tile, :, xs], 6 - 2 * i, 0), 0.0)
        return jnp.concatenate([columns[0:8] + first, columns[8 : n - 8], columns[n - 8 : n] + last], axis=0)


def interface(edges, uf, sp, me, uc, cs, tr, sh, widen, narrow, tables, tall):
    comps, layers, rows, cols = uf.shape
    crows, ccols = sh.shape
    b = layers - 1

    left_f, right_f, left_c, right_c = tables
    some = jnp.concatenate([uf[i % comps, b] for i in range(256 // rows)], axis=0)
    lat_f = lateral12(some, left_f, right_f)
    some = jnp.concatenate([uc[i % comps, 0] for i in range(256 // crows)], axis=0)
    lat_c = lateral12(some, left_c, right_c)
    lf, lc = [], []
    for c in range(comps):
        lf.append(lat_f[c * rows : (c + 1) * rows, :] + edges.plane(edges.fine, c, b - 3, 3))
        lc.append(lat_c[c * crows : (c + 1) * crows, :] + edges.plane(edges.coarse, c, 0, 0))

    def stretch(planes):
        wide = times(jnp.concatenate(planes, axis=0), widen)
        n = len(planes) * crows
        for half in range(cols // LANES):
            part = wide[:, half * LANES : (half + 1) * LANES]
            tall[half, pl.ds(0, n, 2), :] = part
            tall[half, pl.ds(1, n, 2), :] = part
        return [
            jnp.concatenate(
                [tall[half, i * rows : (i + 1) * rows, :] for half in range(cols // LANES)], axis=1
            )
            for i in range(len(planes))
        ]

    def rows_of(planes):
        n = len(planes) * crows
        for i, plane in enumerate(planes):
            for half in range(cols // LANES):
                tall[half, i * rows : (i + 1) * rows, :] = plane[:, half * LANES : (half + 1) * LANES]
        return tuple(
            jnp.concatenate([tall[half, pl.ds(start, n, 2), :] for half in range(cols // LANES)], axis=1)
            for start in range(2)
        )

    s, m = sp[b], me[b]
    m2 = m * m
    gain = 1.0 / (s * m2)
    inv_m2 = 1.0 / m2
    cs0 = cs[0]
    inv_sh = 1.0 / sh[...]
    t = tr[...]
    c0 = [uc[c, 0] for c in range(comps)]
    pull = [
        cs0 * (lc[c] - 29.0 * uc[c, 0] + 16.0 * uc[c, 1] - uc[c, 2]) * TWELFTH for c in range(comps)
    ]
    wide = stretch([cs0] + pull + c0)
    alpha = gain * wide[0]
    beta, first, weighted = [], [], []
    for c in range(comps):
        ub, u1, u2 = uf[c, b], uf[c, b - 1], uf[c, b - 2]
        e = u2 - lf[c] * inv_m2 - 16.0 * u1 + 29.0 * ub
        bc = (12.0 * gain * wide[1 + c] + e) * (1.0 / 14.0)
        beta.append(bc)
        first.append(jnp.max(jnp.abs(alpha * wide[1 + comps + c] + bc - ub), axis=0, keepdims=True))
        weighted.append(t * bc)
        weighted.append(t * (u2 - 8.0 * u1 + 7.0 * ub))
        weighted.append(t * (u2 - 8.0 * u1 + ub))
    even_rows, odd_rows = rows_of([t * alpha] + weighted)
    sums = times(even_rows + odd_rows, narrow)
    even_rows, odd_rows = rows_of([alpha])
    top = jnp.maximum(even_rows, odd_rows)
    top = jnp.maximum(top, turn(top, -1, 1))
    lane = lax.broadcasted_iota(jnp.int32, top.shape, 1)
    top = jnp.where(lax.rem(lane, 2) == 0, top, 0.0)
    top = times(top, narrow)

    def part(i):
        return sums[i * crows : (i + 1) * crows, :]

    rate = part(0) * (0.5 * inv_sh)
    history = [[], [], [], []]
    c3s, c4s = [], []
    for c in range(comps):
        q6 = (8.0 * uc[c, 1] - uc[c, 0] - uc[c, 2]) * (1.0 / 6.0)
        pushed, start, still = part(1 + 3 * c), part(2 + 3 * c), part(3 + 3 * c)
        base = q6 - (still * TWELFTH + 0.5 * pushed) * inv_sh
        c1 = q6 - start * (TWELFTH * inv_sh)
        c2 = base - rate * c0[c]
        c3 = base - rate * c1
        c4 = base - rate * c2
        d1, d2, d3, d4 = (jnp.abs(x) for x in (c1 - c0[c], c2 - c1, c3 - c2, c4 - c3))
        history[0].append(d1)
        history[1].append(jnp.maximum(d2, top * d1))
        history[2].append(jnp.maximum(d3, top * d2))
        history[3].append(jnp.maximum(d4, top * d3))
        c3s.append(c3)
        c4s.append(c4)
    lane = lax.broadcasted_iota(jnp.int32, (1, LANES), 1)
    line = jnp.zeros((1, LANES), jnp.float32)
    for n in range(4):
        d = jnp.maximum(jnp.maximum(history[n][0], history[n][1]), history[n][2])
        d = jnp.max(d, axis=0, keepdims=True)
        if n == 0:
            f = jnp.maximum(jnp.maximum(first[0], first[1]), first[2])
            for half in range(cols // LANES):
                d = jnp.maximum(d, f[:, half * LANES : (half + 1) * LANES])
        line = jnp.where(lane == n, jnp.max(d, axis=1, keepdims=True), line)
    wide = stretch(c3s)
    return [alpha * wide[c] + beta[c] for c in range(comps)], c4s, line[:, 0:4]


def fix_kernel(vf_in, vc_in, pack, uf, sp, me, uc, cs, tr, sh, widen, narrow, *refs):
    tables, unpack, got = refs[0:4], refs[4], refs[5:9]
    vf, vc, change = refs[9:12]
    packed = refs[12:16]
    tall, slots = refs[16:]
    comps, layers, rows, cols = uf.shape
    edges = Edges(got, unpack, slots, (uf.shape[1:], uc.shape[2:]))
    ghost_f, ghost_c, line = interface(edges, uf, sp, me, uc, cs, tr, sh, widen, narrow, tables, tall)
    change[...] = line
    b = layers - 1
    s_last = sp[b] * me[b] * me[b] * TWELFTH
    s_next = sp[b - 1] * me[b - 1] * me[b - 1] * TWELFTH
    for c in range(comps):
        vf[c, b] = vf_in[c, b] + s_last * (14.0 * ghost_f[c] + uf[c, b])
        vf[c, b - 1] = vf_in[c, b - 1] - s_next * ghost_f[c]
        vc[c, 0] = vc_in[c, 0] + cs[0] * TWELFTH * (14.0 * ghost_c[c] + uc[c, 0])
        vc[c, 1] = vc_in[c, 1] - cs[1] * TWELFTH * ghost_c[c]

    @pl.loop(0, layers // 4)
    def _(quarter):
        g = quarter * 4
        for i in range(4):
            s12, cs12 = sp[g + i] * TWELFTH, cs[g + i] * TWELFTH
            for c in range(comps):
                vf[c, g + i] = vf_in[c, g + i] + s12 * edges.plane(edges.fine, c, g, i)
                vc[c, g + i] = vc_in[c, g + i] + cs12 * edges.plane(edges.coarse, c, g, i)

    pack_all(vf, vc, pack, *packed)


def interface_kernel(uf, sp, me, uc, cs, tr, sh, widen, narrow, *refs):
    tables, unpack, got = refs[0:4], refs[4], refs[5:9]
    ghost_f, ghost_c, change = refs[9:12]
    tall, slots = refs[12:]
    edges = Edges(got, unpack, slots, (uf.shape[1:], uc.shape[2:]))
    g, c4, line = interface(edges, uf, sp, me, uc, cs, tr, sh, widen, narrow, tables, tall)
    for c in range(uf.shape[0]):
        ghost_f[c] = g[c]
        ghost_c[c] = c4[c]
    change[...] = line


def last_kernel(first, stop, gate, sp, me, cs, uf, uc, vf, vc, ghost_f, ghost_c, unpack, *refs):
    got = refs[0:4]
    with_coarse = first == 0
    out_f, out_c = refs[4:6] if with_coarse else refs[6:8]
    done_f, done_c, slots, sem = refs[-4:]
    comps, layers, rows, cols = uf.shape
    b = layers - 1
    edges = Edges(got, unpack, slots, (uf.shape[1:], uc.shape[2:]))

    def copy(k):
        return pltpu.make_async_copy(done_f.at[:, k - first], out_f.at[:, k], sem.at[k - first])

    def copy_coarse():
        return pltpu.make_async_copy(done_c, out_c, sem.at[stop - first])

    if with_coarse:

        @pl.loop(0, layers // 4)
        def _(quarter):
            g = quarter * 4
            for i in range(4):
                cs12 = cs[g + i] * TWELFTH
                for c in range(comps):
                    done_c[c, g + i] = vc[c, g + i] + cs12 * edges.plane(edges.coarse, c, g, i)

        for c in range(comps):
            done_c[c, 0] = done_c[c, 0] + cs[0] * TWELFTH * (14.0 * ghost_c[c] + uc[c, 0])
            done_c[c, 1] = done_c[c, 1] - cs[1] * TWELFTH * ghost_c[c]
        copy_coarse().start()
    for g in range(first, stop, 4):
        for i in range(4):
            k = g + i
            s12 = sp[k] * TWELFTH
            for c in range(comps):
                total = edges.plane(edges.fine, c, g, i)
                if k == b:
                    total = total + me[k] * me[k] * (14.0 * ghost_f[c] + uf[c, b])
                if k == b - 1:
                    total = total - me[k] * me[k] * ghost_f[c]
                done_f[c, k - first] = vf[c, k] + s12 * total
            copy(k).start()
    for k in range(first, stop):
        copy(k).wait()
    if with_coarse:
        copy_coarse().wait()


def call(kernel, args, outs, scratch=(), alias={}, flops=0, hbm=()):
    spaces = [pltpu.HBM if i in hbm else pltpu.VMEM for i in range(len(args))]
    return pl.pallas_call(
        kernel,
        out_shape=tuple(outs),
        in_specs=[pl.BlockSpec(memory_space=s) for s in spaces],
        out_specs=tuple(pl.BlockSpec(memory_space=o.memory_space) for o in outs),
        scratch_shapes=list(scratch),
        input_output_aliases=alias,
        cost_estimate=pl.CostEstimate(flops=flops, bytes_accessed=flops, transcendentals=0),
        compiler_params=pltpu.CompilerParams(vmem_limit_bytes=VMEM_LIMIT),
    )(*[pltpu.with_memory_space_constraint(x, s) for x, s in zip(args, spaces)])


def exchange(parts):
    x_down, x_up, y_down, y_up = parts

    def ring(value, axis, by):
        n = lax.axis_size(axis)
        return lax.ppermute(value, axis, [(i, (i + by) % n) for i in range(n)])

    return (ring(x_down, "gx", -1), ring(x_up, "gx", 1), ring(y_down, Y, -1), ring(y_up, Y, 1))


def rounds():
    found = []
    for axis in ("gx", "gy", "grid"):
        n, far = lax.axis_size(axis), 1
        while far < n:
            pairs = [(i, i ^ far) if n & (n - 1) == 0 else (i, (i + far) % n) for i in range(n)]
            found.append((axis, pairs))
            far *= 2
    return found


def on_device(
    fine_field, fine_previous, fine_speed, fine_metric, coarse_field, coarse_previous, coarse_speed,
    fine_traction, coarse_shear,
):
    f32 = jnp.float32
    comps, layers, rows, cols = fine_field.shape
    crows, ccols = coarse_field.shape[2:]
    fine = pltpu.VMEM(fine_field.shape, f32)
    coarse = pltpu.VMEM(coarse_field.shape, f32)
    plane_f = pltpu.VMEM((comps, rows, cols), f32)
    plane_c = pltpu.VMEM((comps, crows, ccols), f32)
    line = pltpu.VMEM((1, 4), f32)
    corrections = pltpu.VMEM((2, rows + crows, LANES), f32)
    edge_outs = [
        pltpu.VMEM((comps * layers // 4, 8, cols + ccols), f32),
        pltpu.VMEM((comps * layers // 4, 8, cols + ccols), f32),
        pltpu.VMEM((rows + crows, LANES), f32),
        pltpu.VMEM((rows + crows, LANES), f32),
    ]
    solve_scratch = [pltpu.VMEM((cols // LANES, 10 * rows, LANES), f32), corrections]
    picks = np.zeros((cols, ccols), np.float32)
    picks[np.arange(cols), np.arange(cols) // 2] = 1.0
    narrow = jnp.asarray(np.tile(picks, (3, 1)), jnp.bfloat16)
    widen = jnp.asarray(np.tile(picks.T, (3, 1)), jnp.bfloat16)
    sp, me, cs = fine_speed, fine_metric, coarse_speed
    tables = (*lateral_tables(rows, cols), *lateral_tables(crows, ccols))
    pack, unpack = column_tables(comps * layers)
    fixed = (fine_traction, coarse_shear, widen, narrow, *tables, unpack)
    lat = pltpu.VMEM((comps, 256, cols), f32)

    uf, uc, *mine = call(
        load_kernel, (fine_field, coarse_field, pack), [fine, coarse] + edge_outs,
        scratch=[pltpu.VMEM(pack.shape, pack.dtype), pltpu.SemaphoreType.DMA((3, layers // 4))], hbm=(0, 1, 2),
    )
    pf, pc = fine_previous, coarse_previous
    theirs = exchange(mine)
    vf, vc = call(
        functools.partial(main_kernel, True), (uf, pf, sp, me, uc, pc, cs, *tables), [fine, coarse],
        scratch=[lat, fine, pltpu.SemaphoreType.DMA((layers,))], hbm=(1,), flops=40_000_000,
    )
    vf, vc, change0, *ours = call(
        fix_kernel,
        (vf, vc, pack, uf, sp, me, uc, cs) + fixed + theirs,
        [fine, coarse, line] + edge_outs, scratch=solve_scratch, alias={0: 0, 1: 1}, flops=20_000_000,
    )
    pf, pc, uf, uc, mine = uf, uc, vf, vc, ours
    theirs = exchange(mine)
    vf, vc = call(
        functools.partial(main_kernel, False), (uf, pf, sp, me, uc, pc, cs, *tables), [fine, coarse],
        scratch=[lat], flops=40_000_000,
    )
    ghost_f, ghost_c, change1 = call(
        interface_kernel,
        (uf, sp, me, uc, cs) + fixed + theirs,
        [plane_f, plane_c, line], scratch=solve_scratch, flops=10_000_000,
    )
    history = jnp.concatenate([change0, change1], axis=0)
    steps = rounds()
    bounds = [0, 4, 8, 12, layers]
    outs = ()
    for i in range(max(len(steps), len(bounds) - 1)):
        if i < len(steps):
            axis, pairs = steps[i]
            arrived = lax.ppermute(history, axis, pairs)
        if i < len(bounds) - 1:
            first, stop = bounds[i : i + 2]
            args = (history, sp, me, cs, uf, uc, vf, vc, ghost_f, ghost_c, unpack, *theirs, *outs)
            n = len(args)
            outs = call(
                functools.partial(last_kernel, first, stop), args,
                [pltpu.HBM(fine_field.shape, f32), pltpu.HBM(coarse_field.shape, f32)],
                scratch=[
                    pltpu.VMEM((comps, stop - first, rows, cols), f32), coarse, corrections,
                    pltpu.SemaphoreType.DMA((stop - first + 1,)),
                ],
                alias={n - 2: 0, n - 1: 1} if outs else {}, hbm=(n - 2, n - 1) if outs else (), flops=10_000_000,
            )
        if i < len(steps):
            history = jnp.maximum(history, arrived)
    return outs[0], outs[1], history


def solution(mesh):
    field = P(None, None, "gx", Y)
    layered = P(None, "gx", Y)
    plane = P("gx", Y)
    return jax.shard_map(
        on_device,
        mesh=mesh,
        in_specs=(field, field, layered, layered, field, field, layered, plane, plane),
        out_specs=(field, field, P()),
        check_vma=False,
    )
```

time: 58.6 us -> 51.9 us (0.89)
  Pallas kernels: 30.5 us -> 23.1 us
  waiting for transfers between devices: 9.78 us -> 13.4 us
  local copies, waits for them, and re-layouts: 1.92 us -> 0.08 us
  starting transfers between devices: 14.7 us -> 13.6 us
    pallas_call x10 -> x9, Pallas kernels: 30.5 us -> 23.1 us  [call(): pl.pallas_call(kernel, out_shape=tuple(outs), in_specs=[pl.BlockSpec(memo...]
    ppermute x5, waiting for transfers between devices: 6.08 us -> 9.71 us  [on_device(): arrived = lax.ppermute(history, axis, pairs)]
    unnamed x18 -> x28, local copies, waits for them, and re-layouts: 1.92 us -> 0.08 us
    ppermute x8, starting transfers between devices: 12.9 us -> 11.9 us  [ring(): return lax.ppermute(value, axis, [(i, (i + by) % n) for i in range(n)])]
  transfers between devices with their start and end apart: 13 -> 13, of which waited for: 5 -> 6; matrix products, arithmetic and copies ran while one was open for 0% -> 0% of each run, Pallas kernels for 35% -> 30%
where the time goes in v3:
time: 51.9 us; the launch traced here: 51.7 us
  Pallas kernels  23.1 us (45%)
  starting transfers between devices  13.6 us (26%)
  waiting for transfers between devices  13.4 us (26%)
  between operations  0.97 us (2%)
  other arithmetic  0.6 us (1%)
    pallas_call x9, Pallas kernels, call(): pl.pallas_call(kernel, out_shape=tuple(outs), in_specs=[pl.BlockSpec(memo...  23.1 us
    ppermute x8, starting transfers between devices, ring(): return lax.ppermute(value, axis, [(i, (i + by) % n) for i in range(n)])  11.9 us
    ppermute x5, waiting for transfers between devices, on_device(): arrived = lax.ppermute(history, axis, pairs)  9.71 us
    ppermute x8, waiting for transfers between devices, ring(): return lax.ppermute(value, axis, [(i, (i + by) % n) for i in range(n)])  3.69 us
    ppermute x5, starting transfers between devices, on_device(): arrived = lax.ppermute(history, axis, pairs)  1.72 us
  transfers between devices with their start and end apart: 13, of which 6 were waited for; matrix products, arithmetic and copies ran while one was open for 0% of the time, Pallas kernels for 30%

profile of v3, /device:TPU:0, one launch (start us, length us, event | category | flops | bytes accessed | tf_op | source)
XLA Modules:
  0.0 51.7 jit_solution(4689613598354852007)
XLA Ops:
  0.6 0.0 copy-start.4
  0.6 0.0 copy-start.5
  0.7 0.0 copy-start.6
  0.7 0.0 copy-start.8
  0.7 3.0 %shard_map.184 = (f32[3,16,64,256]{3,2,1,0:T(8,128)S(1)}, f32[3,16,32,128]{3,2,1,0:T(8,128)S(1)}, f32[12,8,384]{2,1,0:T(8,128)S(1)}, f32[12,8,384]{2,1,0:T(8,128...) custom-call(f32[3,16,64,256]{3,2,1,0:T(8,128)} %uf_hbm.1, f32[3,16,32,128]{3,2,1,0:T(8,128)} %uc_hbm.1, ...), custom_call_target="tpu_custom_call" | custom-call | tf_op jit(solution)/shard_map/pallas_call | solution.py:419
  3.7 2.5 %collective-permute-start = (f32[12,8,384]{2,1,0:T(8,128)S(1)}, f32[12,8,384]{2,1,0:T(8,128)S(1)}, u32[]{:S(2)}, u32[]{:S(2)}) collective-permute-start(f32[12,8,384]{2,1,0:T(8,128)S(1)} %get-tuple-element.35), channel_id=1, source_target_pairs={{0,12},{4,0},{8,4},{12,8},{1,13},{5,1},{9,5},{13,9},{2,14},{6,2},{... | collective-permute-start | bytes 442376 | tf_op jit(solution)/shard_map/ppermute | solution.py:436
  6.1 4.5 %collective-permute-start.2 = (f32[96,128]{1,0:T(8,128)S(1)}, f32[96,128]{1,0:T(8,128)S(1)}, u32[]{:S(2)}, u32[]{:S(2)}) collective-permute-start(f32[96,128]{1,0:T(8,128)S(1)} %get-tuple-element.37), channel_id=1, source_target_pairs={{0,19},{1,0},{2,1},{3,2},{16,3},{17,16},{18,17},{19,18},{4,23},{5,... | collective-permute-start | bytes 147464 | tf_op jit(solution)/shard_map/ppermute | solution.py:436
  10.7 0.0 copy-start.3
  10.8 0.0 copy-start.7
  10.8 0.0 copy-start.10
  10.8 0.0 copy-start.11
  10.8 5.5 %shard_map.185 = (f32[3,16,64,256]{3,2,1,0:T(8,128)S(1)}, f32[3,16,32,128]{3,2,1,0:T(8,128)S(1)}) custom-call(f32[3,16,64,256]{3,2,1,0:T(8,128)S(1)} %get-tuple-element.31.uf.pf_in, f32[3,16,64,256]{3,2,1,0:T(8,128)} %pf_in.1, f32[16,64,256]{2,1,0:T(8,128)S(1)} %copy-done, f32[16,64,256]{2,1,0:T(8,128)S(1)} %copy-done.1, ...), custom_call_target="tpu_custom_call" | custom-call | flops 40000000 | bytes 40000000 | tf_op jit(solution)/shard_map/pallas_call | solution.py:419
  16.4 1.1 %collective-permute-done.3.refs_8_ = f32[96,128]{1,0:T(8,128)S(1)} collective-permute-done((f32[96,128]{1,0:T(8,128)S(1)}, f32[96,128]{1,0:T(8,128)S(1)}, u32[]{:S(2)}, u32[]{:S(2)}) %collective-permute-start.3) | collective-permute-done | bytes 49184 | tf_op jit(solution)/shard_map/ppermute | solution.py:436
  17.5 3.2 %shard_map.186 = (f32[3,16,64,256]{3,2,1,0:T(8,128)S(1)}, f32[3,16,32,128]{3,2,1,0:T(8,128)S(1)}, f32[1,4]{1,0:T(1,128)S(1)}, f32[12,8,384]{2,1,0:T(8,128)S(1)},...) custom-call(f32[3,16,64,256]{3,2,1,0:T(8,128)S(1)} %get-tuple-elemen, ...), custom_call_target="tpu_custom_call", output_to_operand_aliasing={{0}: (0, {}), {1}: (1, {})} | custom-call | flops 20000000 | bytes 20000000 | tf_op jit(solution)/shard_map/pallas_call | solution.py:419
  20.8 1.0 %collective-permute-start.4 = (f32[12,8,384]{2,1,0:T(8,128)S(1)}, f32[12,8,384]{2,1,0:T(8,128)S(1)}, u32[]{:S(2)}, u32[]{:S(2)}) collective-permute-start(f32[12,8,384]{2,1,0:T(8,128)S(1)} %get-tuple-element.42), channel_id=1, source_target_pairs={{0,12},{4,0},{8,4},{12,8},{1,13},{5,1},{9,5},{13,9},{2,14},{6,2},{... | collective-permute-start | bytes 442376 | tf_op jit(solution)/shard_map/ppermute | solution.py:436
  21.8 3.9 %collective-permute-start.6 = (f32[96,128]{1,0:T(8,128)S(1)}, f32[96,128]{1,0:T(8,128)S(1)}, u32[]{:S(2)}, u32[]{:S(2)}) collective-permute-start(f32[96,128]{1,0:T(8,128)S(1)} %get-tuple-element.44), channel_id=1, source_target_pairs={{0,19},{1,0},{2,1},{3,2},{16,3},{17,16},{18,17},{19,18},{4,23},{5,... | collective-permute-start | bytes 147464 | tf_op jit(solution)/shard_map/ppermute | solution.py:436
  25.6 4.2 %shard_map.188 = (f32[3,16,64,256]{3,2,1,0:T(8,128)S(1)}, f32[3,16,32,128]{3,2,1,0:T(8,128)S(1)}) custom-call(f32[3,16,64,256]{3,2,1,0:T(8,128)S(1)} %get-tuple-element.40.uf, f32[3,16,64,256]{3,2,1,0:T(8,128)S(1)} %get-tuple-element.31.uf.pf_in, f32[16,64,256]{2,1,0:T(8,128)S(1)} %copy-done, f32[16,64,256]{2,1,0:T(8,128)S(1)} %copy-done.1, ...), custom_call_target="tpu_custom_call" | custom-call | flops 40000000 | bytes 40000000 | tf_op jit(solution)/shard_map/pallas_call | solution.py:419
  29.9 2.6 %collective-permute-done.7.refs_8_.refs_3_ = f32[96,128]{1,0:T(8,128)S(1)} collective-permute-done((f32[96,128]{1,0:T(8,128)S(1)}, f32[96,128]{1,0:T(8,128)S(1)}, u32[]{:S(2)}, u32[]{:S(2)}) %collective-permute-start.7) | collective-permute-done | bytes 49184 | tf_op jit(solution)/shard_map/ppermute | solution.py:436
  32.4 1.3 %shard_map.187 = (f32[3,64,256]{2,1,0:T(8,128)S(1)}, f32[3,32,128]{2,1,0:T(8,128)S(1)}, f32[1,4]{1,0:T(1,128)S(1)}) custom-call(f32[3,16,64,256]{3,2,1,0:T(8,128)S(1)} %get-tuple-element.40.uf, f32[16,64,256]{2,1,0:T(8,128)S(1)} %copy-done, f32[16,64,256]{2,1,0:T(8,128)S(1)} %copy-done.1, f32[3,16,32,128]{3,2,1,0:T(8,128)S(1)} %get-tuple-element.41.uc, ...), custom_call_target="tpu_custom_call" | custom-call | flops 10000000 | bytes 10000000 | tf_op jit(solution)/shard_map/pallas_call | solution.py:419
  33.7 0.1 collective-permute-start.8
  33.8 2.0 %shard_map.189 = (f32[3,16,64,256]{3,2,1,0:T(8,128)}, f32[3,16,32,128]{3,2,1,0:T(8,128)}) custom-call(f32[2,4]{1,0:T(2,128)S(1)} %pad_maximum_fusion.gate, f32[16,64,256]{2,1,0:T(8,128)S(1)} %copy-done, f32[16,64,256]{2,1,0:T(8,128)S(1)} %copy-done.1, f32[16,32,128]{2,1,0:T(8,128)S(1)} %copy-done.2, f32[3,16,64,256]{3,2,1,0:T(8,128)S(1)} %get-tuple-element.40.uf, ...), custom_call_target="tpu_custom_call" | custom-call | flops 10000000 | bytes 10000000 | tf_op jit(solution)/shard_map/pallas_call | solution.py:419
  35.8 1.0 %collective-permute-start.9 = (f32[2,4]{1,0:T(2,128)S(1)}, f32[2,4]{1,0:T(2,128)S(1)}, u32[]{:S(2)}, u32[]{:S(2)}) collective-permute-start(f32[2,4]{1,0:T(2,128)S(1)} %fusion.gate), channel_id=1, source_target_pairs={{0,8},{4,12},{8,0},{12,4},{1,9},{5,13},{9,1},{13,5},{2,10},{6,14},... | collective-permute-start | bytes 104 | tf_op jit(solution)/shard_map/ppermute | solution.py:515
  36.8 1.3 %shard_map.190 = (f32[3,16,64,256]{3,2,1,0:T(8,128)}, f32[3,16,32,128]{3,2,1,0:T(8,128)}) custom-call(f32[2,4]{1,0:T(2,128)S(1)} %fusion.gate, f32[16,64,256]{2,1,0:T(8,128)S(1)} %copy-done, f32[16,64,256]{2,1,0:T(8,128)S(1)} %copy-done.1, f32[16,32,128]{2,1,0:T(8,128)S(1)} %copy-done.2, ...), custom_call_target="tpu_custom_call", output_to_operand_aliasing={{0}: (15, {}), {1}: (16, {})} | custom-call | flops 10000000 | bytes 10000000 | tf_op jit(solution)/shard_map/pallas_call | solution.py:419
  38.2 1.3 %collective-permute-done.9 = f32[2,4]{1,0:T(2,128)S(1)} collective-permute-done((f32[2,4]{1,0:T(2,128)S(1)}, f32[2,4]{1,0:T(2,128)S(1)}, u32[]{:S(2)}, u32[]{:S(2)}) %collective-permute-start.9) | collective-permute-done | bytes 64 | tf_op jit(solution)/shard_map/ppermute | solution.py:515
  39.5 0.1 collective-permute-start.10
  39.5 1.3 %shard_map.191 = (f32[3,16,64,256]{3,2,1,0:T(8,128)}, f32[3,16,32,128]{3,2,1,0:T(8,128)}) custom-call(f32[2,4]{1,0:T(2,128)S(1)} %fusion.1.gate, f32[16,64,256]{2,1,0:T(8,128)S(1)} %copy-done, f32[16,64,256]{2,1,0:T(8,128)S(1)} %copy-done.1, f32[16,32,128]{2,1,0:T(8,128)S(1)} %copy-done.2, ...), custom_call_target="tpu_custom_call", output_to_operand_aliasing={{0}: (15, {}), {1}: (16, {})} | custom-call | flops 10000000 | bytes 10000000 | tf_op jit(solution)/shard_map/pallas_call | solution.py:419
  40.9 2.2 %collective-permute-done.10 = f32[2,4]{1,0:T(2,128)S(1)} collective-permute-done((f32[2,4]{1,0:T(2,128)S(1)}, f32[2,4]{1,0:T(2,128)S(1)}, u32[]{:S(2)}, u32[]{:S(2)}) %collective-permute-start.10) | collective-permute-done | bytes 64 | tf_op jit(solution)/shard_map/ppermute | solution.py:515
  43.1 1.3 %shard_map.192 = (f32[3,16,64,256]{3,2,1,0:T(8,128)}, f32[3,16,32,128]{3,2,1,0:T(8,128)}) custom-call(f32[2,4]{1,0:T(2,128)S(1)} %max.17.gate, f32[16,64,256]{2,1,0:T(8,128)S(1)} %copy-done, f32[16,64,256]{2,1,0:T(8,128)S(1)} %copy-done.1, f32[16,32,128]{2,1,0:T(8,128)S(1)} %copy-done.2, ...), custom_call_target="tpu_custom_call", output_to_operand_aliasing={{0}: (15, {}), {1}: (16, {})} | custom-call | flops 10000000 | bytes 10000000 | tf_op jit(solution)/shard_map/pallas_call | solution.py:419
  44.4 3.1 %collective-permute-done.11 = f32[2,4]{1,0:T(2,128)S(1)} collective-permute-done((f32[2,4]{1,0:T(2,128)S(1)}, f32[2,4]{1,0:T(2,128)S(1)}, u32[]{:S(2)}, u32[]{:S(2)}) %collective-permute-start.11) | collective-permute-done | bytes 64 | tf_op jit(solution)/shard_map/ppermute | solution.py:515
  47.6 0.5 %collective-permute-start.12 = (f32[2,4]{1,0:T(2,128)S(1)}, f32[2,4]{1,0:T(2,128)S(1)}, u32[]{:S(2)}, u32[]{:S(2)}) collective-permute-start(f32[2,4]{1,0:T(2,128)S(1)} %max.18), channel_id=1, source_target_pairs={{0,16},{16,0},{1,17},{17,1},{2,18},{18,2},{3,19},{19,3},{4,20},{20... | collective-permute-start | bytes 104 | tf_op jit(solution)/shard_map/ppermute | solution.py:515
  48.1 3.0 %collective-permute-done.12 = f32[2,4]{1,0:T(2,128)S(1)} collective-permute-done((f32[2,4]{1,0:T(2,128)S(1)}, f32[2,4]{1,0:T(2,128)S(1)}, u32[]{:S(2)}, u32[]{:S(2)}) %collective-permute-start.12) | collective-permute-done | bytes 64 | tf_op jit(solution)/shard_map/ppermute | solution.py:515
  51.1 0.6 %max.19 = f32[2,4]{1,0:T(2,128)} maximum(f32[2,4]{1,0:T(2,128)S(1)} %max.18, f32[2,4]{1,0:T(2,128)S(1)} %collective-permute-done.12) | non-fusion elementwise | flops 8 | bytes 96 | tf_op jit(solution)/shard_map/max | solution.py:530
  (37 shorter events, 0.1 us)
Async XLA Ops:
  0.6 10.0 %copy-start.4 = (bf16[256,512]{1,0:T(8,128)(2,1)S(1)}, bf16[256,512]{1,0:T(8,128)(2,1)}, u32[]{:S(2)}) copy-start(bf16[256,512]{1,0:T(8,128)(2,1)} %constant.18.clone.left_f.refs_0_) | copy-start | bytes 786436
  0.6 10.0 %copy-start.5 = (bf16[512,256]{1,0:T(8,128)(2,1)S(1)}, bf16[512,256]{1,0:T(8,128)(2,1)}, u32[]{:S(2)}) copy-start(bf16[512,256]{1,0:T(8,128)(2,1)} %constant.19.clone.right_f.refs_1_) | copy-start | bytes 786436
  0.7 10.0 %copy-start.6 = (bf16[256,512]{1,0:T(8,128)(2,1)S(1)}, bf16[256,512]{1,0:T(8,128)(2,1)}, u32[]{:S(2)}) copy-start(bf16[256,512]{1,0:T(8,128)(2,1)} %constant.20.clone.left_c.refs_2_) | copy-start | bytes 786436
  0.7 10.0 %copy-start.8 = (bf16[256,128]{1,0:T(8,128)(2,1)S(1)}, bf16[256,128]{1,0:T(8,128)(2,1)}, u32[]{:S(2)}) copy-start(bf16[256,128]{1,0:T(8,128)(2,1)} %constant.21.clone.right_c.refs_3_) | copy-start | bytes 196612
  0.7 10.0 %copy-start = (f32[16,64,256]{2,1,0:T(8,128)S(1)}, f32[16,64,256]{2,1,0:T(8,128)}, u32[]{:S(2)}) copy-start(f32[16,64,256]{2,1,0:T(8,128)} %sp.15) | copy-start | bytes 3145732
  0.7 10.0 %copy-start.1 = (f32[16,64,256]{2,1,0:T(8,128)S(1)}, f32[16,64,256]{2,1,0:T(8,128)}, u32[]{:S(2)}) copy-start(f32[16,64,256]{2,1,0:T(8,128)} %me.15) | copy-start | bytes 3145732
  0.7 10.0 %copy-start.9 = (f32[3,16,32,128]{3,2,1,0:T(8,128)S(1)}, f32[3,16,32,128]{3,2,1,0:T(8,128)}, u32[]{:S(2)}) copy-start(f32[3,16,32,128]{3,2,1,0:T(8,128)} %pc.1) | copy-start | bytes 2359300
  0.7 10.0 %copy-start.2 = (f32[16,32,128]{2,1,0:T(8,128)S(1)}, f32[16,32,128]{2,1,0:T(8,128)}, u32[]{:S(2)}) copy-start(f32[16,32,128]{2,1,0:T(8,128)} %cs.15) | copy-start | bytes 786436
  3.7 13.8 %collective-permute-start = (f32[12,8,384]{2,1,0:T(8,128)S(1)}, f32[12,8,384]{2,1,0:T(8,128)S(1)}, u32[]{:S(2)}, u32[]{:S(2)}) collective-permute-start(f32[12,8,384]{2,1,0:T(8,128)S(1)} %get-tuple-element.35), channel_id=1, source_target_pairs={{0,12},{4,0},{8,4},{12,8},{1,13},{5,1},{9,5},{13,9},{2,14},{6,2},{... | collective-permute-start | bytes 442376 | tf_op jit(solution)/shard_map/ppermute | solution.py:436
  6.1 11.3 %collective-permute-start.1 = (f32[12,8,384]{2,1,0:T(8,128)S(1)}, f32[12,8,384]{2,1,0:T(8,128)S(1)}, u32[]{:S(2)}, u32[]{:S(2)}) collective-permute-start(f32[12,8,384]{2,1,0:T(8,128)S(1)} %get-tuple-element.36), channel_id=1, source_target_pairs={{0,4},{4,8},{8,12},{12,0},{1,5},{5,9},{9,13},{13,1},{2,6},{6,10},{... | collective-permute-start | bytes 442376 | tf_op jit(solution)/shard_map/ppermute | solution.py:436
  6.1 10.2 %collective-permute-start.2 = (f32[96,128]{1,0:T(8,128)S(1)}, f32[96,128]{1,0:T(8,128)S(1)}, u32[]{:S(2)}, u32[]{:S(2)}) collective-permute-start(f32[96,128]{1,0:T(8,128)S(1)} %get-tuple-element.37), channel_id=1, source_target_pairs={{0,19},{1,0},{2,1},{3,2},{16,3},{17,16},{18,17},{19,18},{4,23},{5,... | collective-permute-start | bytes 147464 | tf_op jit(solution)/shard_map/ppermute | solution.py:436
  10.7 6.8 %collective-permute-start.3 = (f32[96,128]{1,0:T(8,128)S(1)}, f32[96,128]{1,0:T(8,128)S(1)}, u32[]{:S(2)}, u32[]{:S(2)}) collective-permute-start(f32[96,128]{1,0:T(8,128)S(1)} %get-tuple-element.38), channel_id=1, source_target_pairs={{0,1},{1,2},{2,3},{3,16},{16,17},{17,18},{18,19},{19,0},{4,5},{5,6... | collective-permute-start | bytes 147464 | tf_op jit(solution)/shard_map/ppermute | solution.py:436
  10.7 6.7 %copy-start.3 = (bf16[768,256]{1,0:T(8,128)(2,1)S(1)}, bf16[768,256]{1,0:T(8,128)(2,1)}, u32[]{:S(2)}) copy-start(bf16[768,256]{1,0:T(8,128)(2,1)} %constant.23.clone.refs_4_.unpack) | copy-start | bytes 1179652
  10.8 6.7 %copy-start.7 = (bf16[768,256]{1,0:T(8,128)(2,1)S(1)}, bf16[768,256]{1,0:T(8,128)(2,1)}, u32[]{:S(2)}) copy-start(bf16[768,256]{1,0:T(8,128)(2,1)} %constant.22.clone.pack_hbm.pack) | copy-start | bytes 1179652
  10.8 6.7 %copy-start.10 = (bf16[384,256]{1,0:T(8,128)(2,1)S(1)}, bf16[384,256]{1,0:T(8,128)(2,1)}, u32[]{:S(2)}) copy-start(bf16[384,256]{1,0:T(8,128)(2,1)} %constant.17.clone.widen) | copy-start | bytes 589828
  10.8 6.7 %copy-start.11 = (bf16[768,128]{1,0:T(8,128)(2,1)S(1)}, bf16[768,128]{1,0:T(8,128)(2,1)}, u32[]{:S(2)}) copy-start(bf16[768,128]{1,0:T(8,128)(2,1)} %constant.16.clone.narrow) | copy-start | bytes 589828
  10.8 6.7 %copy-start.12 = (f32[64,256]{1,0:T(8,128)S(1)}, f32[64,256]{1,0:T(8,128)}, u32[]{:S(2)}) copy-start(f32[64,256]{1,0:T(8,128)} %tr.3) | copy-start | bytes 196612
  10.8 6.7 %copy-start.13 = (f32[32,128]{1,0:T(8,128)S(1)}, f32[32,128]{1,0:T(8,128)}, u32[]{:S(2)}) copy-start(f32[32,128]{1,0:T(8,128)} %sh.3) | copy-start | bytes 49156
  20.8 11.7 %collective-permute-start.4 = (f32[12,8,384]{2,1,0:T(8,128)S(1)}, f32[12,8,384]{2,1,0:T(8,128)S(1)}, u32[]{:S(2)}, u32[]{:S(2)}) collective-permute-start(f32[12,8,384]{2,1,0:T(8,128)S(1)} %get-tuple-element.42), channel_id=1, source_target_pairs={{0,12},{4,0},{8,4},{12,8},{1,13},{5,1},{9,5},{13,9},{2,14},{6,2},{... | collective-permute-start | bytes 442376 | tf_op jit(solution)/shard_map/ppermute | solution.py:436
  21.8 10.7 %collective-permute-start.5 = (f32[12,8,384]{2,1,0:T(8,128)S(1)}, f32[12,8,384]{2,1,0:T(8,128)S(1)}, u32[]{:S(2)}, u32[]{:S(2)}) collective-permute-start(f32[12,8,384]{2,1,0:T(8,128)S(1)} %get-tuple-element.43), channel_id=1, source_target_pairs={{0,4},{4,8},{8,12},{12,0},{1,5},{5,9},{9,13},{13,1},{2,6},{6,10},{... | collective-permute-start | bytes 442376 | tf_op jit(solution)/shard_map/ppermute | solution.py:436
  21.8 8.1 %collective-permute-start.6 = (f32[96,128]{1,0:T(8,128)S(1)}, f32[96,128]{1,0:T(8,128)S(1)}, u32[]{:S(2)}, u32[]{:S(2)}) collective-permute-start(f32[96,128]{1,0:T(8,128)S(1)} %get-tuple-element.44), channel_id=1, source_target_pairs={{0,19},{1,0},{2,1},{3,2},{16,3},{17,16},{18,17},{19,18},{4,23},{5,... | collective-permute-start | bytes 147464 | tf_op jit(solution)/shard_map/ppermute | solution.py:436
  25.6 6.8 %collective-permute-start.7 = (f32[96,128]{1,0:T(8,128)S(1)}, f32[96,128]{1,0:T(8,128)S(1)}, u32[]{:S(2)}, u32[]{:S(2)}) collective-permute-start(f32[96,128]{1,0:T(8,128)S(1)} %get-tuple-element.45), channel_id=1, source_target_pairs={{0,1},{1,2},{2,3},{3,16},{16,17},{17,18},{18,19},{19,0},{4,5},{5,6... | collective-permute-start | bytes 147464 | tf_op jit(solution)/shard_map/ppermute | solution.py:436
  33.7 2.1 %collective-permute-start.8 = (f32[2,4]{1,0:T(2,128)S(1)}, f32[2,4]{1,0:T(2,128)S(1)}, u32[]{:S(2)}, u32[]{:S(2)}) collective-permute-start(f32[2,4]{1,0:T(2,128)S(1)} %pad_maximum_fusion.gate), channel_id=1, source_target_pairs={{0,4},{4,0},{8,12},{12,8},{1,5},{5,1},{9,13},{13,9},{2,6},{6,2},{1... | collective-permute-start | bytes 104 | tf_op jit(solution)/shard_map/ppermute | solution.py:515
  35.8 3.6 %collective-permute-start.9 = (f32[2,4]{1,0:T(2,128)S(1)}, f32[2,4]{1,0:T(2,128)S(1)}, u32[]{:S(2)}, u32[]{:S(2)}) collective-permute-start(f32[2,4]{1,0:T(2,128)S(1)} %fusion.gate), channel_id=1, source_target_pairs={{0,8},{4,12},{8,0},{12,4},{1,9},{5,13},{9,1},{13,5},{2,10},{6,14},... | collective-permute-start | bytes 104 | tf_op jit(solution)/shard_map/ppermute | solution.py:515
  39.5 3.6 %collective-permute-start.10 = (f32[2,4]{1,0:T(2,128)S(1)}, f32[2,4]{1,0:T(2,128)S(1)}, u32[]{:S(2)}, u32[]{:S(2)}) collective-permute-start(f32[2,4]{1,0:T(2,128)S(1)} %fusion.1.gate), channel_id=1, source_target_pairs={{0,1},{1,0},{2,3},{3,2},{4,5},{5,4},{6,7},{7,6},{8,9},{9,8},{10,11... | collective-permute-start | bytes 104 | tf_op jit(solution)/shard_map/ppermute | solution.py:515
  43.1 4.5 %collective-permute-start.11 = (f32[2,4]{1,0:T(2,128)S(1)}, f32[2,4]{1,0:T(2,128)S(1)}, u32[]{:S(2)}, u32[]{:S(2)}) collective-permute-start(f32[2,4]{1,0:T(2,128)S(1)} %max.17.gate), channel_id=1, source_target_pairs={{0,2},{1,3},{2,0},{3,1},{4,6},{5,7},{6,4},{7,5},{8,10},{9,11},{10,... | collective-permute-start | bytes 104 | tf_op jit(solution)/shard_map/ppermute | solution.py:515
  47.6 3.6 %collective-permute-start.12 = (f32[2,4]{1,0:T(2,128)S(1)}, f32[2,4]{1,0:T(2,128)S(1)}, u32[]{:S(2)}, u32[]{:S(2)}) collective-permute-start(f32[2,4]{1,0:T(2,128)S(1)} %max.18), channel_id=1, source_target_pairs={{0,16},{16,0},{1,17},{17,1},{2,18},{18,2},{3,19},{19,3},{4,20},{20... | collective-permute-start | bytes 104 | tf_op jit(solution)/shard_map/ppermute | solution.py:515

commit v4 on v3

v4 whole, which is shorter than its diff:
```python
import functools

import jax
import jax.numpy as jnp
import numpy as np
from jax import lax
from jax.experimental import pallas as pl
from jax.experimental.pallas import tpu as pltpu
from jax.sharding import PartitionSpec as P

STEPS = 2
LANES = 128
TWELFTH = 1.0 / 12.0
Y = ("grid", "gy")
ALL = ("grid", "gx", "gy")
VMEM_LIMIT = 16 << 20


def turn(x, by, axis):
    return pltpu.roll(x, by % x.shape[axis], axis)


def bands(length, copies):
    one = sum(w * np.eye(length, k=o) for o, w in ((1, 16.0), (-1, 16.0), (2, -1.0), (-2, -1.0)))
    return np.kron(np.eye(copies), one)


def lateral_tables(rows, cols):
    stack = 256 // rows
    left, right = bands(rows, stack), bands(cols, 1)
    return (
        jnp.asarray(np.concatenate([left, left], axis=1), jnp.bfloat16),
        jnp.asarray(np.concatenate([right, right], axis=0), jnp.bfloat16),
    )


def lateral12(planes, left, right):
    a = planes.astype(jnp.bfloat16)
    b = (planes - a.astype(jnp.float32)).astype(jnp.bfloat16)
    y = jnp.dot(jnp.concatenate([a, b], axis=1), right[...], preferred_element_type=jnp.float32)
    x = jnp.dot(left[...], jnp.concatenate([a, b], axis=0), preferred_element_type=jnp.float32)
    return (x + y) - 60.0 * planes


def depth12(ref, c, k):
    last = ref.shape[1] - 1

    def pair(offset):
        taps = [ref[c, k + o] for o in (-offset, offset) if not isinstance(k, int) or 0 <= k + o <= last]
        return taps[0] + taps[1] if len(taps) == 2 else taps[0]

    return 16.0 * pair(1) - pair(2) - 30.0 * ref[c, k]


def slot(p):
    return (p // 32) * LANES + (p % 32) * 4


def column_tables(planes):
    pack, unpack = np.zeros((2 * LANES, 2 * LANES)), np.zeros((2 * LANES, 2 * LANES))
    for p in range(planes):
        v0, v1, u0, u1 = (slot(p) + i for i in range(4))
        down, up = 2 * p, LANES + 2 * p
        pack[u0, down] = -1.0
        pack[u0, down + 1], pack[u1, down + 1] = 16.0, -1.0
        pack[v0, up], pack[v1, up] = -1.0, 16.0
        pack[v1, up + 1] = -1.0
        unpack[2 * p, slot(p) + 2] = unpack[2 * p + 1, slot(p) + 3] = 1.0
        unpack[LANES + 2 * p, slot(p)] = unpack[LANES + 2 * p + 1, slot(p) + 1] = 1.0
    return tuple(jnp.asarray(np.tile(t, (3, 1)), jnp.bfloat16) for t in (pack, unpack))


def pieces(x):
    a = x.astype(jnp.bfloat16)
    rest = x - a.astype(jnp.float32)
    b = rest.astype(jnp.bfloat16)
    c = (rest - b.astype(jnp.float32)).astype(jnp.bfloat16)
    return jnp.concatenate([a, b, c], axis=-1)


def times(x, table):
    return jnp.dot(pieces(x), table[...], preferred_element_type=jnp.float32)


def pack_all(uf, uc, pack, x_down, x_up, y_down, y_up, ready=None, ready_table=None):
    comps, layers, rows, cols = uf.shape
    crows, ccols = uc.shape[2:]
    raw = []
    for ref, at in ((uf, slice(0, cols)), (uc, slice(cols, cols + ccols))):
        n, width = ref.shape[2:]
        lane = lax.broadcasted_iota(jnp.int32, (n, LANES), 1)
        sub = lax.broadcasted_iota(jnp.int32, (8, width), 0)
        columns = [jnp.zeros((n, LANES), jnp.float32) for _ in range(2)]
        for g in range(0, layers, 4):
            if ready is not None:
                ready(ref is uc, g)
            for c in range(comps):
                first = last = jnp.zeros((8, width), jnp.float32)
                for i in range(4):
                    p = c * layers + g + i
                    u = ref[c, g + i, :, 0:LANES]
                    if width > LANES:
                        u = jnp.where(lane < 2, u, ref[c, g + i, :, width - LANES : width])
                    u = turn(u, slot(p) % LANES + 2, 1)
                    half = slot(p) // LANES
                    columns[half] = jnp.where(lane // 4 == slot(p) % LANES // 4, u, columns[half])
                    first = jnp.where(sub // 2 == i, turn(ref[c, g + i, 0:8, :], 2 * i, 0), first)
                    last = jnp.where(sub // 2 == i, turn(ref[c, g + i, n - 8 : n, :], 2 * i + 2, 0), last)
                tile = (c * layers + g) // 4
                x_down[tile, :, at] = jnp.where(lax.rem(sub, 2) == 1, 16.0 * turn(first, 1, 0), 0.0) - first
                x_up[tile, :, at] = jnp.where(lax.rem(sub, 2) == 0, 16.0 * turn(last, -1, 0), 0.0) - last
        raw.append(jnp.concatenate(columns, axis=1))
    if ready_table is not None:
        ready_table()
    packed = times(jnp.concatenate(raw, axis=0), pack)
    y_down[...] = packed[:, 0:LANES]
    y_up[...] = packed[:, LANES : 2 * LANES]


def load_kernel(uf_hbm, uc_hbm, pack_hbm, uf, uc, x_down, x_up, y_down, y_up, pack, sem):
    layers = uf.shape[1]
    copies = {}
    for coarse, src, dst in ((False, uf_hbm, uf), (True, uc_hbm, uc)):
        for g in range(0, layers, 4):
            at = pl.ds(g, 4)
            copies[coarse, g] = pltpu.make_async_copy(src.at[:, at], dst.at[:, at], sem.at[int(coarse), g // 4])
            copies[coarse, g].start()
    table = pltpu.make_async_copy(pack_hbm, pack, sem.at[2, 0])
    table.start()

    def ready(coarse, g):
        copies[coarse, g].wait()

    pack_all(uf, uc, pack, x_down, x_up, y_down, y_up, ready, table.wait)


def groups_do(total, size, body):
    body(0)
    if total > 2 * size:

        @pl.loop(1, total // size - 1)
        def _(g):
            body(g * size)

    body(total - size)


def main_kernel(first_step, uf, sp, me, uc, cs, tr, left_f, right_f, left_c, right_c, widen, narrow, *refs):
    comps, layers, rows, cols = uf.shape
    crows, ccols = uc.shape[2:]
    size_f, size_c = 256 // rows, 256 // crows
    if first_step:
        vf, vc, *prep, lat, tall = refs
    else:
        pf, pc, vf, vc, *prep, lat, tall = refs
    lat_c0 = prep[-1]

    def coarse(first):
        for c in range(comps):
            planes = uc[c, pl.ds(first, size_c)].reshape(256, ccols)
            part = lateral12(planes, left_c, right_c)
            if isinstance(first, int) and first == 0:
                lat_c0[c] = part[0:crows, :]
            for i in range(size_c):
                k = first + i
                old = 2.0 * uc[c, k] if first_step else 2.0 * uc[c, k] - pc[c, k]
                vc[c, k] = old + cs[k] * TWELFTH * (part[i * crows : (i + 1) * crows, :] + depth12(uc, c, k))

    def fine(first):
        for c in range(comps):
            planes = uf[c, pl.ds(first, size_f)].reshape(256, cols)
            lat[c] = lateral12(planes, left_f, right_f)
        for i in range(size_f):
            k = first + i
            s12, m2 = sp[k] * TWELFTH, me[k] * me[k]
            for c in range(comps):
                old = 2.0 * uf[c, k] if first_step else 2.0 * uf[c, k] - pf[c, k]
                vf[c, k] = old + s12 * (lat[c, i * rows : (i + 1) * rows, :] + m2 * depth12(uf, c, k))

    groups_do(layers, size_c, coarse)
    groups_do(layers, size_f, fine)
    prepare(uf, sp, me, uc, cs, tr, widen, narrow, lat, tall, *prep)


class Edges:
    def __init__(self, got, slots, shapes, unpack=None):
        self.got_xd, self.got_xu, got_yd, got_yu = got
        self.slots = slots
        (self.layers, rows, cols), (crows, ccols) = shapes
        self.fine = (slice(0, rows), slice(0, cols), rows, cols)
        self.coarse = (slice(rows, rows + crows), slice(cols, cols + ccols), crows, ccols)
        x_at, x_n = lax.axis_index("gx"), lax.axis_size("gx")
        y_at, y_n = lax.axis_index(Y), lax.axis_size(Y)
        self.x_low, self.x_high = x_at > 0, x_at < x_n - 1
        if unpack is None:
            return
        up = jnp.where(y_at > 0, got_yu[...], 0.0)
        down = jnp.where(y_at < y_n - 1, got_yd[...], 0.0)
        both = times(jnp.concatenate([up, down], axis=1), unpack)
        slots[0] = both[:, 0:LANES]
        slots[1] = both[:, LANES : 2 * LANES]

    def plane(self, grid, c, g, i):
        ys, xs, n, width = grid
        p = c * self.layers + g + i
        lane = lax.broadcasted_iota(jnp.int32, (n, LANES), 1)
        sub = lax.broadcasted_iota(jnp.int32, (8, width), 0)
        half, quad = (p // 32, p % 32) if isinstance(p, int) else (lax.div(p, 32), lax.rem(p, 32))
        u = pltpu.roll(self.slots[half, ys, :], LANES - 2 - 4 * quad, 1)
        low, high = jnp.where(lane < 2, u, 0.0), jnp.where(lane >= LANES - 2, u, 0.0)
        if width == LANES:
            columns = low + high
        else:
            columns = jnp.concatenate([low, high], axis=1)
        tile = p // 4 if isinstance(p, int) else lax.div(c * self.layers + g, 4)
        first = jnp.where(jnp.logical_and(sub < 2, self.x_low), turn(self.got_xu[tile, :, xs], -2 * i, 0), 0.0)
        last = jnp.where(jnp.logical_and(sub >= 6, self.x_high), turn(self.got_xd[tile, :, xs], 6 - 2 * i, 0), 0.0)
        return jnp.concatenate([columns[0:8] + first, columns[8 : n - 8], columns[n - 8 : n] + last], axis=0)


def stretch(planes, widen, tall, rows, cols):
    wide = times(jnp.concatenate(planes, axis=0), widen)
    n = len(planes) * rows // 2
    halves = range(cols // LANES)
    for half in halves:
        part = wide[:, half * LANES : (half + 1) * LANES]
        tall[half, pl.ds(0, n, 2), :] = part
        tall[half, pl.ds(1, n, 2), :] = part
    return [
        jnp.concatenate([tall[half, i * rows : (i + 1) * rows, :] for half in halves], axis=1)
        for i in range(len(planes))
    ]


def row_pairs(planes, tall):
    rows, cols = planes[0].shape
    n = len(planes) * rows // 2
    halves = range(cols // LANES)
    for i, plane in enumerate(planes):
        for half in halves:
            tall[half, i * rows : (i + 1) * rows, :] = plane[:, half * LANES : (half + 1) * LANES]
    return tuple(
        jnp.concatenate([tall[half, pl.ds(start, n, 2), :] for half in halves], axis=1) for start in range(2)
    )


def prepare(uf, sp, me, uc, cs, tr, widen, narrow, lat, tall, alpha_o, gain_o, metric_o, beta_o, first_o, sums_o, top_o, lat_c0):
    comps, layers, rows, cols = uf.shape
    b = layers - 1
    s, m = sp[b], me[b]
    m2 = m * m
    gain = 1.0 / (s * m2)
    inv_m2 = 1.0 / m2
    cs0 = cs[0]
    t = tr[...]
    c0 = [uc[c, 0] for c in range(comps)]
    pull = [
        cs0 * (lat_c0[c] - 29.0 * uc[c, 0] + 16.0 * uc[c, 1] - uc[c, 2]) * TWELFTH for c in range(comps)
    ]
    wide = stretch([cs0] + pull + c0, widen, tall, rows, cols)
    alpha = gain * wide[0]
    gain14 = gain * (12.0 / 14.0)
    alpha_o[...] = alpha
    gain_o[...] = gain14
    metric_o[...] = inv_m2 * (1.0 / 14.0)
    weighted = []
    for c in range(comps):
        ub, u1, u2 = uf[c, b], uf[c, b - 1], uf[c, b - 2]
        e = u2 - lat[c, 256 - rows : 256, :] * inv_m2 - 16.0 * u1 + 29.0 * ub
        bc = gain14 * wide[1 + c] + e * (1.0 / 14.0)
        beta_o[c] = bc
        first_o[c] = alpha * wide[1 + comps + c] - ub
        weighted.append(t * bc)
        weighted.append(t * (u2 - 8.0 * u1 + 7.0 * ub))
        weighted.append(t * (u2 - 8.0 * u1 + ub))
    even_rows, odd_rows = row_pairs([t * alpha] + weighted, tall)
    sums_o[...] = times(even_rows + odd_rows, narrow)
    even_rows, odd_rows = row_pairs([alpha], tall)
    top = jnp.maximum(even_rows, odd_rows)
    top = jnp.maximum(top, turn(top, -1, 1))
    lane = lax.broadcasted_iota(jnp.int32, top.shape, 1)
    top_o[...] = times(jnp.where(lax.rem(lane, 2) == 0, top, 0.0), narrow)


def interface(edges, uc, cs, tr, sh, widen, narrow, tall, alpha, gain14, metric14, beta_in, first_in, sums, top, lat_c0):
    comps, rows, cols = beta_in.shape
    crows, ccols = sh.shape
    layers = edges.layers
    inv_sh = 1.0 / sh[...]
    t = tr[...]
    pull = [cs[0] * TWELFTH * edges.plane(edges.coarse, c, 0, 0) for c in range(comps)]
    wide = stretch(pull, widen, tall, rows, cols)
    beta, weighted, first = [], [], None
    for c in range(comps):
        more = gain14[...] * wide[c] - metric14[...] * edges.plane(edges.fine, c, layers - 4, 3)
        bc = beta_in[c] + more
        beta.append(bc)
        weighted.append(t * more)
        change = jnp.max(jnp.abs(first_in[c] + bc), axis=0, keepdims=True)
        first = change if first is None else jnp.maximum(first, change)
    even_rows, odd_rows = row_pairs(weighted, tall)
    more = times(even_rows + odd_rows, narrow)

    def part(i):
        return sums[i * crows : (i + 1) * crows, :]

    rate = part(0) * (0.5 * inv_sh)
    history = [[], [], [], []]
    c3s, c4s = [], []
    for c in range(comps):
        c0 = uc[c, 0]
        q6 = (8.0 * uc[c, 1] - c0 - uc[c, 2]) * (1.0 / 6.0)
        pushed = part(1 + 3 * c) + more[c * crows : (c + 1) * crows, :]
        start, still = part(2 + 3 * c), part(3 + 3 * c)
        base = q6 - (still * TWELFTH + 0.5 * pushed) * inv_sh
        c1 = q6 - start * (TWELFTH * inv_sh)
        c2 = base - rate * c0
        c3 = base - rate * c1
        c4 = base - rate * c2
        d1, d2, d3, d4 = (jnp.abs(x) for x in (c1 - c0, c2 - c1, c3 - c2, c4 - c3))
        history[0].append(d1)
        history[1].append(jnp.maximum(d2, top[...] * d1))
        history[2].append(jnp.maximum(d3, top[...] * d2))
        history[3].append(jnp.maximum(d4, top[...] * d3))
        c3s.append(c3)
        c4s.append(c4)
    lane = lax.broadcasted_iota(jnp.int32, (1, LANES), 1)
    line = jnp.zeros((1, LANES), jnp.float32)
    for n in range(4):
        d = jnp.maximum(jnp.maximum(history[n][0], history[n][1]), history[n][2])
        d = jnp.max(d, axis=0, keepdims=True)
        if n == 0:
            for half in range(cols // LANES):
                d = jnp.maximum(d, first[:, half * LANES : (half + 1) * LANES])
        line = jnp.where(lane == n, jnp.max(d, axis=1, keepdims=True), line)
    wide = stretch(c3s, widen, tall, rows, cols)
    return [alpha[...] * wide[c] + beta[c] for c in range(comps)], c4s, line[:, 0:4]


PREP = 8


def fix_kernel(vf_in, vc_in, pack, unpack, uf, pf, sp, me, uc, pc, cs, tr, sh, widen, narrow, *refs):
    prep, got = refs[:PREP], refs[PREP : PREP + 4]
    vf, vc, change, *packed = refs[PREP + 4 : -2]
    tall, slots = refs[-2:]
    comps, layers, rows, cols = uf.shape
    edges = Edges(got, slots, (uf.shape[1:], uc.shape[2:]), unpack)
    ghost_f, ghost_c, line = interface(edges, uc, cs, tr, sh, widen, narrow, tall, *prep)
    change[...] = line
    b = layers - 1
    s_last = sp[b] * me[b] * me[b] * TWELFTH
    s_next = sp[b - 1] * me[b - 1] * me[b - 1] * TWELFTH
    for c in range(comps):
        vf[c, b] = vf_in[c, b] + s_last * (14.0 * ghost_f[c] + uf[c, b])
        vf[c, b - 1] = vf_in[c, b - 1] - s_next * ghost_f[c]
        vc[c, 0] = vc_in[c, 0] + cs[0] * TWELFTH * (14.0 * ghost_c[c] + uc[c, 0])
        vc[c, 1] = vc_in[c, 1] - cs[1] * TWELFTH * ghost_c[c]

    @pl.loop(0, layers // 4)
    def _(quarter):
        g = quarter * 4
        for i in range(4):
            s12, cs12 = sp[g + i] * TWELFTH, cs[g + i] * TWELFTH
            for c in range(comps):
                vf[c, g + i] = vf_in[c, g + i] - pf[c, g + i] + s12 * edges.plane(edges.fine, c, g, i)
                vc[c, g + i] = vc_in[c, g + i] - pc[c, g + i] + cs12 * edges.plane(edges.coarse, c, g, i)

    pack_all(vf, vc, pack, *packed)


def interface_kernel(unpack, uf, uc, cs, tr, sh, widen, narrow, *refs):
    prep, got = refs[:PREP], refs[PREP : PREP + 4]
    ghost_f, ghost_c, change, slots, tall = refs[PREP + 4 :]
    edges = Edges(got, slots, (uf.shape[1:], uc.shape[2:]), unpack)
    g, c4, line = interface(edges, uc, cs, tr, sh, widen, narrow, tall, *prep)
    for c in range(uf.shape[0]):
        ghost_f[c] = g[c]
        ghost_c[c] = c4[c]
    change[...] = line


def last_kernel(change0, change1, sp, me, cs, uf, uc, vf, vc, ghost_f, ghost_c, slots, *refs):
    got = refs[0:4]
    out_f, out_c, spread, done_f, done_c, sem = refs[4:]
    comps, layers, rows, cols = uf.shape
    b = layers - 1
    edges = Edges(got, slots, (uf.shape[1:], uc.shape[2:]))
    for step, line in enumerate((change0, change1)):
        spread[:, step : step + 1, :] = jnp.broadcast_to(line[...][None], (spread.shape[0], 1, spread.shape[2]))

    def copy(k):
        return pltpu.make_async_copy(done_f.at[:, k], out_f.at[:, k], sem.at[k])

    copy_coarse = pltpu.make_async_copy(done_c, out_c, sem.at[layers])

    def fine(k, g, i):
        s12 = sp[k] * TWELFTH
        for c in range(comps):
            total = edges.plane(edges.fine, c, g, i)
            if isinstance(k, int) and k == b:
                total = total + me[k] * me[k] * (14.0 * ghost_f[c] + uf[c, b])
            if isinstance(k, int) and k == b - 1:
                total = total - me[k] * me[k] * ghost_f[c]
            done_f[c, k] = vf[c, k] + s12 * total
        copy(k).start()

    @pl.loop(0, layers // 4 - 1)
    def _(quarter):
        for i in range(4):
            fine(quarter * 4 + i, quarter * 4, i)

    for i in range(4):
        fine(layers - 4 + i, layers - 4, i)

    @pl.loop(0, layers // 4)
    def _(quarter):
        g = quarter * 4
        for i in range(4):
            cs12 = cs[g + i] * TWELFTH
            for c in range(comps):
                done_c[c, g + i] = vc[c, g + i] + cs12 * edges.plane(edges.coarse, c, g, i)

    for c in range(comps):
        done_c[c, 0] = done_c[c, 0] + cs[0] * TWELFTH * (14.0 * ghost_c[c] + uc[c, 0])
        done_c[c, 1] = done_c[c, 1] - cs[1] * TWELFTH * ghost_c[c]
    copy_coarse.start()
    for k in range(layers):
        copy(k).wait()
    copy_coarse.wait()


def call(kernel, args, outs, scratch=(), alias={}, flops=0, hbm=()):
    spaces = [pltpu.HBM if i in hbm else pltpu.VMEM for i in range(len(args))]
    return pl.pallas_call(
        kernel,
        out_shape=tuple(outs),
        in_specs=[pl.BlockSpec(memory_space=s) for s in spaces],
        out_specs=tuple(pl.BlockSpec(memory_space=o.memory_space) for o in outs),
        scratch_shapes=list(scratch),
        input_output_aliases=alias,
        cost_estimate=pl.CostEstimate(flops=flops, bytes_accessed=flops, transcendentals=0),
        compiler_params=pltpu.CompilerParams(vmem_limit_bytes=VMEM_LIMIT),
    )(*[pltpu.with_memory_space_constraint(x, s) for x, s in zip(args, spaces)])


def exchange(parts):
    x_down, x_up, y_down, y_up = parts

    def ring(value, axis, by):
        n = lax.axis_size(axis)
        return lax.ppermute(value, axis, [(i, (i + by) % n) for i in range(n)])

    return (ring(x_down, "gx", -1), ring(x_up, "gx", 1), ring(y_down, Y, -1), ring(y_up, Y, 1))


def on_device(
    fine_field, fine_previous, fine_speed, fine_metric, coarse_field, coarse_previous, coarse_speed,
    fine_traction, coarse_shear,
):
    f32 = jnp.float32
    comps, layers, rows, cols = fine_field.shape
    crows, ccols = coarse_field.shape[2:]
    fine = pltpu.VMEM(fine_field.shape, f32)
    coarse = pltpu.VMEM(coarse_field.shape, f32)
    plane_f = pltpu.VMEM((comps, rows, cols), f32)
    plane_c = pltpu.VMEM((comps, crows, ccols), f32)
    line = pltpu.VMEM((1, 4), f32)
    corrections = pltpu.VMEM((2, rows + crows, LANES), f32)
    edge_outs = [
        pltpu.VMEM((comps * layers // 4, 8, cols + ccols), f32),
        pltpu.VMEM((comps * layers // 4, 8, cols + ccols), f32),
        pltpu.VMEM((rows + crows, LANES), f32),
        pltpu.VMEM((rows + crows, LANES), f32),
    ]
    tall = pltpu.VMEM((cols // LANES, 10 * rows, LANES), f32)
    prep_outs = [pltpu.VMEM((rows, cols), f32)] * 3 + [plane_f, plane_f]
    prep_outs += [pltpu.VMEM((10 * crows, ccols), f32), pltpu.VMEM((crows, ccols), f32), plane_c]
    picks = np.zeros((cols, ccols), np.float32)
    picks[np.arange(cols), np.arange(cols) // 2] = 1.0
    narrow = jnp.asarray(np.tile(picks, (3, 1)), jnp.bfloat16)
    widen = jnp.asarray(np.tile(picks.T, (3, 1)), jnp.bfloat16)
    tables = (*lateral_tables(rows, cols), *lateral_tables(crows, ccols), widen, narrow)
    pack, unpack = column_tables(comps * layers)
    lat = pltpu.VMEM((comps, 256, cols), f32)
    tr, sh = fine_traction, coarse_shear

    uf, uc, *mine = call(
        load_kernel, (fine_field, coarse_field, pack), [fine, coarse] + edge_outs,
        scratch=[pltpu.VMEM(pack.shape, pack.dtype), pltpu.SemaphoreType.DMA((3, layers // 4))], hbm=(0, 1, 2),
    )
    theirs = exchange(mine)
    sp, me, cs = fine_speed, fine_metric, coarse_speed
    vf, vc, *prep = call(
        functools.partial(main_kernel, True), (uf, sp, me, uc, cs, tr, *tables), [fine, coarse, *prep_outs],
        scratch=[lat, tall], flops=40_000_000,
    )
    vf, vc, change0, *mine = call(
        fix_kernel,
        (vf, vc, pack, unpack, uf, fine_previous, sp, me, uc, coarse_previous, cs, tr, sh, widen, narrow, *prep, *theirs),
        [fine, coarse, line] + edge_outs, scratch=[tall, corrections], alias={0: 0, 1: 1}, flops=20_000_000,
    )
    pf, pc, uf, uc = uf, uc, vf, vc
    theirs = exchange(mine)
    vf, vc, *prep = call(
        functools.partial(main_kernel, False), (uf, sp, me, uc, cs, tr, *tables, pf, pc), [fine, coarse, *prep_outs],
        scratch=[lat, tall], flops=40_000_000,
    )
    ghost_f, ghost_c, change1, slots = call(
        interface_kernel, (unpack, uf, uc, cs, tr, sh, widen, narrow, *prep, *theirs),
        [plane_f, plane_c, line, corrections], scratch=[tall], flops=10_000_000,
    )
    n = lax.axis_size(ALL)
    out_f, out_c, spread = call(
        last_kernel,
        (change0, change1, sp, me, cs, uf, uc, vf, vc, ghost_f, ghost_c, slots, *theirs),
        [pltpu.HBM(fine_field.shape, f32), pltpu.HBM(coarse_field.shape, f32), pltpu.VMEM((n, STEPS, 4), f32)],
        scratch=[fine, coarse, pltpu.SemaphoreType.DMA((layers + 1,))], flops=40_000_000,
    )
    return out_f, out_c, jnp.max(lax.all_to_all(spread, ALL, 0, 0, tiled=True), axis=0)


def solution(mesh):
    field = P(None, None, "gx", Y)
    layered = P(None, "gx", Y)
    plane = P("gx", Y)
    return jax.shard_map(
        on_device,
        mesh=mesh,
        in_specs=(field, field, layered, layered, field, field, layered, plane, plane),
        out_specs=(field, field, P()),
        check_vma=False,
    )
```

time: 51.9 us -> 46.9 us (0.904)
  blocking collectives: 0 us -> 11.1 us
  waiting for transfers between devices: 13.4 us -> 3.43 us
  Pallas kernels: 23.1 us -> 19.3 us
  starting transfers between devices: 13.6 us -> 11.3 us
    all_to_all x0 -> x1, blocking collectives: none -> 11.1 us  [on_device(): lax.all_to_all(spread, ALL, 0, 0, tiled=True)]
    ppermute x5 -> x0, waiting for transfers between devices: 9.71 us -> none  [on_device(): arrived = lax.ppermute(history, axis, pairs)]
    pallas_call x9 -> x6, Pallas kernels: 23.1 us -> 19.3 us  [call(): pl.pallas_call(kernel, out_shape=tuple(outs), in_specs=[pl.BlockSpec(memo...]
    ppermute x5 -> x0, starting transfers between devices: 1.72 us -> none  [on_device(): arrived = lax.ppermute(history, axis, pairs)]
    reduce_max x0 -> x1, other arithmetic: none -> 0.6 us  [on_device(): jnp.max(lax.all_to_all(spread, ALL, 0, 0, tiled=True), axis=0)]
    max x5 -> x0, other arithmetic: 0.59 us -> none  [on_device(): history = jnp.maximum(history, arrived)]
    ppermute x8, starting transfers between devices: 11.9 us -> 11.3 us  [ring(): return lax.ppermute(value, axis, [(i, (i + by) % n) for i in range(n)])]
  transfers between devices with their start and end apart: 13 -> 8, of which waited for: 6 -> 2; matrix products, arithmetic and copies ran while one was open for 0% -> 0% of each run, Pallas kernels for 30% -> 21%
where the time goes in v4:
time: 46.9 us; the launch traced here: 46.7 us
  Pallas kernels  19.3 us (41%)
  starting transfers between devices  11.3 us (24%)
  blocking collectives  11.1 us (24%)
  waiting for transfers between devices  3.43 us (7%)
  between operations  0.92 us (2%)
  other arithmetic  0.6 us (1%)
    pallas_call x6, Pallas kernels, call(): pl.pallas_call(kernel, out_shape=tuple(outs), in_specs=[pl.BlockSpec(memo...  19.3 us
    ppermute x8, starting transfers between devices, ring(): return lax.ppermute(value, axis, [(i, (i + by) % n) for i in range(n)])  11.3 us
    all_to_all x1, blocking collectives, on_device(): lax.all_to_all(spread, ALL, 0, 0, tiled=True)  11.1 us
    ppermute x8, waiting for transfers between devices, ring(): return lax.ppermute(value, axis, [(i, (i + by) % n) for i in range(n)])  3.43 us
  transfers between devices with their start and end apart: 8, of which 2 were waited for; matrix products, arithmetic and copies ran while one was open for 0% of the time, Pallas kernels for 21%

profile of v4, /device:TPU:0, one launch (start us, length us, event | category | flops | bytes accessed | tf_op | source)
XLA Modules:
  0.0 46.7 jit_solution(11972267945201057399)
XLA Ops:
  0.6 0.0 copy-start.4
  0.6 0.0 copy-start.5
  0.7 0.0 copy-start.13
  0.7 0.0 copy-start.9
  0.7 0.0 copy-start.10
  0.7 0.0 copy-start.11
  0.7 3.0 %shard_map.184 = (f32[3,16,64,256]{3,2,1,0:T(8,128)S(1)}, f32[3,16,32,128]{3,2,1,0:T(8,128)S(1)}, f32[12,8,384]{2,1,0:T(8,128)S(1)}, f32[12,8,384]{2,1,0:T(8,128...) custom-call(f32[3,16,64,256]{3,2,1,0:T(8,128)} %uf_hbm.1, f32[3,16,32,128]{3,2,1,0:T(8,128)} %uc_hbm.1, ...), custom_call_target="tpu_custom_call" | custom-call | tf_op jit(solution)/shard_map/pallas_call | solution.py:435
  3.7 2.5 %collective-permute-start = (f32[12,8,384]{2,1,0:T(8,128)S(1)}, f32[12,8,384]{2,1,0:T(8,128)S(1)}, u32[]{:S(2)}, u32[]{:S(2)}) collective-permute-start(f32[12,8,384]{2,1,0:T(8,128)S(1)} %get-tuple-element.55), channel_id=1, source_target_pairs={{0,12},{4,0},{8,4},{12,8},{1,13},{5,1},{9,5},{13,9},{2,14},{6,2},{... | collective-permute-start | bytes 442376 | tf_op jit(solution)/shard_map/ppermute | solution.py:452
  6.2 0.0 collective-permute-start.1
  6.2 4.5 %collective-permute-start.2 = (f32[96,128]{1,0:T(8,128)S(1)}, f32[96,128]{1,0:T(8,128)S(1)}, u32[]{:S(2)}, u32[]{:S(2)}) collective-permute-start(f32[96,128]{1,0:T(8,128)S(1)} %get-tuple-element.57), channel_id=1, source_target_pairs={{0,19},{1,0},{2,1},{3,2},{16,3},{17,16},{18,17},{19,18},{4,23},{5,... | collective-permute-start | bytes 147464 | tf_op jit(solution)/shard_map/ppermute | solution.py:452
  10.7 0.0 collective-permute-start.3
  10.8 0.0 copy-start.3
  10.8 0.0 copy-start.6
  10.8 0.0 copy-start.7
  10.8 0.0 copy-start.12
  10.8 0.0 copy-start.14
  10.9 4.9 %shard_map.185 = (f32[3,16,64,256]{3,2,1,0:T(8,128)S(1)}, f32[3,16,32,128]{3,2,1,0:T(8,128)S(1)}, f32[64,256]{1,0:T(8,128)S(1)}, f32[64,256]{1,0:T(8,128)S(1)}, ...) custom-call(f32[3,16,64,256]{3,2,1,0:T(8,128)S(1)} %get-tuple-elemen, ...), custom_call_target="tpu_custom_call" | custom-call | flops 40000000 | bytes 40000000 | tf_op jit(solution)/shard_map/pallas_call | solution.py:435
  15.8 0.0 collective-permute-done.2.refs_10_
  15.8 1.7 %collective-permute-done.3.refs_11_ = f32[96,128]{1,0:T(8,128)S(1)} collective-permute-done((f32[96,128]{1,0:T(8,128)S(1)}, f32[96,128]{1,0:T(8,128)S(1)}, u32[]{:S(2)}, u32[]{:S(2)}) %collective-permute-start.3) | collective-permute-done | bytes 49184 | tf_op jit(solution)/shard_map/ppermute | solution.py:452
  17.6 3.0 %shard_map.186 = (f32[3,16,64,256]{3,2,1,0:T(8,128)S(1)}, f32[3,16,32,128]{3,2,1,0:T(8,128)S(1)}, f32[1,4]{1,0:T(1,128)S(1)}, f32[12,8,384]{2,1,0:T(8,128)S(1)},...) custom-call(f32[3,16,64,256]{3,2,1,0:T(8,128)S(1)} %get-tuple-elemen, ...), custom_call_target="tpu_custom_call", output_to_operand_aliasing={{0}: (0, {}), {1}: (1, {})} | custom-call | flops 20000000 | bytes 20000000 | tf_op jit(solution)/shard_map/pallas_call | solution.py:435
  20.5 1.0 %collective-permute-start.4 = (f32[12,8,384]{2,1,0:T(8,128)S(1)}, f32[12,8,384]{2,1,0:T(8,128)S(1)}, u32[]{:S(2)}, u32[]{:S(2)}) collective-permute-start(f32[12,8,384]{2,1,0:T(8,128)S(1)} %get-tuple-element.70), channel_id=1, source_target_pairs={{0,12},{4,0},{8,4},{12,8},{1,13},{5,1},{9,5},{13,9},{2,14},{6,2},{... | collective-permute-start | bytes 442376 | tf_op jit(solution)/shard_map/ppermute | solution.py:452
  21.5 0.0 collective-permute-start.5
  21.5 3.3 %collective-permute-start.6 = (f32[96,128]{1,0:T(8,128)S(1)}, f32[96,128]{1,0:T(8,128)S(1)}, u32[]{:S(2)}, u32[]{:S(2)}) collective-permute-start(f32[96,128]{1,0:T(8,128)S(1)} %get-tuple-element.72), channel_id=1, source_target_pairs={{0,19},{1,0},{2,1},{3,2},{16,3},{17,16},{18,17},{19,18},{4,23},{5,... | collective-permute-start | bytes 147464 | tf_op jit(solution)/shard_map/ppermute | solution.py:452
  24.8 0.0 collective-permute-start.7
  24.8 5.1 %shard_map.187 = (f32[3,16,64,256]{3,2,1,0:T(8,128)S(1)}, f32[3,16,32,128]{3,2,1,0:T(8,128)S(1)}, f32[64,256]{1,0:T(8,128)S(1)}, f32[64,256]{1,0:T(8,128)S(1)}, ...) custom-call(f32[3,16,64,256]{3,2,1,0:T(8,128)S(1)} %get-tuple-elemen, ...), custom_call_target="tpu_custom_call" | custom-call | flops 40000000 | bytes 40000000 | tf_op jit(solution)/shard_map/pallas_call | solution.py:435
  29.9 0.0 collective-permute-done.6.refs_10_.refs_2_
  29.9 1.7 %collective-permute-done.7.refs_11_.refs_3_ = f32[96,128]{1,0:T(8,128)S(1)} collective-permute-done((f32[96,128]{1,0:T(8,128)S(1)}, f32[96,128]{1,0:T(8,128)S(1)}, u32[]{:S(2)}, u32[]{:S(2)}) %collective-permute-start.7) | collective-permute-done | bytes 49184 | tf_op jit(solution)/shard_map/ppermute | solution.py:452
  31.6 0.0 collective-permute-done.5.refs_9_.refs_1_
  31.6 0.8 %shard_map.188 = (f32[3,64,256]{2,1,0:T(8,128)S(1)}, f32[3,32,128]{2,1,0:T(8,128)S(1)}, f32[1,4]{1,0:T(1,128)S(1)}, f32[2,96,128]{2,1,0:T(8,128)S(1)}) custom-call(bf16[768,256]{1,0:T(8,128)(2,1)S(1)} %copy-done.6, f32[3,16,64,256]{3,2,1,0:T(8,128)S(1)} %get-tuple-element.60.uf, f32[3,16,32,128]{3,2,1,0:T(8,128)S(1)} %get-tuple-element.61.uc, ...), custom_call_target="tpu_custom_call" | custom-call | flops 10000000 | bytes 10000000 | tf_op jit(solution)/shard_map/pallas_call | solution.py:435
  32.5 2.5 %shard_map.189 = (f32[3,16,64,256]{3,2,1,0:T(8,128)}, f32[3,16,32,128]{3,2,1,0:T(8,128)}, f32[32,2,4]{2,1,0:T(2,128)S(1)}) custom-call(f32[1,4]{1,0:T(1,128)S(1)} %get-tuple-element.59.change0, f32[1,4]{1,0:T(1,128)S(1)} %get-tuple-element.74.change1, f32[16,64,256]{2,1,0:T(8,128)S(1)} %copy-done, f32[16,64,256]{2,1,0:T(8,128)S(1)} %copy-done.1, ...), custom_call_target="tpu_custom_call" | custom-call | flops 40000000 | bytes 40000000 | tf_op jit(solution)/shard_map/pallas_call | solution.py:435
  35.0 11.1 %all_to_all.5 = f32[32,2,4]{2,1,0:T(2,128)S(1)} all-to-all(f32[32,2,4]{2,1,0:T(2,128)S(1)} %get-tuple-element.82), channel_id=1, replica_groups=mesh['grid'=2,'gx'=4,'gy'=4] {'grid','gx','gy'}, dimensions={0} | all-to-all | bytes 2048 | tf_op jit(solution)/shard_map/all_to_all | solution.py:520
  46.1 0.6 %reduce_max.9 = f32[2,4]{1,0:T(2,128)} reduce(f32[32,2,4]{2,1,0:T(2,128)S(1)} %all_to_all.5, f32[]{:T(128)} %constant.8.clone.1), dimensions={0}, to_apply=%region_0.0 | reduce | flops 248 | bytes 1060 | tf_op jit(solution)/shard_map/reduce_max | solution.py:520
  (22 shorter events, 0.0 us)
Async XLA Ops:
  0.6 10.1 %copy-start.4 = (bf16[384,256]{1,0:T(8,128)(2,1)S(1)}, bf16[384,256]{1,0:T(8,128)(2,1)}, u32[]{:S(2)}) copy-start(bf16[384,256]{1,0:T(8,128)(2,1)} %constant.19.clone.widen) | copy-start | bytes 589828
  0.6 10.1 %copy-start.5 = (bf16[768,128]{1,0:T(8,128)(2,1)S(1)}, bf16[768,128]{1,0:T(8,128)(2,1)}, u32[]{:S(2)}) copy-start(bf16[768,128]{1,0:T(8,128)(2,1)} %constant.18.clone.narrow) | copy-start | bytes 589828
  0.7 10.1 %copy-start.13 = (bf16[256,128]{1,0:T(8,128)(2,1)S(1)}, bf16[256,128]{1,0:T(8,128)(2,1)}, u32[]{:S(2)}) copy-start(bf16[256,128]{1,0:T(8,128)(2,1)} %constant.23.clone.right_c) | copy-start | bytes 196612
  0.7 10.1 %copy-start.9 = (bf16[256,512]{1,0:T(8,128)(2,1)S(1)}, bf16[256,512]{1,0:T(8,128)(2,1)}, u32[]{:S(2)}) copy-start(bf16[256,512]{1,0:T(8,128)(2,1)} %constant.22.clone.left_c) | copy-start | bytes 786436
  0.7 10.0 %copy-start.10 = (bf16[512,256]{1,0:T(8,128)(2,1)S(1)}, bf16[512,256]{1,0:T(8,128)(2,1)}, u32[]{:S(2)}) copy-start(bf16[512,256]{1,0:T(8,128)(2,1)} %constant.21.clone.right_f) | copy-start | bytes 786436
  0.7 10.0 %copy-start.11 = (bf16[256,512]{1,0:T(8,128)(2,1)S(1)}, bf16[256,512]{1,0:T(8,128)(2,1)}, u32[]{:S(2)}) copy-start(bf16[256,512]{1,0:T(8,128)(2,1)} %constant.20.clone.left_f) | copy-start | bytes 786436
  0.7 10.0 %copy-start.2 = (f32[16,32,128]{2,1,0:T(8,128)S(1)}, f32[16,32,128]{2,1,0:T(8,128)}, u32[]{:S(2)}) copy-start(f32[16,32,128]{2,1,0:T(8,128)} %cs.9) | copy-start | bytes 786436
  0.7 10.0 %copy-start.8 = (f32[64,256]{1,0:T(8,128)S(1)}, f32[64,256]{1,0:T(8,128)}, u32[]{:S(2)}) copy-start(f32[64,256]{1,0:T(8,128)} %tr.7) | copy-start | bytes 196612
  0.7 10.0 %copy-start.1 = (f32[16,64,256]{2,1,0:T(8,128)S(1)}, f32[16,64,256]{2,1,0:T(8,128)}, u32[]{:S(2)}) copy-start(f32[16,64,256]{2,1,0:T(8,128)} %me.7) | copy-start | bytes 3145732
  0.7 10.0 %copy-start = (f32[16,64,256]{2,1,0:T(8,128)S(1)}, f32[16,64,256]{2,1,0:T(8,128)}, u32[]{:S(2)}) copy-start(f32[16,64,256]{2,1,0:T(8,128)} %sp.7) | copy-start | bytes 3145732
  3.7 13.8 %collective-permute-start = (f32[12,8,384]{2,1,0:T(8,128)S(1)}, f32[12,8,384]{2,1,0:T(8,128)S(1)}, u32[]{:S(2)}, u32[]{:S(2)}) collective-permute-start(f32[12,8,384]{2,1,0:T(8,128)S(1)} %get-tuple-element.55), channel_id=1, source_target_pairs={{0,12},{4,0},{8,4},{12,8},{1,13},{5,1},{9,5},{13,9},{2,14},{6,2},{... | collective-permute-start | bytes 442376 | tf_op jit(solution)/shard_map/ppermute | solution.py:452
  6.2 11.3 %collective-permute-start.1 = (f32[12,8,384]{2,1,0:T(8,128)S(1)}, f32[12,8,384]{2,1,0:T(8,128)S(1)}, u32[]{:S(2)}, u32[]{:S(2)}) collective-permute-start(f32[12,8,384]{2,1,0:T(8,128)S(1)} %get-tuple-element.56), channel_id=1, source_target_pairs={{0,4},{4,8},{8,12},{12,0},{1,5},{5,9},{9,13},{13,1},{2,6},{6,10},{... | collective-permute-start | bytes 442376 | tf_op jit(solution)/shard_map/ppermute | solution.py:452
  6.2 9.6 %collective-permute-start.2 = (f32[96,128]{1,0:T(8,128)S(1)}, f32[96,128]{1,0:T(8,128)S(1)}, u32[]{:S(2)}, u32[]{:S(2)}) collective-permute-start(f32[96,128]{1,0:T(8,128)S(1)} %get-tuple-element.57), channel_id=1, source_target_pairs={{0,19},{1,0},{2,1},{3,2},{16,3},{17,16},{18,17},{19,18},{4,23},{5,... | collective-permute-start | bytes 147464 | tf_op jit(solution)/shard_map/ppermute | solution.py:452
  10.7 6.8 %collective-permute-start.3 = (f32[96,128]{1,0:T(8,128)S(1)}, f32[96,128]{1,0:T(8,128)S(1)}, u32[]{:S(2)}, u32[]{:S(2)}) collective-permute-start(f32[96,128]{1,0:T(8,128)S(1)} %get-tuple-element.58), channel_id=1, source_target_pairs={{0,1},{1,2},{2,3},{3,16},{16,17},{17,18},{18,19},{19,0},{4,5},{5,6... | collective-permute-start | bytes 147464 | tf_op jit(solution)/shard_map/ppermute | solution.py:452
  10.8 6.7 %copy-start.3 = (f32[3,16,64,256]{3,2,1,0:T(8,128)S(1)}, f32[3,16,64,256]{3,2,1,0:T(8,128)}, u32[]{:S(2)}) copy-start(f32[3,16,64,256]{3,2,1,0:T(8,128)} %pf.1) | copy-start | bytes 9437188
  10.8 6.7 %copy-start.6 = (bf16[768,256]{1,0:T(8,128)(2,1)S(1)}, bf16[768,256]{1,0:T(8,128)(2,1)}, u32[]{:S(2)}) copy-start(bf16[768,256]{1,0:T(8,128)(2,1)} %constant.25.clone.unpack) | copy-start | bytes 1179652
  10.8 6.7 %copy-start.7 = (bf16[768,256]{1,0:T(8,128)(2,1)S(1)}, bf16[768,256]{1,0:T(8,128)(2,1)}, u32[]{:S(2)}) copy-start(bf16[768,256]{1,0:T(8,128)(2,1)} %constant.24.clone.pack_hbm.pack) | copy-start | bytes 1179652
  10.8 6.7 %copy-start.12 = (f32[3,16,32,128]{3,2,1,0:T(8,128)S(1)}, f32[3,16,32,128]{3,2,1,0:T(8,128)}, u32[]{:S(2)}) copy-start(f32[3,16,32,128]{3,2,1,0:T(8,128)} %pc.1) | copy-start | bytes 2359300
  10.8 6.7 %copy-start.14 = (f32[32,128]{1,0:T(8,128)S(1)}, f32[32,128]{1,0:T(8,128)}, u32[]{:S(2)}) copy-start(f32[32,128]{1,0:T(8,128)} %sh.3) | copy-start | bytes 49156
  20.5 11.1 %collective-permute-start.4 = (f32[12,8,384]{2,1,0:T(8,128)S(1)}, f32[12,8,384]{2,1,0:T(8,128)S(1)}, u32[]{:S(2)}, u32[]{:S(2)}) collective-permute-start(f32[12,8,384]{2,1,0:T(8,128)S(1)} %get-tuple-element.70), channel_id=1, source_target_pairs={{0,12},{4,0},{8,4},{12,8},{1,13},{5,1},{9,5},{13,9},{2,14},{6,2},{... | collective-permute-start | bytes 442376 | tf_op jit(solution)/shard_map/ppermute | solution.py:452
  21.5 10.1 %collective-permute-start.5 = (f32[12,8,384]{2,1,0:T(8,128)S(1)}, f32[12,8,384]{2,1,0:T(8,128)S(1)}, u32[]{:S(2)}, u32[]{:S(2)}) collective-permute-start(f32[12,8,384]{2,1,0:T(8,128)S(1)} %get-tuple-element.71), channel_id=1, source_target_pairs={{0,4},{4,8},{8,12},{12,0},{1,5},{5,9},{9,13},{13,1},{2,6},{6,10},{... | collective-permute-start | bytes 442376 | tf_op jit(solution)/shard_map/ppermute | solution.py:452
  21.5 8.4 %collective-permute-start.6 = (f32[96,128]{1,0:T(8,128)S(1)}, f32[96,128]{1,0:T(8,128)S(1)}, u32[]{:S(2)}, u32[]{:S(2)}) collective-permute-start(f32[96,128]{1,0:T(8,128)S(1)} %get-tuple-element.72), channel_id=1, source_target_pairs={{0,19},{1,0},{2,1},{3,2},{16,3},{17,16},{18,17},{19,18},{4,23},{5,... | collective-permute-start | bytes 147464 | tf_op jit(solution)/shard_map/ppermute | solution.py:452
  24.8 6.8 %collective-permute-start.7 = (f32[96,128]{1,0:T(8,128)S(1)}, f32[96,128]{1,0:T(8,128)S(1)}, u32[]{:S(2)}, u32[]{:S(2)}) collective-permute-start(f32[96,128]{1,0:T(8,128)S(1)} %get-tuple-element.73), channel_id=1, source_target_pairs={{0,1},{1,2},{2,3},{3,16},{16,17},{17,18},{18,19},{19,0},{4,5},{5,6... | collective-permute-start | bytes 147464 | tf_op jit(solution)/shard_map/ppermute | solution.py:452

commit v5 on v4

--- a/solution.py
+++ b/solution.py
@@ -134,52 +134,51 @@
     pack_all(uf, uc, pack, x_down, x_up, y_down, y_up, ready, table.wait)
 
 
-def groups_do(total, size, body):
-    body(0)
-    if total > 2 * size:
-
-        @pl.loop(1, total // size - 1)
-        def _(g):
-            body(g * size)
-
-    body(total - size)
-
-
 def main_kernel(first_step, uf, sp, me, uc, cs, tr, left_f, right_f, left_c, right_c, widen, narrow, *refs):
     comps, layers, rows, cols = uf.shape
     crows, ccols = uc.shape[2:]
     size_f, size_c = 256 // rows, 256 // crows
     if first_step:
-        vf, vc, *prep, lat, tall = refs
+        vf, vc, *fixed, beta, first, sums, lat_c0, lat, tall = refs
     else:
-        pf, pc, vf, vc, *prep, lat, tall = refs
-    lat_c0 = prep[-1]
-
-    def coarse(first):
+        *fixed, pf, pc, vf, vc, beta, first, sums, lat_c0, lat, tall = refs
+
+    def coarse(start):
         for c in range(comps):
-            planes = uc[c, pl.ds(first, size_c)].reshape(256, ccols)
+            planes = uc[c, start : start + size_c].reshape(256, ccols)
             part = lateral12(planes, left_c, right_c)
-            if isinstance(first, int) and first == 0:
+            if start == 0:
                 lat_c0[c] = part[0:crows, :]
             for i in range(size_c):
-                k = first + i
+                k = start + i
                 old = 2.0 * uc[c, k] if first_step else 2.0 * uc[c, k] - pc[c, k]
                 vc[c, k] = old + cs[k] * TWELFTH * (part[i * crows : (i + 1) * crows, :] + depth12(uc, c, k))
 
-    def fine(first):
+    def fine_lateral(start):
         for c in range(comps):
-            planes = uf[c, pl.ds(first, size_f)].reshape(256, cols)
-            lat[c] = lateral12(planes, left_f, right_f)
+            planes = uf[c, start : start + size_f].reshape(256, cols)
+            lat[start // size_f % 2, c] = lateral12(planes, left_f, right_f)
+
+    def fine(start):
         for i in range(size_f):
-            k = first + i
+            k = start + i
             s12, m2 = sp[k] * TWELFTH, me[k] * me[k]
             for c in range(comps):
                 old = 2.0 * uf[c, k] if first_step else 2.0 * uf[c, k] - pf[c, k]
-                vf[c, k] = old + s12 * (lat[c, i * rows : (i + 1) * rows, :] + m2 * depth12(uf, c, k))
-
-    groups_do(layers, size_c, coarse)
-    groups_do(layers, size_f, fine)
-    prepare(uf, sp, me, uc, cs, tr, widen, narrow, lat, tall, *prep)
+                side = lat[start // size_f % 2, c, i * rows : (i + 1) * rows, :]
+                vf[c, k] = old + s12 * (side + m2 * depth12(uf, c, k))
+
+    fine_lateral(0)
+    for start in range(0, layers, size_f):
+        if start + size_f < layers:
+            fine_lateral(start + size_f)
+        fine(start)
+    if first_step:
+        prepare_fixed(sp, me, cs, tr, widen, narrow, tall, *fixed)
+    lat_b = lat.at[(layers - 1) // size_f % 2, :, 256 - rows : 256]
+    for start in range(0, layers, size_c):
+        coarse(start)
+    prepare(uf, uc, cs, tr, widen, narrow, lat_b, tall, *fixed, beta, first, sums, lat_c0)
 
 
 class Edges:
@@ -244,45 +243,50 @@
     )
 
 
-def prepare(uf, sp, me, uc, cs, tr, widen, narrow, lat, tall, alpha_o, gain_o, metric_o, beta_o, first_o, sums_o, top_o, lat_c0):
-    comps, layers, rows, cols = uf.shape
-    b = layers - 1
+def prepare_fixed(sp, me, cs, tr, widen, narrow, tall, alpha_o, gain_o, metric_o, rate_o, top_o):
+    rows, cols = tr.shape
+    b = sp.shape[0] - 1
     s, m = sp[b], me[b]
     m2 = m * m
     gain = 1.0 / (s * m2)
-    inv_m2 = 1.0 / m2
-    cs0 = cs[0]
+    alpha = gain * stretch([cs[0]], widen, tall, rows, cols)[0]
+    alpha_o[...] = alpha
+    gain_o[...] = gain * (12.0 / 14.0)
+    metric_o[...] = (1.0 / 14.0) / m2
+    even_rows, odd_rows = row_pairs([tr[...] * alpha, alpha], tall)
+    crows = rows // 2
+    top = jnp.maximum(even_rows[crows:], odd_rows[crows:])
+    top = jnp.maximum(top, turn(top, -1, 1))
+    lane = lax.broadcasted_iota(jnp.int32, top.shape, 1)
+    top = jnp.where(lax.rem(lane, 2) == 0, top, 0.0)
+    both = times(jnp.concatenate([even_rows[:crows] + odd_rows[:crows], top], axis=0), narrow)
+    rate_o[...] = both[:crows]
+    top_o[...] = both[crows:]
+
+
+def prepare(uf, uc, cs, tr, widen, narrow, lat_b, tall, alpha, gain14, metric14, rate, top, beta_o, first_o, sums_o, lat_c0):
+    comps, layers, rows, cols = uf.shape
+    b = layers - 1
     t = tr[...]
     c0 = [uc[c, 0] for c in range(comps)]
     pull = [
-        cs0 * (lat_c0[c] - 29.0 * uc[c, 0] + 16.0 * uc[c, 1] - uc[c, 2]) * TWELFTH for c in range(comps)
+        cs[0] * (lat_c0[c] - 29.0 * uc[c, 0] + 16.0 * uc[c, 1] - uc[c, 2]) * TWELFTH for c in range(comps)
     ]
-    wide = stretch([cs0] + pull + c0, widen, tall, rows, cols)
-    alpha = gain * wide[0]
-    gain14 = gain * (12.0 / 14.0)
-    alpha_o[...] = alpha
-    gain_o[...] = gain14
-    metric_o[...] = inv_m2 * (1.0 / 14.0)
+    wide = stretch(pull + c0, widen, tall, rows, cols)
     weighted = []
     for c in range(comps):
         ub, u1, u2 = uf[c, b], uf[c, b - 1], uf[c, b - 2]
-        e = u2 - lat[c, 256 - rows : 256, :] * inv_m2 - 16.0 * u1 + 29.0 * ub
-        bc = gain14 * wide[1 + c] + e * (1.0 / 14.0)
+        bc = gain14[...] * wide[c] - metric14[...] * lat_b[c] + (u2 - 16.0 * u1 + 29.0 * ub) * (1.0 / 14.0)
         beta_o[c] = bc
-        first_o[c] = alpha * wide[1 + comps + c] - ub
-        weighted.append(t * bc)
-        weighted.append(t * (u2 - 8.0 * u1 + 7.0 * ub))
-        weighted.append(t * (u2 - 8.0 * u1 + ub))
-    even_rows, odd_rows = row_pairs([t * alpha] + weighted, tall)
+        first_o[c] = alpha[...] * wide[comps + c] - ub
+        still = (u2 - 8.0 * u1 + ub) * TWELFTH
+        weighted.append(t * (still + 0.5 * bc))
+        weighted.append(t * (still + 0.5 * ub))
+    even_rows, odd_rows = row_pairs(weighted, tall)
     sums_o[...] = times(even_rows + odd_rows, narrow)
-    even_rows, odd_rows = row_pairs([alpha], tall)
-    top = jnp.maximum(even_rows, odd_rows)
-    top = jnp.maximum(top, turn(top, -1, 1))
-    lane = lax.broadcasted_iota(jnp.int32, top.shape, 1)
-    top_o[...] = times(jnp.where(lax.rem(lane, 2) == 0, top, 0.0), narrow)
-
-
-def interface(edges, uc, cs, tr, sh, widen, narrow, tall, alpha, gain14, metric14, beta_in, first_in, sums, top, lat_c0):
+
+
+def interface(edges, uc, cs, tr, sh, widen, narrow, tall, alpha, gain14, metric14, rate_in, top, beta_in, first_in, sums):
     comps, rows, cols = beta_in.shape
     crows, ccols = sh.shape
     layers = edges.layers
@@ -295,7 +299,7 @@
         more = gain14[...] * wide[c] - metric14[...] * edges.plane(edges.fine, c, layers - 4, 3)
         bc = beta_in[c] + more
         beta.append(bc)
-        weighted.append(t * more)
+        weighted.append(0.5 * t * more)
         change = jnp.max(jnp.abs(first_in[c] + bc), axis=0, keepdims=True)
         first = change if first is None else jnp.maximum(first, change)
     even_rows, odd_rows = row_pairs(weighted, tall)
@@ -304,16 +308,14 @@
     def part(i):
         return sums[i * crows : (i + 1) * crows, :]
 
-    rate = part(0) * (0.5 * inv_sh)
+    rate = rate_in[...] * (0.5 * inv_sh)
     history = [[], [], [], []]
     c3s, c4s = [], []
     for c in range(comps):
         c0 = uc[c, 0]
         q6 = (8.0 * uc[c, 1] - c0 - uc[c, 2]) * (1.0 / 6.0)
-        pushed = part(1 + 3 * c) + more[c * crows : (c + 1) * crows, :]
-        start, still = part(2 + 3 * c), part(3 + 3 * c)
-        base = q6 - (still * TWELFTH + 0.5 * pushed) * inv_sh
-        c1 = q6 - start * (TWELFTH * inv_sh)
+        base = q6 - (part(2 * c) + more[c * crows : (c + 1) * crows, :]) * inv_sh
+        c1 = q6 - part(2 * c + 1) * inv_sh
         c2 = base - rate * c0
         c3 = base - rate * c1
         c4 = base - rate * c2
@@ -357,9 +359,7 @@
         vc[c, 0] = vc_in[c, 0] + cs[0] * TWELFTH * (14.0 * ghost_c[c] + uc[c, 0])
         vc[c, 1] = vc_in[c, 1] - cs[1] * TWELFTH * ghost_c[c]
 
-    @pl.loop(0, layers // 4)
-    def _(quarter):
-        g = quarter * 4
+    for g in range(0, layers, 4):
         for i in range(4):
             s12, cs12 = sp[g + i] * TWELFTH, cs[g + i] * TWELFTH
             for c in range(comps):
@@ -405,17 +405,10 @@
             done_f[c, k] = vf[c, k] + s12 * total
         copy(k).start()
 
-    @pl.loop(0, layers // 4 - 1)
-    def _(quarter):
-        for i in range(4):
-            fine(quarter * 4 + i, quarter * 4, i)
-
-    for i in range(4):
-        fine(layers - 4 + i, layers - 4, i)
-
-    @pl.loop(0, layers // 4)
-    def _(quarter):
-        g = quarter * 4
+    for k in range(layers):
+        fine(k, k // 4 * 4, k % 4)
+
+    for g in range(0, layers, 4):
         for i in range(4):
             cs12 = cs[g + i] * TWELFTH
             for c in range(comps):
@@ -473,16 +466,17 @@
         pltpu.VMEM((rows + crows, LANES), f32),
         pltpu.VMEM((rows + crows, LANES), f32),
     ]
-    tall = pltpu.VMEM((cols // LANES, 10 * rows, LANES), f32)
-    prep_outs = [pltpu.VMEM((rows, cols), f32)] * 3 + [plane_f, plane_f]
-    prep_outs += [pltpu.VMEM((10 * crows, ccols), f32), pltpu.VMEM((crows, ccols), f32), plane_c]
+    tall = pltpu.VMEM((cols // LANES, 2 * comps * rows, LANES), f32)
+    one_c = pltpu.VMEM((crows, ccols), f32)
+    fixed_outs = [pltpu.VMEM((rows, cols), f32)] * 3 + [one_c, one_c]
+    prep_outs = [plane_f, plane_f, pltpu.VMEM((2 * comps * crows, ccols), f32), plane_c]
     picks = np.zeros((cols, ccols), np.float32)
     picks[np.arange(cols), np.arange(cols) // 2] = 1.0
     narrow = jnp.asarray(np.tile(picks, (3, 1)), jnp.bfloat16)
     widen = jnp.asarray(np.tile(picks.T, (3, 1)), jnp.bfloat16)
     tables = (*lateral_tables(rows, cols), *lateral_tables(crows, ccols), widen, narrow)
     pack, unpack = column_tables(comps * layers)
-    lat = pltpu.VMEM((comps, 256, cols), f32)
+    lat = pltpu.VMEM((2, comps, 256, cols), f32)
     tr, sh = fine_traction, coarse_shear
 
     uf, uc, *mine = call(
@@ -492,22 +486,23 @@
     theirs = exchange(mine)
     sp, me, cs = fine_speed, fine_metric, coarse_speed
     vf, vc, *prep = call(
-        functools.partial(main_kernel, True), (uf, sp, me, uc, cs, tr, *tables), [fine, coarse, *prep_outs],
+        functools.partial(main_kernel, True), (uf, sp, me, uc, cs, tr, *tables), [fine, coarse, *fixed_outs, *prep_outs],
         scratch=[lat, tall], flops=40_000_000,
     )
     vf, vc, change0, *mine = call(
         fix_kernel,
-        (vf, vc, pack, unpack, uf, fine_previous, sp, me, uc, coarse_previous, cs, tr, sh, widen, narrow, *prep, *theirs),
+        (vf, vc, pack, unpack, uf, fine_previous, sp, me, uc, coarse_previous, cs, tr, sh, widen, narrow, *prep[:-1], *theirs),
         [fine, coarse, line] + edge_outs, scratch=[tall, corrections], alias={0: 0, 1: 1}, flops=20_000_000,
     )
-    pf, pc, uf, uc = uf, uc, vf, vc
+    pf, pc, uf, uc, fixed = uf, uc, vf, vc, prep[: len(fixed_outs)]
     theirs = exchange(mine)
     vf, vc, *prep = call(
-        functools.partial(main_kernel, False), (uf, sp, me, uc, cs, tr, *tables, pf, pc), [fine, coarse, *prep_outs],
+        functools.partial(main_kernel, False), (uf, sp, me, uc, cs, tr, *tables, *fixed, pf, pc),
+        [fine, coarse, *prep_outs],
         scratch=[lat, tall], flops=40_000_000,
     )
     ghost_f, ghost_c, change1, slots = call(
-        interface_kernel, (unpack, uf, uc, cs, tr, sh, widen, narrow, *prep, *theirs),
+        interface_kernel, (unpack, uf, uc, cs, tr, sh, widen, narrow, *fixed, *prep[:-1], *theirs),
         [plane_f, plane_c, line, corrections], scratch=[tall], flops=10_000_000,
     )
     n = lax.axis_size(ALL)

time: 46.9 us -> 46.5 us (level)
  transfers between devices with their start and end apart: 8 -> 8, of which waited for: 2 -> 2; matrix products, arithmetic and copies ran while one was open for 0% -> 0% of each run, Pallas kernels for 21% -> 22%
where the time goes in v5:
time: 46.5 us; the launch traced here: 46.3 us
  Pallas kernels  18.9 us (41%)
  starting transfers between devices  11.4 us (25%)
  blocking collectives  11.1 us (24%)
  waiting for transfers between devices  3.35 us (7%)
  between operations  0.89 us (2%)
  other arithmetic  0.6 us (1%)
    pallas_call x6, Pallas kernels, call(): pl.pallas_call(kernel, out_shape=tuple(outs), in_specs=[pl.BlockSpec(memo...  18.9 us
    ppermute x8, starting transfers between devices, ring(): return lax.ppermute(value, axis, [(i, (i + by) % n) for i in range(n)])  11.4 us
    all_to_all x1, blocking collectives, on_device(): lax.all_to_all(spread, ALL, 0, 0, tiled=True)  11.1 us
    ppermute x8, waiting for transfers between devices, ring(): return lax.ppermute(value, axis, [(i, (i + by) % n) for i in range(n)])  3.35 us
  transfers between devices with their start and end apart: 8, of which 2 were waited for; matrix products, arithmetic and copies ran while one was open for 0% of the time, Pallas kernels for 22%

profile of v5, /device:TPU:0, one launch (start us, length us, event | category | flops | bytes accessed | tf_op | source)
XLA Modules:
  0.0 46.3 jit_solution(16227510112134469334)
XLA Ops:
  0.6 0.0 copy-start.4
  0.6 0.0 copy-start.5
  0.7 0.0 copy-start.13
  0.7 0.0 copy-start.9
  0.7 0.0 copy-start.10
  0.7 0.0 copy-start.11
  0.7 3.0 %shard_map.184 = (f32[3,16,64,256]{3,2,1,0:T(8,128)S(1)}, f32[3,16,32,128]{3,2,1,0:T(8,128)S(1)}, f32[12,8,384]{2,1,0:T(8,128)S(1)}, f32[12,8,384]{2,1,0:T(8,128...) custom-call(f32[3,16,64,256]{3,2,1,0:T(8,128)} %uf_hbm.1, f32[3,16,32,128]{3,2,1,0:T(8,128)} %uc_hbm.1, ...), custom_call_target="tpu_custom_call" | custom-call | tf_op jit(solution)/shard_map/pallas_call | solution.py:428
  3.7 2.5 %collective-permute-start = (f32[12,8,384]{2,1,0:T(8,128)S(1)}, f32[12,8,384]{2,1,0:T(8,128)S(1)}, u32[]{:S(2)}, u32[]{:S(2)}) collective-permute-start(f32[12,8,384]{2,1,0:T(8,128)S(1)} %get-tuple-element.50), channel_id=1, source_target_pairs={{0,12},{4,0},{8,4},{12,8},{1,13},{5,1},{9,5},{13,9},{2,14},{6,2},{... | collective-permute-start | bytes 442376 | tf_op jit(solution)/shard_map/ppermute | solution.py:445
  6.2 0.0 collective-permute-start.1
  6.2 4.5 %collective-permute-start.2 = (f32[96,128]{1,0:T(8,128)S(1)}, f32[96,128]{1,0:T(8,128)S(1)}, u32[]{:S(2)}, u32[]{:S(2)}) collective-permute-start(f32[96,128]{1,0:T(8,128)S(1)} %get-tuple-element.52), channel_id=1, source_target_pairs={{0,19},{1,0},{2,1},{3,2},{16,3},{17,16},{18,17},{19,18},{4,23},{5,... | collective-permute-start | bytes 147464 | tf_op jit(solution)/shard_map/ppermute | solution.py:445
  10.7 0.0 collective-permute-start.3
  10.8 0.0 copy-start.3
  10.8 0.0 copy-start.6
  10.8 0.0 copy-start.7
  10.8 0.0 copy-start.12
  10.8 0.0 copy-start.14
  10.9 5.1 %shard_map.185 = (f32[3,16,64,256]{3,2,1,0:T(8,128)S(1)}, f32[3,16,32,128]{3,2,1,0:T(8,128)S(1)}, f32[64,256]{1,0:T(8,128)S(1)}, f32[64,256]{1,0:T(8,128)S(1)}, ...) custom-call(f32[3,16,64,256]{3,2,1,0:T(8,128)S(1)} %get-tuple-elemen, ...), custom_call_target="tpu_custom_call" | custom-call | flops 40000000 | bytes 40000000 | tf_op jit(solution)/shard_map/pallas_call | solution.py:428
  15.9 0.0 collective-permute-done.2.refs_10_
  15.9 1.6 %collective-permute-done.3.refs_11_ = f32[96,128]{1,0:T(8,128)S(1)} collective-permute-done((f32[96,128]{1,0:T(8,128)S(1)}, f32[96,128]{1,0:T(8,128)S(1)}, u32[]{:S(2)}, u32[]{:S(2)}) %collective-permute-start.3) | collective-permute-done | bytes 49184 | tf_op jit(solution)/shard_map/ppermute | solution.py:445
  17.6 2.8 %shard_map.186 = (f32[3,16,64,256]{3,2,1,0:T(8,128)S(1)}, f32[3,16,32,128]{3,2,1,0:T(8,128)S(1)}, f32[1,4]{1,0:T(1,128)S(1)}, f32[12,8,384]{2,1,0:T(8,128)S(1)},...) custom-call(f32[3,16,64,256]{3,2,1,0:T(8,128)S(1)} %get-tuple-elemen, ...), custom_call_target="tpu_custom_call", output_to_operand_aliasing={{0}: (0, {}), {1}: (1, {})} | custom-call | flops 20000000 | bytes 20000000 | tf_op jit(solution)/shard_map/pallas_call | solution.py:428
  20.4 1.0 %collective-permute-start.4 = (f32[12,8,384]{2,1,0:T(8,128)S(1)}, f32[12,8,384]{2,1,0:T(8,128)S(1)}, u32[]{:S(2)}, u32[]{:S(2)}) collective-permute-start(f32[12,8,384]{2,1,0:T(8,128)S(1)} %get-tuple-element.60), channel_id=1, source_target_pairs={{0,12},{4,0},{8,4},{12,8},{1,13},{5,1},{9,5},{13,9},{2,14},{6,2},{... | collective-permute-start | bytes 442376 | tf_op jit(solution)/shard_map/ppermute | solution.py:445
  21.4 0.0 collective-permute-start.5
  21.4 3.4 %collective-permute-start.6 = (f32[96,128]{1,0:T(8,128)S(1)}, f32[96,128]{1,0:T(8,128)S(1)}, u32[]{:S(2)}, u32[]{:S(2)}) collective-permute-start(f32[96,128]{1,0:T(8,128)S(1)} %get-tuple-element.62), channel_id=1, source_target_pairs={{0,19},{1,0},{2,1},{3,2},{16,3},{17,16},{18,17},{19,18},{4,23},{5,... | collective-permute-start | bytes 147464 | tf_op jit(solution)/shard_map/ppermute | solution.py:445
  24.8 0.0 collective-permute-start.7
  24.8 5.1 %shard_map.187 = (f32[3,16,64,256]{3,2,1,0:T(8,128)S(1)}, f32[3,16,32,128]{3,2,1,0:T(8,128)S(1)}, f32[3,64,256]{2,1,0:T(8,128)S(1)}, f32[3,64,256]{2,1,0:T(8,128...) custom-call(f32[3,16,64,256]{3,2,1,0:T(8,128)S(1)} %get-tuple-element.55.uf, f32[16,64,256]{2,1,0:T(8,128)S(1)} %copy-done, ...), custom_call_target="tpu_custom_call" | custom-call | flops 40000000 | bytes 40000000 | tf_op jit(solution)/shard_map/pallas_call | solution.py:428
  29.8 0.0 collective-permute-done.6.refs_10_.refs_2_
  29.8 1.7 %collective-permute-done.7.refs_11_.refs_3_ = f32[96,128]{1,0:T(8,128)S(1)} collective-permute-done((f32[96,128]{1,0:T(8,128)S(1)}, f32[96,128]{1,0:T(8,128)S(1)}, u32[]{:S(2)}, u32[]{:S(2)}) %collective-permute-start.7) | collective-permute-done | bytes 49184 | tf_op jit(solution)/shard_map/ppermute | solution.py:445
  31.6 0.0 collective-permute-done.4.refs_8_.refs_0_
  31.6 0.8 %shard_map.188 = (f32[3,64,256]{2,1,0:T(8,128)S(1)}, f32[3,32,128]{2,1,0:T(8,128)S(1)}, f32[1,4]{1,0:T(1,128)S(1)}, f32[2,96,128]{2,1,0:T(8,128)S(1)}) custom-call(bf16[768,256]{1,0:T(8,128)(2,1)S(1)} %copy-done.6, f32[3,16,64,256]{3,2,1,0:T(8,128)S(1)} %get-tuple-element.55.uf, f32[3,16,32,128]{3,2,1,0:T(8,128)S(1)} %get-tuple-element.56.uc, ...), custom_call_target="tpu_custom_call" | custom-call | flops 10000000 | bytes 10000000 | tf_op jit(solution)/shard_map/pallas_call | solution.py:428
  32.4 2.2 %shard_map.189 = (f32[3,16,64,256]{3,2,1,0:T(8,128)}, f32[3,16,32,128]{3,2,1,0:T(8,128)}, f32[32,2,4]{2,1,0:T(2,128)S(1)}) custom-call(f32[1,4]{1,0:T(1,128)S(1)} %get-tuple-element.54.change0, f32[1,4]{1,0:T(1,128)S(1)} %get-tuple-element.64.change1, f32[16,64,256]{2,1,0:T(8,128)S(1)} %copy-done, f32[16,64,256]{2,1,0:T(8,128)S(1)} %copy-done.1, ...), custom_call_target="tpu_custom_call" | custom-call | flops 40000000 | bytes 40000000 | tf_op jit(solution)/shard_map/pallas_call | solution.py:428
  34.6 11.1 %all_to_all.5 = f32[32,2,4]{2,1,0:T(2,128)S(1)} all-to-all(f32[32,2,4]{2,1,0:T(2,128)S(1)} %get-tuple-element.72), channel_id=1, replica_groups=mesh['grid'=2,'gx'=4,'gy'=4] {'grid','gx','gy'}, dimensions={0} | all-to-all | bytes 2048 | tf_op jit(solution)/shard_map/all_to_all | solution.py:515
  45.7 0.6 %reduce_max.9 = f32[2,4]{1,0:T(2,128)} reduce(f32[32,2,4]{2,1,0:T(2,128)S(1)} %all_to_all.5, f32[]{:T(128)} %constant.8.clone.1), dimensions={0}, to_apply=%region_0.0 | reduce | flops 248 | bytes 1060 | tf_op jit(solution)/shard_map/reduce_max | solution.py:515
  (22 shorter events, 0.0 us)
Async XLA Ops:
  0.6 10.1 %copy-start.4 = (bf16[384,256]{1,0:T(8,128)(2,1)S(1)}, bf16[384,256]{1,0:T(8,128)(2,1)}, u32[]{:S(2)}) copy-start(bf16[384,256]{1,0:T(8,128)(2,1)} %constant.19.clone.widen) | copy-start | bytes 589828
  0.6 10.1 %copy-start.5 = (bf16[768,128]{1,0:T(8,128)(2,1)S(1)}, bf16[768,128]{1,0:T(8,128)(2,1)}, u32[]{:S(2)}) copy-start(bf16[768,128]{1,0:T(8,128)(2,1)} %constant.18.clone.narrow) | copy-start | bytes 589828
  0.7 10.1 %copy-start.13 = (bf16[256,128]{1,0:T(8,128)(2,1)S(1)}, bf16[256,128]{1,0:T(8,128)(2,1)}, u32[]{:S(2)}) copy-start(bf16[256,128]{1,0:T(8,128)(2,1)} %constant.23.clone.right_c) | copy-start | bytes 196612
  0.7 10.1 %copy-start.9 = (bf16[256,512]{1,0:T(8,128)(2,1)S(1)}, bf16[256,512]{1,0:T(8,128)(2,1)}, u32[]{:S(2)}) copy-start(bf16[256,512]{1,0:T(8,128)(2,1)} %constant.22.clone.left_c) | copy-start | bytes 786436
  0.7 10.1 %copy-start.10 = (bf16[512,256]{1,0:T(8,128)(2,1)S(1)}, bf16[512,256]{1,0:T(8,128)(2,1)}, u32[]{:S(2)}) copy-start(bf16[512,256]{1,0:T(8,128)(2,1)} %constant.21.clone.right_f) | copy-start | bytes 786436
  0.7 10.0 %copy-start.11 = (bf16[256,512]{1,0:T(8,128)(2,1)S(1)}, bf16[256,512]{1,0:T(8,128)(2,1)}, u32[]{:S(2)}) copy-start(bf16[256,512]{1,0:T(8,128)(2,1)} %constant.20.clone.left_f) | copy-start | bytes 786436
  0.7 10.0 %copy-start.2 = (f32[16,32,128]{2,1,0:T(8,128)S(1)}, f32[16,32,128]{2,1,0:T(8,128)}, u32[]{:S(2)}) copy-start(f32[16,32,128]{2,1,0:T(8,128)} %cs.9) | copy-start | bytes 786436
  0.7 10.0 %copy-start.8 = (f32[64,256]{1,0:T(8,128)S(1)}, f32[64,256]{1,0:T(8,128)}, u32[]{:S(2)}) copy-start(f32[64,256]{1,0:T(8,128)} %tr.7) | copy-start | bytes 196612
  0.7 10.0 %copy-start.1 = (f32[16,64,256]{2,1,0:T(8,128)S(1)}, f32[16,64,256]{2,1,0:T(8,128)}, u32[]{:S(2)}) copy-start(f32[16,64,256]{2,1,0:T(8,128)} %me.7) | copy-start | bytes 3145732
  0.7 10.0 %copy-start = (f32[16,64,256]{2,1,0:T(8,128)S(1)}, f32[16,64,256]{2,1,0:T(8,128)}, u32[]{:S(2)}) copy-start(f32[16,64,256]{2,1,0:T(8,128)} %sp.7) | copy-start | bytes 3145732
  3.7 13.8 %collective-permute-start = (f32[12,8,384]{2,1,0:T(8,128)S(1)}, f32[12,8,384]{2,1,0:T(8,128)S(1)}, u32[]{:S(2)}, u32[]{:S(2)}) collective-permute-start(f32[12,8,384]{2,1,0:T(8,128)S(1)} %get-tuple-element.50), channel_id=1, source_target_pairs={{0,12},{4,0},{8,4},{12,8},{1,13},{5,1},{9,5},{13,9},{2,14},{6,2},{... | collective-permute-start | bytes 442376 | tf_op jit(solution)/shard_map/ppermute | solution.py:445
  6.2 11.3 %collective-permute-start.1 = (f32[12,8,384]{2,1,0:T(8,128)S(1)}, f32[12,8,384]{2,1,0:T(8,128)S(1)}, u32[]{:S(2)}, u32[]{:S(2)}) collective-permute-start(f32[12,8,384]{2,1,0:T(8,128)S(1)} %get-tuple-element.51), channel_id=1, source_target_pairs={{0,4},{4,8},{8,12},{12,0},{1,5},{5,9},{9,13},{13,1},{2,6},{6,10},{... | collective-permute-start | bytes 442376 | tf_op jit(solution)/shard_map/ppermute | solution.py:445
  6.2 9.7 %collective-permute-start.2 = (f32[96,128]{1,0:T(8,128)S(1)}, f32[96,128]{1,0:T(8,128)S(1)}, u32[]{:S(2)}, u32[]{:S(2)}) collective-permute-start(f32[96,128]{1,0:T(8,128)S(1)} %get-tuple-element.52), channel_id=1, source_target_pairs={{0,19},{1,0},{2,1},{3,2},{16,3},{17,16},{18,17},{19,18},{4,23},{5,... | collective-permute-start | bytes 147464 | tf_op jit(solution)/shard_map/ppermute | solution.py:445
  10.7 6.8 %collective-permute-start.3 = (f32[96,128]{1,0:T(8,128)S(1)}, f32[96,128]{1,0:T(8,128)S(1)}, u32[]{:S(2)}, u32[]{:S(2)}) collective-permute-start(f32[96,128]{1,0:T(8,128)S(1)} %get-tuple-element.53), channel_id=1, source_target_pairs={{0,1},{1,2},{2,3},{3,16},{16,17},{17,18},{18,19},{19,0},{4,5},{5,6... | collective-permute-start | bytes 147464 | tf_op jit(solution)/shard_map/ppermute | solution.py:445
  10.8 6.7 %copy-start.3 = (f32[3,16,64,256]{3,2,1,0:T(8,128)S(1)}, f32[3,16,64,256]{3,2,1,0:T(8,128)}, u32[]{:S(2)}) copy-start(f32[3,16,64,256]{3,2,1,0:T(8,128)} %pf.1) | copy-start | bytes 9437188
  10.8 6.7 %copy-start.6 = (bf16[768,256]{1,0:T(8,128)(2,1)S(1)}, bf16[768,256]{1,0:T(8,128)(2,1)}, u32[]{:S(2)}) copy-start(bf16[768,256]{1,0:T(8,128)(2,1)} %constant.25.clone.unpack) | copy-start | bytes 1179652
  10.8 6.7 %copy-start.7 = (bf16[768,256]{1,0:T(8,128)(2,1)S(1)}, bf16[768,256]{1,0:T(8,128)(2,1)}, u32[]{:S(2)}) copy-start(bf16[768,256]{1,0:T(8,128)(2,1)} %constant.24.clone.pack_hbm.pack) | copy-start | bytes 1179652
  10.8 6.7 %copy-start.12 = (f32[3,16,32,128]{3,2,1,0:T(8,128)S(1)}, f32[3,16,32,128]{3,2,1,0:T(8,128)}, u32[]{:S(2)}) copy-start(f32[3,16,32,128]{3,2,1,0:T(8,128)} %pc.1) | copy-start | bytes 2359300
  10.8 6.7 %copy-start.14 = (f32[32,128]{1,0:T(8,128)S(1)}, f32[32,128]{1,0:T(8,128)}, u32[]{:S(2)}) copy-start(f32[32,128]{1,0:T(8,128)} %sh.3) | copy-start | bytes 49156
  20.4 11.2 %collective-permute-start.4 = (f32[12,8,384]{2,1,0:T(8,128)S(1)}, f32[12,8,384]{2,1,0:T(8,128)S(1)}, u32[]{:S(2)}, u32[]{:S(2)}) collective-permute-start(f32[12,8,384]{2,1,0:T(8,128)S(1)} %get-tuple-element.60), channel_id=1, source_target_pairs={{0,12},{4,0},{8,4},{12,8},{1,13},{5,1},{9,5},{13,9},{2,14},{6,2},{... | collective-permute-start | bytes 442376 | tf_op jit(solution)/shard_map/ppermute | solution.py:445
  21.4 10.2 %collective-permute-start.5 = (f32[12,8,384]{2,1,0:T(8,128)S(1)}, f32[12,8,384]{2,1,0:T(8,128)S(1)}, u32[]{:S(2)}, u32[]{:S(2)}) collective-permute-start(f32[12,8,384]{2,1,0:T(8,128)S(1)} %get-tuple-element.61), channel_id=1, source_target_pairs={{0,4},{4,8},{8,12},{12,0},{1,5},{5,9},{9,13},{13,1},{2,6},{6,10},{... | collective-permute-start | bytes 442376 | tf_op jit(solution)/shard_map/ppermute | solution.py:445
  21.4 8.5 %collective-permute-start.6 = (f32[96,128]{1,0:T(8,128)S(1)}, f32[96,128]{1,0:T(8,128)S(1)}, u32[]{:S(2)}, u32[]{:S(2)}) collective-permute-start(f32[96,128]{1,0:T(8,128)S(1)} %get-tuple-element.62), channel_id=1, source_target_pairs={{0,19},{1,0},{2,1},{3,2},{16,3},{17,16},{18,17},{19,18},{4,23},{5,... | collective-permute-start | bytes 147464 | tf_op jit(solution)/shard_map/ppermute | solution.py:445
  24.8 6.8 %collective-permute-start.7 = (f32[96,128]{1,0:T(8,128)S(1)}, f32[96,128]{1,0:T(8,128)S(1)}, u32[]{:S(2)}, u32[]{:S(2)}) collective-permute-start(f32[96,128]{1,0:T(8,128)S(1)} %get-tuple-element.63), channel_id=1, source_target_pairs={{0,1},{1,2},{2,3},{3,16},{16,17},{17,18},{18,19},{19,0},{4,5},{5,6... | collective-permute-start | bytes 147464 | tf_op jit(solution)/shard_map/ppermute | solution.py:445

commit v6 on v5

--- a/solution.py
+++ b/solution.py
@@ -82,56 +82,62 @@
     return jnp.dot(pieces(x), table[...], preferred_element_type=jnp.float32)
 
 
-def pack_all(uf, uc, pack, x_down, x_up, y_down, y_up, ready=None, ready_table=None):
-    comps, layers, rows, cols = uf.shape
-    crows, ccols = uc.shape[2:]
-    raw = []
-    for ref, at in ((uf, slice(0, cols)), (uc, slice(cols, cols + ccols))):
-        n, width = ref.shape[2:]
-        lane = lax.broadcasted_iota(jnp.int32, (n, LANES), 1)
+def pack_rows(tops, bottoms, x_down, x_up):
+    lanes = 0
+    for top, bottom in zip(tops, bottoms):
+        comps, layers, _, width = top.shape
+        at = slice(lanes, lanes + width)
+        lanes += width
         sub = lax.broadcasted_iota(jnp.int32, (8, width), 0)
-        columns = [jnp.zeros((n, LANES), jnp.float32) for _ in range(2)]
-        for g in range(0, layers, 4):
-            if ready is not None:
-                ready(ref is uc, g)
-            for c in range(comps):
+        for c in range(comps):
+            for g in range(0, layers, 4):
                 first = last = jnp.zeros((8, width), jnp.float32)
                 for i in range(4):
-                    p = c * layers + g + i
-                    u = ref[c, g + i, :, 0:LANES]
-                    if width > LANES:
-                        u = jnp.where(lane < 2, u, ref[c, g + i, :, width - LANES : width])
-                    u = turn(u, slot(p) % LANES + 2, 1)
-                    half = slot(p) // LANES
-                    columns[half] = jnp.where(lane // 4 == slot(p) % LANES // 4, u, columns[half])
-                    first = jnp.where(sub // 2 == i, turn(ref[c, g + i, 0:8, :], 2 * i, 0), first)
-                    last = jnp.where(sub // 2 == i, turn(ref[c, g + i, n - 8 : n, :], 2 * i + 2, 0), last)
+                    first = jnp.where(sub // 2 == i, turn(top[c, g + i], 2 * i, 0), first)
+                    last = jnp.where(sub // 2 == i, turn(bottom[c, g + i], 2 * i + 2, 0), last)
                 tile = (c * layers + g) // 4
                 x_down[tile, :, at] = jnp.where(lax.rem(sub, 2) == 1, 16.0 * turn(first, 1, 0), 0.0) - first
                 x_up[tile, :, at] = jnp.where(lax.rem(sub, 2) == 0, 16.0 * turn(last, -1, 0), 0.0) - last
+
+
+def pack_columns(uf, uc, pack, y_down, y_up):
+    raw = []
+    for ref in (uf, uc):
+        comps, layers, n, width = ref.shape
+        lane = lax.broadcasted_iota(jnp.int32, (n, LANES), 1)
+        columns = [jnp.zeros((n, LANES), jnp.float32) for _ in range(2)]
+        for c in range(comps):
+            for k in range(layers):
+                p = c * layers + k
+                u = ref[c, k, :, 0:LANES]
+                if width > LANES:
+                    u = jnp.where(lane < 2, u, ref[c, k, :, width - LANES : width])
+                u = turn(u, slot(p) % LANES + 2, 1)
+                half = slot(p) // LANES
+                columns[half] = jnp.where(lane // 4 == slot(p) % LANES // 4, u, columns[half])
         raw.append(jnp.concatenate(columns, axis=1))
-    if ready_table is not None:
-        ready_table()
     packed = times(jnp.concatenate(raw, axis=0), pack)
     y_down[...] = packed[:, 0:LANES]
     y_up[...] = packed[:, LANES : 2 * LANES]
 
 
-def load_kernel(uf_hbm, uc_hbm, pack_hbm, uf, uc, x_down, x_up, y_down, y_up, pack, sem):
-    layers = uf.shape[1]
-    copies = {}
-    for coarse, src, dst in ((False, uf_hbm, uf), (True, uc_hbm, uc)):
-        for g in range(0, layers, 4):
-            at = pl.ds(g, 4)
-            copies[coarse, g] = pltpu.make_async_copy(src.at[:, at], dst.at[:, at], sem.at[int(coarse), g // 4])
-            copies[coarse, g].start()
-    table = pltpu.make_async_copy(pack_hbm, pack, sem.at[2, 0])
+def rows_kernel(uf_hbm, uc_hbm, pack_hbm, x_down, x_up, pack, top_f, bottom_f, top_c, bottom_c, sem):
+    table = pltpu.make_async_copy(pack_hbm, pack, sem.at[4])
+    copies = []
+    for ref, top, bottom in ((uf_hbm, top_f, bottom_f), (uc_hbm, top_c, bottom_c)):
+        rows = ref.shape[2]
+        for at, into in ((pl.ds(0, 8), top), (pl.ds(rows - 8, 8), bottom)):
+            copies.append(pltpu.make_async_copy(ref.at[:, :, at], into, sem.at[len(copies)]))
+            copies[-1].start()
     table.start()
-
-    def ready(coarse, g):
-        copies[coarse, g].wait()
-
-    pack_all(uf, uc, pack, x_down, x_up, y_down, y_up, ready, table.wait)
+    for copy in copies:
+        copy.wait()
+    pack_rows((top_f, top_c), (bottom_f, bottom_c), x_down, x_up)
+    table.wait()
+
+
+def columns_kernel(uf, uc, pack, y_down, y_up):
+    pack_columns(uf, uc, pack, y_down, y_up)
 
 
 def main_kernel(first_step, uf, sp, me, uc, cs, tr, left_f, right_f, left_c, right_c, widen, narrow, *refs):
@@ -366,7 +372,10 @@
                 vf[c, g + i] = vf_in[c, g + i] - pf[c, g + i] + s12 * edges.plane(edges.fine, c, g, i)
                 vc[c, g + i] = vc_in[c, g + i] - pc[c, g + i] + cs12 * edges.plane(edges.coarse, c, g, i)
 
-    pack_all(vf, vc, pack, *packed)
+    pack_columns(vf, vc, pack, *packed[2:])
+    tops = [v.at[:, :, 0:8] for v in (vf, vc)]
+    bottoms = [v.at[:, :, v.shape[2] - 8 : v.shape[2]] for v in (vf, vc)]
+    pack_rows(tops, bottoms, *packed[:2])
 
 
 def interface_kernel(unpack, uf, uc, cs, tr, sh, widen, narrow, *refs):
@@ -466,7 +475,7 @@
         pltpu.VMEM((rows + crows, LANES), f32),
         pltpu.VMEM((rows + crows, LANES), f32),
     ]
-    tall = pltpu.VMEM((cols // LANES, 2 * comps * rows, LANES), f32)
+    tall = pltpu.VMEM((cols // LANES, 2 * comps * rows + 8, LANES), f32)
     one_c = pltpu.VMEM((crows, ccols), f32)
     fixed_outs = [pltpu.VMEM((rows, cols), f32)] * 3 + [one_c, one_c]
     prep_outs = [plane_f, plane_f, pltpu.VMEM((2 * comps * crows, ccols), f32), plane_c]
@@ -479,10 +488,13 @@
     lat = pltpu.VMEM((2, comps, 256, cols), f32)
     tr, sh = fine_traction, coarse_shear
 
-    uf, uc, *mine = call(
-        load_kernel, (fine_field, coarse_field, pack), [fine, coarse] + edge_outs,
-        scratch=[pltpu.VMEM(pack.shape, pack.dtype), pltpu.SemaphoreType.DMA((3, layers // 4))], hbm=(0, 1, 2),
-    )
+    uf, uc = fine_field, coarse_field
+    ends = [pltpu.VMEM((*x.shape[:2], 8, x.shape[3]), f32) for x in (uf, uf, uc, uc)]
+    x_down, x_up, pack = call(
+        rows_kernel, (uf, uc, pack), [*edge_outs[:2], pltpu.VMEM(pack.shape, pack.dtype)],
+        scratch=[*ends, pltpu.SemaphoreType.DMA((5,))], hbm=(0, 1, 2),
+    )
+    mine = (x_down, x_up, *call(columns_kernel, (uf, uc, pack), edge_outs[2:]))
     theirs = exchange(mine)
     sp, me, cs = fine_speed, fine_metric, coarse_speed
     vf, vc, *prep = call(

time: 46.5 us -> 46.1 us (level)
    pallas_call x6 -> x7, Pallas kernels: 18.9 us -> 18.5 us  [call(): pl.pallas_call(kernel, out_shape=tuple(outs), in_specs=[pl.BlockSpec(memo...]
  transfers between devices with their start and end apart: 8 -> 8, of which waited for: 2 -> 2; matrix products, arithmetic and copies ran while one was open for 0% -> 0% of each run, Pallas kernels for 22% -> 24%
where the time goes in v6:
time: 46.1 us; the launch traced here: 45.9 us
  Pallas kernels  18.5 us (40%)
  starting transfers between devices  11.5 us (25%)
  blocking collectives  11.2 us (24%)
  waiting for transfers between devices  3.25 us (7%)
  between operations  0.89 us (2%)
  other arithmetic  0.6 us (1%)
    pallas_call x7, Pallas kernels, call(): pl.pallas_call(kernel, out_shape=tuple(outs), in_specs=[pl.BlockSpec(memo...  18.5 us
    ppermute x8, starting transfers between devices, ring(): return lax.ppermute(value, axis, [(i, (i + by) % n) for i in range(n)])  11.5 us
    all_to_all x1, blocking collectives, on_device(): lax.all_to_all(spread, ALL, 0, 0, tiled=True)  11.2 us
    ppermute x8, waiting for transfers between devices, ring(): return lax.ppermute(value, axis, [(i, (i + by) % n) for i in range(n)])  3.25 us
  transfers between devices with their start and end apart: 8, of which 2 were waited for; matrix products, arithmetic and copies ran while one was open for 0% of the time, Pallas kernels for 24%

profile of v6, /device:TPU:0, one launch (start us, length us, event | category | flops | bytes accessed | tf_op | source)
XLA Modules:
  0.0 45.9 jit_solution(500926616763885757)
XLA Ops:
  0.6 1.6 %shard_map.185 = (f32[12,8,384]{2,1,0:T(8,128)S(1)}, f32[12,8,384]{2,1,0:T(8,128)S(1)}, bf16[768,256]{1,0:T(8,128)(2,1)S(1)}) custom-call(f32[3,16,64,256]{3,2,1,0:T(8,128)} %refs_5_.1, f32[3,16,32,128]{3,2,1,0:T(8,128)} %refs_6_.1, bf16[768,256]{1,0:T(8,128)(2,1)} %constant.24.clone.pack_hbm), custom_call_target="tpu_custom_call" | custom-call | tf_op jit(solution)/shard_map/pallas_call | solution.py:437
  2.2 0.0 copy-start.2
  2.2 0.0 copy-start.3
  2.2 0.0 copy-start.4
  2.3 0.0 copy-start.6
  2.3 0.0 copy-start.7
  2.3 0.0 copy-start.9
  2.3 0.0 copy-start.10
  2.3 0.0 copy-start.11
  2.3 0.0 copy-start.12
  2.3 0.0 copy-start.14
  2.3 2.5 %collective-permute-start = (f32[12,8,384]{2,1,0:T(8,128)S(1)}, f32[12,8,384]{2,1,0:T(8,128)S(1)}, u32[]{:S(2)}, u32[]{:S(2)}) collective-permute-start(f32[12,8,384]{2,1,0:T(8,128)S(1)} %get-tuple-element.48), channel_id=1, source_target_pairs={{0,12},{4,0},{8,4},{12,8},{1,13},{5,1},{9,5},{13,9},{2,14},{6,2},{... | collective-permute-start | bytes 442376 | tf_op jit(solution)/shard_map/ppermute | solution.py:454
  4.8 0.0 collective-permute-start.1
  4.8 0.9 %shard_map.186 = (f32[96,128]{1,0:T(8,128)S(1)}, f32[96,128]{1,0:T(8,128)S(1)}) custom-call(f32[3,16,64,256]{3,2,1,0:T(8,128)S(1)} %copy-done, f32[3,16,32,128]{3,2,1,0:T(8,128)S(1)} %copy-done.1, bf16[768,256]{1,0:T(8,128)(2,1)S(1)} %get-tuple-element.39.pack), custom_call_target="tpu_custom_call" | custom-call | tf_op jit(solution)/shard_map/pallas_call | solution.py:437
  5.7 4.6 %collective-permute-start.2 = (f32[96,128]{1,0:T(8,128)S(1)}, f32[96,128]{1,0:T(8,128)S(1)}, u32[]{:S(2)}, u32[]{:S(2)}) collective-permute-start(f32[96,128]{1,0:T(8,128)S(1)} %get-tuple-element.50), channel_id=1, source_target_pairs={{0,19},{1,0},{2,1},{3,2},{16,3},{17,16},{18,17},{19,18},{4,23},{5,... | collective-permute-start | bytes 147464 | tf_op jit(solution)/shard_map/ppermute | solution.py:454
  10.3 0.1 collective-permute-start.3
  10.4 5.1 %shard_map.184 = (f32[3,16,64,256]{3,2,1,0:T(8,128)S(1)}, f32[3,16,32,128]{3,2,1,0:T(8,128)S(1)}, f32[64,256]{1,0:T(8,128)S(1)}, f32[64,256]{1,0:T(8,128)S(1)}, ...) custom-call(f32[3,16,64,256]{3,2,1,0:T(8,128)S(1)} %copy-done, ...), custom_call_target="tpu_custom_call" | custom-call | flops 40000000 | bytes 40000000 | tf_op jit(solution)/shard_map/pallas_call | solution.py:437
  15.5 0.0 collective-permute-done.2.refs_10_
  15.6 1.6 %collective-permute-done.3.refs_11_ = f32[96,128]{1,0:T(8,128)S(1)} collective-permute-done((f32[96,128]{1,0:T(8,128)S(1)}, f32[96,128]{1,0:T(8,128)S(1)}, u32[]{:S(2)}, u32[]{:S(2)}) %collective-permute-start.3) | collective-permute-done | bytes 49184 | tf_op jit(solution)/shard_map/ppermute | solution.py:454
  17.1 0.0 collective-permute-done.refs_8_
  17.2 2.8 %shard_map.187 = (f32[3,16,64,256]{3,2,1,0:T(8,128)S(1)}, f32[3,16,32,128]{3,2,1,0:T(8,128)S(1)}, f32[1,4]{1,0:T(1,128)S(1)}, f32[12,8,384]{2,1,0:T(8,128)S(1)},...) custom-call(f32[3,16,64,256]{3,2,1,0:T(8,128)S(1)} %get-tuple-elemen, ...), custom_call_target="tpu_custom_call", output_to_operand_aliasing={{0}: (0, {}), {1}: (1, {})} | custom-call | flops 20000000 | bytes 20000000 | tf_op jit(solution)/shard_map/pallas_call | solution.py:437
  20.0 0.3 collective-permute-start.4
  20.3 0.2 collective-permute-start.5
  20.5 3.8 %collective-permute-start.6 = (f32[96,128]{1,0:T(8,128)S(1)}, f32[96,128]{1,0:T(8,128)S(1)}, u32[]{:S(2)}, u32[]{:S(2)}) collective-permute-start(f32[96,128]{1,0:T(8,128)S(1)} %get-tuple-element.60), channel_id=1, source_target_pairs={{0,19},{1,0},{2,1},{3,2},{16,3},{17,16},{18,17},{19,18},{4,23},{5,... | collective-permute-start | bytes 147464 | tf_op jit(solution)/shard_map/ppermute | solution.py:454
  24.3 0.0 collective-permute-start.7
  24.3 5.1 %shard_map.188 = (f32[3,16,64,256]{3,2,1,0:T(8,128)S(1)}, f32[3,16,32,128]{3,2,1,0:T(8,128)S(1)}, f32[3,64,256]{2,1,0:T(8,128)S(1)}, f32[3,64,256]{2,1,0:T(8,128...) custom-call(f32[3,16,64,256]{3,2,1,0:T(8,128)S(1)} %get-tuple-element.53.uf, f32[16,64,256]{2,1,0:T(8,128)S(1)} %copy-done.2, ...), custom_call_target="tpu_custom_call" | custom-call | flops 40000000 | bytes 40000000 | tf_op jit(solution)/shard_map/pallas_call | solution.py:437
  29.5 0.0 collective-permute-done.6.refs_10_.refs_2_
  29.5 1.7 %collective-permute-done.7.refs_11_.refs_3_ = f32[96,128]{1,0:T(8,128)S(1)} collective-permute-done((f32[96,128]{1,0:T(8,128)S(1)}, f32[96,128]{1,0:T(8,128)S(1)}, u32[]{:S(2)}, u32[]{:S(2)}) %collective-permute-start.7) | collective-permute-done | bytes 49184 | tf_op jit(solution)/shard_map/ppermute | solution.py:454
  31.1 0.8 %shard_map.189 = (f32[3,64,256]{2,1,0:T(8,128)S(1)}, f32[3,32,128]{2,1,0:T(8,128)S(1)}, f32[1,4]{1,0:T(1,128)S(1)}, f32[2,96,128]{2,1,0:T(8,128)S(1)}) custom-call(bf16[768,256]{1,0:T(8,128)(2,1)S(1)} %copy-done.8, f32[3,16,64,256]{3,2,1,0:T(8,128)S(1)} %get-tuple-element.53.uf, f32[3,16,32,128]{3,2,1,0:T(8,128)S(1)} %get-tuple-element.54.uc, ...), custom_call_target="tpu_custom_call" | custom-call | flops 10000000 | bytes 10000000 | tf_op jit(solution)/shard_map/pallas_call | solution.py:437
  32.0 2.2 %shard_map.190 = (f32[3,16,64,256]{3,2,1,0:T(8,128)}, f32[3,16,32,128]{3,2,1,0:T(8,128)}, f32[32,2,4]{2,1,0:T(2,128)S(1)}) custom-call(f32[1,4]{1,0:T(1,128)S(1)} %get-tuple-element.52.change0, f32[1,4]{1,0:T(1,128)S(1)} %get-tuple-element.62.change1, f32[16,64,256]{2,1,0:T(8,128)S(1)} %copy-done.2, f32[16,64,256]{2,1,0:T(8,128)S(1)} %copy-done.3, ...), custom_call_target="tpu_custom_call" | custom-call | flops 40000000 | bytes 40000000 | tf_op jit(solution)/shard_map/pallas_call | solution.py:437
  34.2 11.2 %all_to_all.5 = f32[32,2,4]{2,1,0:T(2,128)S(1)} all-to-all(f32[32,2,4]{2,1,0:T(2,128)S(1)} %get-tuple-element.70), channel_id=1, replica_groups=mesh['grid'=2,'gx'=4,'gy'=4] {'grid','gx','gy'}, dimensions={0} | all-to-all | bytes 2048 | tf_op jit(solution)/shard_map/all_to_all | solution.py:527
  45.3 0.6 %reduce_max.9 = f32[2,4]{1,0:T(2,128)} reduce(f32[32,2,4]{2,1,0:T(2,128)S(1)} %all_to_all.5, f32[]{:T(128)} %constant.8.clone.1), dimensions={0}, to_apply=%region_0.0 | reduce | flops 248 | bytes 1060 | tf_op jit(solution)/shard_map/reduce_max | solution.py:527
  (25 shorter events, 0.1 us)
Async XLA Ops:
  0.6 4.2 %copy-start.1 = (f32[3,16,32,128]{3,2,1,0:T(8,128)S(1)}, f32[3,16,32,128]{3,2,1,0:T(8,128)}, u32[]{:S(2)}) copy-start(f32[3,16,32,128]{3,2,1,0:T(8,128)} %refs_6_.1) | copy-start | bytes 2359300
  0.6 4.2 %copy-start = (f32[3,16,64,256]{3,2,1,0:T(8,128)S(1)}, f32[3,16,64,256]{3,2,1,0:T(8,128)}, u32[]{:S(2)}) copy-start(f32[3,16,64,256]{3,2,1,0:T(8,128)} %refs_5_.1) | copy-start | bytes 9437188
  2.2 8.1 %copy-start.2 = (f32[16,64,256]{2,1,0:T(8,128)S(1)}, f32[16,64,256]{2,1,0:T(8,128)}, u32[]{:S(2)}) copy-start(f32[16,64,256]{2,1,0:T(8,128)} %sp.7) | copy-start | bytes 3145732
  2.2 8.1 %copy-start.3 = (f32[16,64,256]{2,1,0:T(8,128)S(1)}, f32[16,64,256]{2,1,0:T(8,128)}, u32[]{:S(2)}) copy-start(f32[16,64,256]{2,1,0:T(8,128)} %me.7) | copy-start | bytes 3145732
  2.2 8.1 %copy-start.4 = (f32[16,32,128]{2,1,0:T(8,128)S(1)}, f32[16,32,128]{2,1,0:T(8,128)}, u32[]{:S(2)}) copy-start(f32[16,32,128]{2,1,0:T(8,128)} %cs.9) | copy-start | bytes 786436
  2.3 8.1 %copy-start.6 = (bf16[384,256]{1,0:T(8,128)(2,1)S(1)}, bf16[384,256]{1,0:T(8,128)(2,1)}, u32[]{:S(2)}) copy-start(bf16[384,256]{1,0:T(8,128)(2,1)} %constant.19.clone.widen) | copy-start | bytes 589828
  2.3 8.1 %copy-start.7 = (bf16[768,128]{1,0:T(8,128)(2,1)S(1)}, bf16[768,128]{1,0:T(8,128)(2,1)}, u32[]{:S(2)}) copy-start(bf16[768,128]{1,0:T(8,128)(2,1)} %constant.18.clone.narrow) | copy-start | bytes 589828
  2.3 8.1 %copy-start.9 = (f32[64,256]{1,0:T(8,128)S(1)}, f32[64,256]{1,0:T(8,128)}, u32[]{:S(2)}) copy-start(f32[64,256]{1,0:T(8,128)} %tr.7) | copy-start | bytes 196612
  2.3 8.1 %copy-start.10 = (bf16[256,512]{1,0:T(8,128)(2,1)S(1)}, bf16[256,512]{1,0:T(8,128)(2,1)}, u32[]{:S(2)}) copy-start(bf16[256,512]{1,0:T(8,128)(2,1)} %constant.22.clone.left_c) | copy-start | bytes 786436
  2.3 8.1 %copy-start.11 = (bf16[512,256]{1,0:T(8,128)(2,1)S(1)}, bf16[512,256]{1,0:T(8,128)(2,1)}, u32[]{:S(2)}) copy-start(bf16[512,256]{1,0:T(8,128)(2,1)} %constant.21.clone.right_f) | copy-start | bytes 786436
  2.3 8.1 %copy-start.12 = (bf16[256,512]{1,0:T(8,128)(2,1)S(1)}, bf16[256,512]{1,0:T(8,128)(2,1)}, u32[]{:S(2)}) copy-start(bf16[256,512]{1,0:T(8,128)(2,1)} %constant.20.clone.left_f) | copy-start | bytes 786436
  2.3 8.1 %copy-start.14 = (bf16[256,128]{1,0:T(8,128)(2,1)S(1)}, bf16[256,128]{1,0:T(8,128)(2,1)}, u32[]{:S(2)}) copy-start(bf16[256,128]{1,0:T(8,128)(2,1)} %constant.23.clone.right_c) | copy-start | bytes 196612
  2.3 14.8 %collective-permute-start = (f32[12,8,384]{2,1,0:T(8,128)S(1)}, f32[12,8,384]{2,1,0:T(8,128)S(1)}, u32[]{:S(2)}, u32[]{:S(2)}) collective-permute-start(f32[12,8,384]{2,1,0:T(8,128)S(1)} %get-tuple-element.48), channel_id=1, source_target_pairs={{0,12},{4,0},{8,4},{12,8},{1,13},{5,1},{9,5},{13,9},{2,14},{6,2},{... | collective-permute-start | bytes 442376 | tf_op jit(solution)/shard_map/ppermute | solution.py:454
  4.8 12.3 %collective-permute-start.1 = (f32[12,8,384]{2,1,0:T(8,128)S(1)}, f32[12,8,384]{2,1,0:T(8,128)S(1)}, u32[]{:S(2)}, u32[]{:S(2)}) collective-permute-start(f32[12,8,384]{2,1,0:T(8,128)S(1)} %get-tuple-element.49), channel_id=1, source_target_pairs={{0,4},{4,8},{8,12},{12,0},{1,5},{5,9},{9,13},{13,1},{2,6},{6,10},{... | collective-permute-start | bytes 442376 | tf_op jit(solution)/shard_map/ppermute | solution.py:454
  5.7 9.9 %collective-permute-start.2 = (f32[96,128]{1,0:T(8,128)S(1)}, f32[96,128]{1,0:T(8,128)S(1)}, u32[]{:S(2)}, u32[]{:S(2)}) collective-permute-start(f32[96,128]{1,0:T(8,128)S(1)} %get-tuple-element.50), channel_id=1, source_target_pairs={{0,19},{1,0},{2,1},{3,2},{16,3},{17,16},{18,17},{19,18},{4,23},{5,... | collective-permute-start | bytes 147464 | tf_op jit(solution)/shard_map/ppermute | solution.py:454
  10.3 6.9 %copy-start.5 = (f32[3,16,64,256]{3,2,1,0:T(8,128)S(1)}, f32[3,16,64,256]{3,2,1,0:T(8,128)}, u32[]{:S(2)}) copy-start(f32[3,16,64,256]{3,2,1,0:T(8,128)} %pf.1) | copy-start | bytes 9437188
  10.3 6.9 %copy-start.8 = (bf16[768,256]{1,0:T(8,128)(2,1)S(1)}, bf16[768,256]{1,0:T(8,128)(2,1)}, u32[]{:S(2)}) copy-start(bf16[768,256]{1,0:T(8,128)(2,1)} %constant.25.clone.unpack) | copy-start | bytes 1179652
  10.3 6.9 %copy-start.13 = (f32[3,16,32,128]{3,2,1,0:T(8,128)S(1)}, f32[3,16,32,128]{3,2,1,0:T(8,128)}, u32[]{:S(2)}) copy-start(f32[3,16,32,128]{3,2,1,0:T(8,128)} %pc.1) | copy-start | bytes 2359300
  10.3 6.9 %copy-start.15 = (f32[32,128]{1,0:T(8,128)S(1)}, f32[32,128]{1,0:T(8,128)}, u32[]{:S(2)}) copy-start(f32[32,128]{1,0:T(8,128)} %sh.3) | copy-start | bytes 49156
  10.3 6.9 %collective-permute-start.3 = (f32[96,128]{1,0:T(8,128)S(1)}, f32[96,128]{1,0:T(8,128)S(1)}, u32[]{:S(2)}, u32[]{:S(2)}) collective-permute-start(f32[96,128]{1,0:T(8,128)S(1)} %get-tuple-element.51), channel_id=1, source_target_pairs={{0,1},{1,2},{2,3},{3,16},{16,17},{17,18},{18,19},{19,0},{4,5},{5,6... | collective-permute-start | bytes 147464 | tf_op jit(solution)/shard_map/ppermute | solution.py:454
  20.0 11.2 %collective-permute-start.4 = (f32[12,8,384]{2,1,0:T(8,128)S(1)}, f32[12,8,384]{2,1,0:T(8,128)S(1)}, u32[]{:S(2)}, u32[]{:S(2)}) collective-permute-start(f32[12,8,384]{2,1,0:T(8,128)S(1)} %get-tuple-element.58), channel_id=1, source_target_pairs={{0,12},{4,0},{8,4},{12,8},{1,13},{5,1},{9,5},{13,9},{2,14},{6,2},{... | collective-permute-start | bytes 442376 | tf_op jit(solution)/shard_map/ppermute | solution.py:454
  20.3 10.8 %collective-permute-start.5 = (f32[12,8,384]{2,1,0:T(8,128)S(1)}, f32[12,8,384]{2,1,0:T(8,128)S(1)}, u32[]{:S(2)}, u32[]{:S(2)}) collective-permute-start(f32[12,8,384]{2,1,0:T(8,128)S(1)} %get-tuple-element.59), channel_id=1, source_target_pairs={{0,4},{4,8},{8,12},{12,0},{1,5},{5,9},{9,13},{13,1},{2,6},{6,10},{... | collective-permute-start | bytes 442376 | tf_op jit(solution)/shard_map/ppermute | solution.py:454
  20.5 8.9 %collective-permute-start.6 = (f32[96,128]{1,0:T(8,128)S(1)}, f32[96,128]{1,0:T(8,128)S(1)}, u32[]{:S(2)}, u32[]{:S(2)}) collective-permute-start(f32[96,128]{1,0:T(8,128)S(1)} %get-tuple-element.60), channel_id=1, source_target_pairs={{0,19},{1,0},{2,1},{3,2},{16,3},{17,16},{18,17},{19,18},{4,23},{5,... | collective-permute-start | bytes 147464 | tf_op jit(solution)/shard_map/ppermute | solution.py:454
  24.3 6.8 %collective-permute-start.7 = (f32[96,128]{1,0:T(8,128)S(1)}, f32[96,128]{1,0:T(8,128)S(1)}, u32[]{:S(2)}, u32[]{:S(2)}) collective-permute-start(f32[96,128]{1,0:T(8,128)S(1)} %get-tuple-element.61), channel_id=1, source_target_pairs={{0,1},{1,2},{2,3},{3,16},{16,17},{17,18},{18,19},{19,0},{4,5},{5,6... | collective-permute-start | bytes 147464 | tf_op jit(solution)/shard_map/ppermute | solution.py:454

commit v7 on v6

--- a/solution.py
+++ b/solution.py
@@ -378,54 +378,45 @@
     pack_rows(tops, bottoms, *packed[:2])
 
 
-def interface_kernel(unpack, uf, uc, cs, tr, sh, widen, narrow, *refs):
+def last_kernel(change0, unpack, sp, me, cs, uf, uc, vf, vc, tr, sh, widen, narrow, *refs):
     prep, got = refs[:PREP], refs[PREP : PREP + 4]
-    ghost_f, ghost_c, change, slots, tall = refs[PREP + 4 :]
-    edges = Edges(got, slots, (uf.shape[1:], uc.shape[2:]), unpack)
-    g, c4, line = interface(edges, uc, cs, tr, sh, widen, narrow, tall, *prep)
-    for c in range(uf.shape[0]):
-        ghost_f[c] = g[c]
-        ghost_c[c] = c4[c]
-    change[...] = line
-
-
-def last_kernel(change0, change1, sp, me, cs, uf, uc, vf, vc, ghost_f, ghost_c, slots, *refs):
-    got = refs[0:4]
-    out_f, out_c, spread, done_f, done_c, sem = refs[4:]
+    out_f, out_c, spread, done_f, done_c, tall, slots, sem = refs[PREP + 4 :]
     comps, layers, rows, cols = uf.shape
     b = layers - 1
-    edges = Edges(got, slots, (uf.shape[1:], uc.shape[2:]))
-    for step, line in enumerate((change0, change1)):
-        spread[:, step : step + 1, :] = jnp.broadcast_to(line[...][None], (spread.shape[0], 1, spread.shape[2]))
+    edges = Edges(got, slots, (uf.shape[1:], uc.shape[2:]), unpack)
 
     def copy(k):
         return pltpu.make_async_copy(done_f.at[:, k], out_f.at[:, k], sem.at[k])
 
     copy_coarse = pltpu.make_async_copy(done_c, out_c, sem.at[layers])
 
-    def fine(k, g, i):
+    def fine(k):
         s12 = sp[k] * TWELFTH
         for c in range(comps):
-            total = edges.plane(edges.fine, c, g, i)
-            if isinstance(k, int) and k == b:
-                total = total + me[k] * me[k] * (14.0 * ghost_f[c] + uf[c, b])
-            if isinstance(k, int) and k == b - 1:
-                total = total - me[k] * me[k] * ghost_f[c]
-            done_f[c, k] = vf[c, k] + s12 * total
+            done_f[c, k] = vf[c, k] + s12 * edges.plane(edges.fine, c, k // 4 * 4, k % 4)
+
+    for k in range(b - 1):
+        fine(k)
         copy(k).start()
-
+    ghost_f, ghost_c, line = interface(edges, uc, cs, tr, sh, widen, narrow, tall, *prep)
+    for step, change in enumerate((change0[...], line)):
+        spread[:, step : step + 1, :] = jnp.broadcast_to(change[None], (spread.shape[0], 1, spread.shape[2]))
+    for k in (b - 1, b):
+        fine(k)
+        scale = sp[k] * me[k] * me[k] * TWELFTH
+        for c in range(comps):
+            more = 14.0 * ghost_f[c] + uf[c, b] if k == b else -ghost_f[c]
+            done_f[c, k] = done_f[c, k] + scale * more
+        copy(k).start()
     for k in range(layers):
-        fine(k, k // 4 * 4, k % 4)
-
-    for g in range(0, layers, 4):
-        for i in range(4):
-            cs12 = cs[g + i] * TWELFTH
-            for c in range(comps):
-                done_c[c, g + i] = vc[c, g + i] + cs12 * edges.plane(edges.coarse, c, g, i)
-
-    for c in range(comps):
-        done_c[c, 0] = done_c[c, 0] + cs[0] * TWELFTH * (14.0 * ghost_c[c] + uc[c, 0])
-        done_c[c, 1] = done_c[c, 1] - cs[1] * TWELFTH * ghost_c[c]
+        cs12 = cs[k] * TWELFTH
+        for c in range(comps):
+            total = edges.plane(edges.coarse, c, k // 4 * 4, k % 4)
+            if k == 0:
+                total = total + 14.0 * ghost_c[c] + uc[c, 0]
+            if k == 1:
+                total = total - ghost_c[c]
+            done_c[c, k] = vc[c, k] + cs12 * total
     copy_coarse.start()
     for k in range(layers):
         copy(k).wait()
@@ -513,16 +504,12 @@
         [fine, coarse, *prep_outs],
         scratch=[lat, tall], flops=40_000_000,
     )
-    ghost_f, ghost_c, change1, slots = call(
-        interface_kernel, (unpack, uf, uc, cs, tr, sh, widen, narrow, *fixed, *prep[:-1], *theirs),
-        [plane_f, plane_c, line, corrections], scratch=[tall], flops=10_000_000,
-    )
     n = lax.axis_size(ALL)
     out_f, out_c, spread = call(
         last_kernel,
-        (change0, change1, sp, me, cs, uf, uc, vf, vc, ghost_f, ghost_c, slots, *theirs),
+        (change0, unpack, sp, me, cs, uf, uc, vf, vc, tr, sh, widen, narrow, *fixed, *prep[:-1], *theirs),
         [pltpu.HBM(fine_field.shape, f32), pltpu.HBM(coarse_field.shape, f32), pltpu.VMEM((n, STEPS, 4), f32)],
-        scratch=[fine, coarse, pltpu.SemaphoreType.DMA((layers + 1,))], flops=40_000_000,
+        scratch=[fine, coarse, tall, corrections, pltpu.SemaphoreType.DMA((layers + 1,))], flops=40_000_000,
     )
     return out_f, out_c, jnp.max(lax.all_to_all(spread, ALL, 0, 0, tiled=True), axis=0)
 

time: 46.1 us -> 45.7 us (level)
    pallas_call x7 -> x6, Pallas kernels: 18.5 us -> 18.1 us  [call(): pl.pallas_call(kernel, out_shape=tuple(outs), in_specs=[pl.BlockSpec(memo...]
where the time goes in v7:
time: 45.7 us; the launch traced here: 45.6 us
  Pallas kernels  18.1 us (40%)
  starting transfers between devices  11.4 us (25%)
  blocking collectives  11.2 us (25%)
  waiting for transfers between devices  3.25 us (7%)
  between operations  0.88 us (2%)
  other arithmetic  0.6 us (1%)
    pallas_call x6, Pallas kernels, call(): pl.pallas_call(kernel, out_shape=tuple(outs), in_specs=[pl.BlockSpec(memo...  18.1 us
    ppermute x8, starting transfers between devices, ring(): return lax.ppermute(value, axis, [(i, (i + by) % n) for i in range(n)])  11.4 us
    all_to_all x1, blocking collectives, on_device(): lax.all_to_all(spread, ALL, 0, 0, tiled=True)  11.2 us
    ppermute x8, waiting for transfers between devices, ring(): return lax.ppermute(value, axis, [(i, (i + by) % n) for i in range(n)])  3.25 us
  transfers between devices with their start and end apart: 8, of which 2 were waited for; matrix products, arithmetic and copies ran while one was open for 0% of the time, Pallas kernels for 24%

profile of v7, /device:TPU:0, one launch (start us, length us, event | category | flops | bytes accessed | tf_op | source)
XLA Modules:
  0.0 45.6 jit_solution(8671183617832560629)
XLA Ops:
  0.6 1.6 %shard_map.185 = (f32[12,8,384]{2,1,0:T(8,128)S(1)}, f32[12,8,384]{2,1,0:T(8,128)S(1)}, bf16[768,256]{1,0:T(8,128)(2,1)S(1)}) custom-call(f32[3,16,64,256]{3,2,1,0:T(8,128)} %refs_5_.1, f32[3,16,32,128]{3,2,1,0:T(8,128)} %refs_6_.1, bf16[768,256]{1,0:T(8,128)(2,1)} %constant.24.clone.pack_hbm), custom_call_target="tpu_custom_call" | custom-call | tf_op jit(solution)/shard_map/pallas_call | solution.py:428
  2.2 0.0 copy-start.2
  2.2 0.0 copy-start.3
  2.2 0.0 copy-start.4
  2.3 0.0 copy-start.6
  2.3 0.0 copy-start.7
  2.3 0.0 copy-start.9
  2.3 0.0 copy-start.10
  2.3 0.0 copy-start.11
  2.3 0.0 copy-start.12
  2.3 0.0 copy-start.14
  2.3 2.5 %collective-permute-start = (f32[12,8,384]{2,1,0:T(8,128)S(1)}, f32[12,8,384]{2,1,0:T(8,128)S(1)}, u32[]{:S(2)}, u32[]{:S(2)}) collective-permute-start(f32[12,8,384]{2,1,0:T(8,128)S(1)} %get-tuple-element.44), channel_id=1, source_target_pairs={{0,12},{4,0},{8,4},{12,8},{1,13},{5,1},{9,5},{13,9},{2,14},{6,2},{... | collective-permute-start | bytes 442376 | tf_op jit(solution)/shard_map/ppermute | solution.py:445
  4.8 0.0 collective-permute-start.1
  4.8 0.9 %shard_map.186 = (f32[96,128]{1,0:T(8,128)S(1)}, f32[96,128]{1,0:T(8,128)S(1)}) custom-call(f32[3,16,64,256]{3,2,1,0:T(8,128)S(1)} %copy-done, f32[3,16,32,128]{3,2,1,0:T(8,128)S(1)} %copy-done.1, bf16[768,256]{1,0:T(8,128)(2,1)S(1)} %get-tuple-element.35.pack), custom_call_target="tpu_custom_call" | custom-call | tf_op jit(solution)/shard_map/pallas_call | solution.py:428
  5.7 4.6 %collective-permute-start.2 = (f32[96,128]{1,0:T(8,128)S(1)}, f32[96,128]{1,0:T(8,128)S(1)}, u32[]{:S(2)}, u32[]{:S(2)}) collective-permute-start(f32[96,128]{1,0:T(8,128)S(1)} %get-tuple-element.46), channel_id=1, source_target_pairs={{0,19},{1,0},{2,1},{3,2},{16,3},{17,16},{18,17},{19,18},{4,23},{5,... | collective-permute-start | bytes 147464 | tf_op jit(solution)/shard_map/ppermute | solution.py:445
  10.3 0.1 collective-permute-start.3
  10.4 5.1 %shard_map.184 = (f32[3,16,64,256]{3,2,1,0:T(8,128)S(1)}, f32[3,16,32,128]{3,2,1,0:T(8,128)S(1)}, f32[64,256]{1,0:T(8,128)S(1)}, f32[64,256]{1,0:T(8,128)S(1)}, ...) custom-call(f32[3,16,64,256]{3,2,1,0:T(8,128)S(1)} %copy-done, ...), custom_call_target="tpu_custom_call" | custom-call | flops 40000000 | bytes 40000000 | tf_op jit(solution)/shard_map/pallas_call | solution.py:428
  15.5 0.0 collective-permute-done.2.refs_10_
  15.5 1.6 %collective-permute-done.3.refs_11_ = f32[96,128]{1,0:T(8,128)S(1)} collective-permute-done((f32[96,128]{1,0:T(8,128)S(1)}, f32[96,128]{1,0:T(8,128)S(1)}, u32[]{:S(2)}, u32[]{:S(2)}) %collective-permute-start.3) | collective-permute-done | bytes 49184 | tf_op jit(solution)/shard_map/ppermute | solution.py:445
  17.1 0.0 collective-permute-done.refs_8_
  17.2 2.8 %shard_map.187 = (f32[3,16,64,256]{3,2,1,0:T(8,128)S(1)}, f32[3,16,32,128]{3,2,1,0:T(8,128)S(1)}, f32[1,4]{1,0:T(1,128)S(1)}, f32[12,8,384]{2,1,0:T(8,128)S(1)},...) custom-call(f32[3,16,64,256]{3,2,1,0:T(8,128)S(1)} %get-tuple-elemen, ...), custom_call_target="tpu_custom_call", output_to_operand_aliasing={{0}: (0, {}), {1}: (1, {})} | custom-call | flops 20000000 | bytes 20000000 | tf_op jit(solution)/shard_map/pallas_call | solution.py:428
  20.0 0.3 collective-permute-start.4
  20.3 0.2 collective-permute-start.5
  20.6 3.8 %collective-permute-start.6 = (f32[96,128]{1,0:T(8,128)S(1)}, f32[96,128]{1,0:T(8,128)S(1)}, u32[]{:S(2)}, u32[]{:S(2)}) collective-permute-start(f32[96,128]{1,0:T(8,128)S(1)} %get-tuple-element.58), channel_id=1, source_target_pairs={{0,19},{1,0},{2,1},{3,2},{16,3},{17,16},{18,17},{19,18},{4,23},{5,... | collective-permute-start | bytes 147464 | tf_op jit(solution)/shard_map/ppermute | solution.py:445
  24.3 0.0 collective-permute-start.7
  24.3 5.1 %shard_map.188 = (f32[3,16,64,256]{3,2,1,0:T(8,128)S(1)}, f32[3,16,32,128]{3,2,1,0:T(8,128)S(1)}, f32[3,64,256]{2,1,0:T(8,128)S(1)}, f32[3,64,256]{2,1,0:T(8,128...) custom-call(f32[3,16,64,256]{3,2,1,0:T(8,128)S(1)} %get-tuple-element.49.uf, f32[16,64,256]{2,1,0:T(8,128)S(1)} %copy-done.2, ...), custom_call_target="tpu_custom_call" | custom-call | flops 40000000 | bytes 40000000 | tf_op jit(solution)/shard_map/pallas_call | solution.py:428
  29.5 1.7 %collective-permute-done.7.refs_11_ = f32[96,128]{1,0:T(8,128)S(1)} collective-permute-done((f32[96,128]{1,0:T(8,128)S(1)}, f32[96,128]{1,0:T(8,128)S(1)}, u32[]{:S(2)}, u32[]{:S(2)}) %collective-permute-start.7) | collective-permute-done | bytes 49184 | tf_op jit(solution)/shard_map/ppermute | solution.py:445
  31.2 0.0 collective-permute-done.4.refs_8_
  31.2 0.0 collective-permute-done.5.refs_9_
  31.2 2.6 %shard_map.189 = (f32[3,16,64,256]{3,2,1,0:T(8,128)}, f32[3,16,32,128]{3,2,1,0:T(8,128)}, f32[32,2,4]{2,1,0:T(2,128)S(1)}) custom-call(f32[1,4]{1,0:T(1,128)S(1)} %get-tuple-element.48.change0, bf16[768,256]{1,0:T(8,128)(2,1)S(1)} %copy-done.8, f32[16,64,256]{2,1,0:T(8,128)S(1)} %copy-done.2, f32[16,64,256]{2,1,0:T(8,128)S(1)} %copy-done.3, ...), custom_call_target="tpu_custom_call" | custom-call | flops 40000000 | bytes 40000000 | tf_op jit(solution)/shard_map/pallas_call | solution.py:428
  33.8 11.2 %all_to_all.5 = f32[32,2,4]{2,1,0:T(2,128)S(1)} all-to-all(f32[32,2,4]{2,1,0:T(2,128)S(1)} %get-tuple-element.62), channel_id=1, replica_groups=mesh['grid'=2,'gx'=4,'gy'=4] {'grid','gx','gy'}, dimensions={0} | all-to-all | bytes 2048 | tf_op jit(solution)/shard_map/all_to_all | solution.py:514
  45.0 0.6 %reduce_max.9 = f32[2,4]{1,0:T(2,128)} reduce(f32[32,2,4]{2,1,0:T(2,128)S(1)} %all_to_all.5, f32[]{:T(128)} %constant.8.clone.1), dimensions={0}, to_apply=%region_0.0 | reduce | flops 248 | bytes 1060 | tf_op jit(solution)/shard_map/reduce_max | solution.py:514
  (24 shorter events, 0.0 us)
Async XLA Ops:
  0.6 4.2 %copy-start.1 = (f32[3,16,32,128]{3,2,1,0:T(8,128)S(1)}, f32[3,16,32,128]{3,2,1,0:T(8,128)}, u32[]{:S(2)}) copy-start(f32[3,16,32,128]{3,2,1,0:T(8,128)} %refs_6_.1) | copy-start | bytes 2359300
  0.6 4.2 %copy-start = (f32[3,16,64,256]{3,2,1,0:T(8,128)S(1)}, f32[3,16,64,256]{3,2,1,0:T(8,128)}, u32[]{:S(2)}) copy-start(f32[3,16,64,256]{3,2,1,0:T(8,128)} %refs_5_.1) | copy-start | bytes 9437188
  2.2 8.1 %copy-start.2 = (f32[16,64,256]{2,1,0:T(8,128)S(1)}, f32[16,64,256]{2,1,0:T(8,128)}, u32[]{:S(2)}) copy-start(f32[16,64,256]{2,1,0:T(8,128)} %sp.7) | copy-start | bytes 3145732
  2.2 8.1 %copy-start.3 = (f32[16,64,256]{2,1,0:T(8,128)S(1)}, f32[16,64,256]{2,1,0:T(8,128)}, u32[]{:S(2)}) copy-start(f32[16,64,256]{2,1,0:T(8,128)} %me.7) | copy-start | bytes 3145732
  2.2 8.1 %copy-start.4 = (f32[16,32,128]{2,1,0:T(8,128)S(1)}, f32[16,32,128]{2,1,0:T(8,128)}, u32[]{:S(2)}) copy-start(f32[16,32,128]{2,1,0:T(8,128)} %cs.7) | copy-start | bytes 786436
  2.3 8.1 %copy-start.6 = (bf16[384,256]{1,0:T(8,128)(2,1)S(1)}, bf16[384,256]{1,0:T(8,128)(2,1)}, u32[]{:S(2)}) copy-start(bf16[384,256]{1,0:T(8,128)(2,1)} %constant.19.clone.widen) | copy-start | bytes 589828
  2.3 8.1 %copy-start.7 = (bf16[768,128]{1,0:T(8,128)(2,1)S(1)}, bf16[768,128]{1,0:T(8,128)(2,1)}, u32[]{:S(2)}) copy-start(bf16[768,128]{1,0:T(8,128)(2,1)} %constant.18.clone.narrow) | copy-start | bytes 589828
  2.3 8.1 %copy-start.9 = (f32[64,256]{1,0:T(8,128)S(1)}, f32[64,256]{1,0:T(8,128)}, u32[]{:S(2)}) copy-start(f32[64,256]{1,0:T(8,128)} %tr.7) | copy-start | bytes 196612
  2.3 8.1 %copy-start.10 = (bf16[256,512]{1,0:T(8,128)(2,1)S(1)}, bf16[256,512]{1,0:T(8,128)(2,1)}, u32[]{:S(2)}) copy-start(bf16[256,512]{1,0:T(8,128)(2,1)} %constant.22.clone.left_c) | copy-start | bytes 786436
  2.3 8.1 %copy-start.11 = (bf16[512,256]{1,0:T(8,128)(2,1)S(1)}, bf16[512,256]{1,0:T(8,128)(2,1)}, u32[]{:S(2)}) copy-start(bf16[512,256]{1,0:T(8,128)(2,1)} %constant.21.clone.right_f) | copy-start | bytes 786436
  2.3 8.1 %copy-start.12 = (bf16[256,512]{1,0:T(8,128)(2,1)S(1)}, bf16[256,512]{1,0:T(8,128)(2,1)}, u32[]{:S(2)}) copy-start(bf16[256,512]{1,0:T(8,128)(2,1)} %constant.20.clone.left_f) | copy-start | bytes 786436
  2.3 8.1 %copy-start.14 = (bf16[256,128]{1,0:T(8,128)(2,1)S(1)}, bf16[256,128]{1,0:T(8,128)(2,1)}, u32[]{:S(2)}) copy-start(bf16[256,128]{1,0:T(8,128)(2,1)} %constant.23.clone.right_c) | copy-start | bytes 196612
  2.3 14.8 %collective-permute-start = (f32[12,8,384]{2,1,0:T(8,128)S(1)}, f32[12,8,384]{2,1,0:T(8,128)S(1)}, u32[]{:S(2)}, u32[]{:S(2)}) collective-permute-start(f32[12,8,384]{2,1,0:T(8,128)S(1)} %get-tuple-element.44), channel_id=1, source_target_pairs={{0,12},{4,0},{8,4},{12,8},{1,13},{5,1},{9,5},{13,9},{2,14},{6,2},{... | collective-permute-start | bytes 442376 | tf_op jit(solution)/shard_map/ppermute | solution.py:445
  4.8 12.3 %collective-permute-start.1 = (f32[12,8,384]{2,1,0:T(8,128)S(1)}, f32[12,8,384]{2,1,0:T(8,128)S(1)}, u32[]{:S(2)}, u32[]{:S(2)}) collective-permute-start(f32[12,8,384]{2,1,0:T(8,128)S(1)} %get-tuple-element.45), channel_id=1, source_target_pairs={{0,4},{4,8},{8,12},{12,0},{1,5},{5,9},{9,13},{13,1},{2,6},{6,10},{... | collective-permute-start | bytes 442376 | tf_op jit(solution)/shard_map/ppermute | solution.py:445
  5.7 9.9 %collective-permute-start.2 = (f32[96,128]{1,0:T(8,128)S(1)}, f32[96,128]{1,0:T(8,128)S(1)}, u32[]{:S(2)}, u32[]{:S(2)}) collective-permute-start(f32[96,128]{1,0:T(8,128)S(1)} %get-tuple-element.46), channel_id=1, source_target_pairs={{0,19},{1,0},{2,1},{3,2},{16,3},{17,16},{18,17},{19,18},{4,23},{5,... | collective-permute-start | bytes 147464 | tf_op jit(solution)/shard_map/ppermute | solution.py:445
  10.3 6.9 %copy-start.5 = (f32[3,16,64,256]{3,2,1,0:T(8,128)S(1)}, f32[3,16,64,256]{3,2,1,0:T(8,128)}, u32[]{:S(2)}) copy-start(f32[3,16,64,256]{3,2,1,0:T(8,128)} %pf.1) | copy-start | bytes 9437188
  10.3 6.9 %copy-start.8 = (bf16[768,256]{1,0:T(8,128)(2,1)S(1)}, bf16[768,256]{1,0:T(8,128)(2,1)}, u32[]{:S(2)}) copy-start(bf16[768,256]{1,0:T(8,128)(2,1)} %constant.25.clone.unpack) | copy-start | bytes 1179652
  10.3 6.9 %copy-start.13 = (f32[3,16,32,128]{3,2,1,0:T(8,128)S(1)}, f32[3,16,32,128]{3,2,1,0:T(8,128)}, u32[]{:S(2)}) copy-start(f32[3,16,32,128]{3,2,1,0:T(8,128)} %pc.1) | copy-start | bytes 2359300
  10.3 6.9 %copy-start.15 = (f32[32,128]{1,0:T(8,128)S(1)}, f32[32,128]{1,0:T(8,128)}, u32[]{:S(2)}) copy-start(f32[32,128]{1,0:T(8,128)} %sh.3) | copy-start | bytes 49156
  10.3 6.9 %collective-permute-start.3 = (f32[96,128]{1,0:T(8,128)S(1)}, f32[96,128]{1,0:T(8,128)S(1)}, u32[]{:S(2)}, u32[]{:S(2)}) collective-permute-start(f32[96,128]{1,0:T(8,128)S(1)} %get-tuple-element.47), channel_id=1, source_target_pairs={{0,1},{1,2},{2,3},{3,16},{16,17},{17,18},{18,19},{19,0},{4,5},{5,6... | collective-permute-start | bytes 147464 | tf_op jit(solution)/shard_map/ppermute | solution.py:445
  20.0 11.2 %collective-permute-start.4 = (f32[12,8,384]{2,1,0:T(8,128)S(1)}, f32[12,8,384]{2,1,0:T(8,128)S(1)}, u32[]{:S(2)}, u32[]{:S(2)}) collective-permute-start(f32[12,8,384]{2,1,0:T(8,128)S(1)} %get-tuple-element.56), channel_id=1, source_target_pairs={{0,12},{4,0},{8,4},{12,8},{1,13},{5,1},{9,5},{13,9},{2,14},{6,2},{... | collective-permute-start | bytes 442376 | tf_op jit(solution)/shard_map/ppermute | solution.py:445
  20.3 10.8 %collective-permute-start.5 = (f32[12,8,384]{2,1,0:T(8,128)S(1)}, f32[12,8,384]{2,1,0:T(8,128)S(1)}, u32[]{:S(2)}, u32[]{:S(2)}) collective-permute-start(f32[12,8,384]{2,1,0:T(8,128)S(1)} %get-tuple-element.57), channel_id=1, source_target_pairs={{0,4},{4,8},{8,12},{12,0},{1,5},{5,9},{9,13},{13,1},{2,6},{6,10},{... | collective-permute-start | bytes 442376 | tf_op jit(solution)/shard_map/ppermute | solution.py:445
  20.6 8.9 %collective-permute-start.6 = (f32[96,128]{1,0:T(8,128)S(1)}, f32[96,128]{1,0:T(8,128)S(1)}, u32[]{:S(2)}, u32[]{:S(2)}) collective-permute-start(f32[96,128]{1,0:T(8,128)S(1)} %get-tuple-element.58), channel_id=1, source_target_pairs={{0,19},{1,0},{2,1},{3,2},{16,3},{17,16},{18,17},{19,18},{4,23},{5,... | collective-permute-start | bytes 147464 | tf_op jit(solution)/shard_map/ppermute | solution.py:445
  24.3 6.8 %collective-permute-start.7 = (f32[96,128]{1,0:T(8,128)S(1)}, f32[96,128]{1,0:T(8,128)S(1)}, u32[]{:S(2)}, u32[]{:S(2)}) collective-permute-start(f32[96,128]{1,0:T(8,128)S(1)} %get-tuple-element.59), channel_id=1, source_target_pairs={{0,1},{1,2},{2,3},{3,16},{16,17},{17,18},{18,19},{19,0},{4,5},{5,6... | collective-permute-start | bytes 147464 | tf_op jit(solution)/shard_map/ppermute | solution.py:445
